TPU v7x, 32 devices: a whole 2x2x4 slice. The times are simulated.
32 devices in a mesh: passage: 8 (over y, x, core), sub: 4 (over z).
Axes of the slice: x: 2, y: 2, z: 4, core: 2. Of those that a mesh axis runs over, the one named last changes fastest.
Arguments:
- block_vectors: float32 [32, 8192], P(None, ('passage', 'sub')), may hold values from -75 to 75
- stiffness: float32 [8192], P(('passage', 'sub')), may hold values from 2 to 8
- mass_diag: float32 [8192], P(('passage', 'sub')), may hold values from 0.5 to 2
- kblocks: float32 [64, 4, 128, 128], P(('passage', 'sub')), may hold values from -0.25 to 0.25
- block_cols: int32 [64, 4], P(('passage', 'sub')), may hold values from 0 to 5
- slot_node: int32 [32768], P(('passage', 'sub')), may hold values from 0 to 255
- slot_owner: int32 [32768, 1], P(('passage', 'sub')), may hold values from 0 to 3; in each aligned block of 1024 rows (0 to 1023, 1024 to 2047, ...) at most 512 rows name the same one
- slot_cell: int32 [32768], P(('passage', 'sub')), may hold values from 0 to 8191
- slot_weight: float32 [32768], P(('passage', 'sub')), may hold values from 0.5 to 4
- live_slots: int32 [32], P(('passage', 'sub')), may hold values from 768 to 1024, as said below
Outputs:
- residual: float32 [32, 8192], P(None, ('passage', 'sub'))
- gram_stiff: float32 [64, 64], replicated
- gram_plain: float32 [64, 64], replicated
Inputs may be any that keep to these rules, and one draw needn't show every extreme that they name: `slot_owner`: per device at most 512 slots name the same owner, and some device reaches 512 for some owner. `live_slots`: some device has all 1024 slots live.
All inputs are finite; a program needn't handle non-finite values.
Results may differ from a plain program's by a relative error of at most 0.00019.
Values sent between devices are 32-bit elements; how exact they have to be, the bound alone decides.
No kernel may reach another device: no remote copies, remote signals or barrier semaphores. Data moves between devices by JAX's collectives and lax.ppermute only.
A program may use at most 64 MiB of HBM per device.

v0:
```python
import jax
import jax.numpy as jnp
from jax import lax
from jax.sharding import PartitionSpec as P

CX = 8
CY = 8
CZ = 128


center_weight = 15.0
lower_bound = 1.0 / 15.0
upper_bound = 17.0 / 15.0
middle = (upper_bound + lower_bound) / 2.0
radius = (upper_bound - lower_bound) / 2.0
sigma_ratio = middle / radius
first_rho = 1.0 / sigma_ratio
second_rho = 1.0 / (2.0 * sigma_ratio - first_rho)
third_rho = 1.0 / (2.0 * sigma_ratio - second_rho)


def padded_2(block, sides, width, periodic):
    for axis, dim in sides:
        count = lax.axis_size(axis)
        forward = [(i, i + 1) for i in range(count - 1)]
        if periodic:
            forward.append((count - 1, 0))
        backward = [(target, source) for source, target in forward]
        low = lax.ppermute(
            lax.slice_in_dim(block, block.shape[dim] - width, None, axis=dim), axis, forward
        )
        high = lax.ppermute(lax.slice_in_dim(block, 0, width, axis=dim), axis, backward)
        block = jnp.concatenate([low, block, high], axis=dim)
    return block


def laplace_inner(padded):
    rows_one = padded.shape[1] - 2
    rows_two = padded.shape[2] - 2
    depth = padded.shape[3]
    zpadded = jnp.pad(padded, ((0, 0), (0, 0), (0, 0), (1, 1)))
    neighbours = jnp.zeros((padded.shape[0], rows_one, rows_two, depth), jnp.float32)
    for offset_one in range(3):
        for offset_two in range(3):
            for offset_three in range(3):
                distance = abs(offset_one - 1) + abs(offset_two - 1) + abs(offset_three - 1)
                if distance == 0:
                    continue
                weight = 0.5 ** (distance - 1)
                neighbours = (
                    neighbours
                    + weight
                    * zpadded[
                        :,
                        offset_one : offset_one + rows_one,
                        offset_two : offset_two + rows_two,
                        offset_three : offset_three + depth,
                    ]
                )
    return center_weight * padded[:, 1:-1, 1:-1, :] - neighbours


def pressure_solve(source):
    wider = padded_2(source, (("passage", 1),), 2, True)
    wider = padded_2(wider, (("sub", 2),), 2, False)
    rows_sub = source.shape[2]
    global_row = lax.axis_index("sub") * rows_sub + jnp.arange(rows_sub + 2, dtype=jnp.int32) - 1
    inside = ((global_row >= 0) & (global_row < rows_sub * lax.axis_size("sub"))).astype(
        jnp.float32
    )[None, None, :, None]
    first = wider / (center_weight * middle)
    resid = wider[:, 1:-1, 1:-1] - laplace_inner(first)
    second_step = (
        second_rho * first_rho * first[:, 1:-1, 1:-1]
        + 2.0 * second_rho / radius * (resid / center_weight)
    ) * inside
    second = first[:, 1:-1, 1:-1] + second_step
    resid = source - laplace_inner(second)
    third_step = third_rho * second_rho * second_step[:, 1:-1, 1:-1] + 2.0 * third_rho / radius * (
        resid / center_weight
    )
    result = second[:, 1:-1, 1:-1] + third_step
    return result


def stiffness_apply(field, block_cols, kblocks, stiffness):
    width, local = field.shape
    block_size = kblocks.shape[2]
    window = padded_2(field, (("sub", 1),), local, False)
    blocks = window.reshape(width, 3 * local // block_size, block_size)
    gathered = blocks[:, block_cols]
    mixed = jnp.einsum("mrnb,rnbk->mrk", gathered, kblocks, precision=lax.Precision.HIGHEST)
    return stiffness[None, :] * field + mixed.reshape(width, local)


def inner(left, right):
    return lax.dot_general(
        left,
        right,
        (((1,), (1,)), ((), ())),
        precision=lax.Precision.HIGHEST,
        preferred_element_type=jnp.float32,
    )


def body(
    block_vectors,
    stiffness,
    mass_diag,
    kblocks,
    block_cols,
    slot_node,
    slot_owner,
    slot_cell,
    slot_weight,
    live_slots,
):
    modes, local = block_vectors.shape
    groups = lax.axis_size("sub")
    slots = slot_node.shape[0]
    capacity = 2 * slots // groups
    total = local * lax.axis_size("passage") * groups
    live = (jnp.arange(slots, dtype=jnp.int32) < live_slots[0]).astype(jnp.float32)
    scaled = slot_weight * live
    owner = slot_owner[:, 0]
    onehot = (owner[:, None] == jnp.arange(groups, dtype=jnp.int32)[None, :]).astype(jnp.int32)
    before = jnp.cumsum(onehot, axis=0) - onehot
    target = owner * capacity + jnp.sum(before * onehot, axis=1)
    cells_out = (
        jnp.zeros((groups * capacity,), jnp.int32)
        .at[target]
        .set(slot_cell)
        .reshape(groups, capacity)
    )
    cells_in = lax.all_to_all(cells_out, "sub", split_axis=0, concat_axis=0, tiled=True).reshape(-1)
    stiff_image = stiffness_apply(block_vectors, block_cols, kblocks, stiffness)
    values = block_vectors[:, slot_node] * scaled[None, :]
    outgoing = (
        jnp.zeros((modes, groups * capacity), jnp.float32)
        .at[:, target]
        .set(values)
        .reshape(modes, groups, capacity)
    )
    incoming = lax.all_to_all(outgoing, "sub", split_axis=1, concat_axis=1, tiled=True).reshape(
        modes, -1
    )
    source = (
        jnp.zeros((modes, CX * CY * CZ), jnp.float32)
        .at[:, cells_in]
        .add(incoming)
        .reshape(modes, CX, CY, CZ)
    )
    press = pressure_solve(source).reshape(modes, -1)
    picked = press[:, cells_in].reshape(modes, groups, capacity)
    returned = lax.all_to_all(picked, "sub", split_axis=1, concat_axis=1, tiled=True).reshape(
        modes, -1
    )
    forces = returned[:, target] * scaled[None, :]
    mass_image = mass_diag[None, :] * block_vectors + jnp.zeros((modes, local), jnp.float32).at[
        :, slot_node
    ].add(forces)
    numer, denom = lax.psum(
        (jnp.sum(block_vectors * stiff_image, axis=1), jnp.sum(block_vectors * mass_image, axis=1)),
        ("passage", "sub"),
    )
    theta = numer / denom
    residual = stiff_image - theta[:, None] * mass_image
    stiff_resid = stiffness_apply(residual, block_cols, kblocks, stiffness)
    search = jnp.concatenate([block_vectors, residual], axis=0)
    image = jnp.concatenate([stiff_image, stiff_resid], axis=0)
    gram_stiff, gram_plain = lax.psum(
        (inner(search, image), inner(search, search)), ("passage", "sub")
    )
    return (residual, gram_stiff / total, gram_plain / total)


def solution(mesh):
    return jax.shard_map(
        body,
        mesh=mesh,
        in_specs=(
            P(None, ("passage", "sub")),
            P(("passage", "sub")),
            P(("passage", "sub")),
            P(("passage", "sub"), None, None, None),
            P(("passage", "sub"), None),
            P(("passage", "sub")),
            P(("passage", "sub"), None),
            P(("passage", "sub")),
            P(("passage", "sub")),
            P(("passage", "sub")),
        ),
        out_specs=(P(None, ("passage", "sub")), P(), P()),
        check_vma=False,
    )
```

profile of v0, /device:TPU:0, one launch (start us, length us, event | category | flops | bytes accessed | tf_op | source)
XLA Modules:
  0.0 229.7 jit_solution(4799401068273451031)
XLA Ops:
  0.6 5.1 %collective-permute-start = (f32[32,256]{1,0:T(8,128)}, f32[32,256]{1,0:T(8,128)S(1)}, u32[]{:S(2)}, u32[]{:S(2)}) collective-permute-start(f32[32,256]{1,0:T(8,128)} %param.10), channel_id=1, source_target_pairs={{0,1},{1,2},{2,3},{4,5},{5,6},{6,7},{8,9},{9,10},{10,11},{12,13},{... | collective-permute-start | bytes 98312 | tf_op jit(solution)/shard_map/ppermute | solution.py:29
  5.7 1.3 collective-permute-start.1
  7.7 1.1 reduce-window.6
  10.8 5.0 %scatter_custom_fusion = s32[2048]{0:T(1024)} fusion(s32[1024]{0:T(1024)S(1)} %bitcast.89, s32[1024]{0:T(1024)} %param.17, s32[]{:T(128)} %constant.20.clone.1), kind=kCustom, calls=%fused_computation.196 | custom fusion | bytes 8704 | tf_op jit(solution)/shard_map/scatter | solution.py:132
  15.8 5.9 %all-to-all-start = ((s32[4,1,512]{2,1,0:T(1,128)}), s32[4,1,512]{2,1,0:T(1,128)S(1)}, u32[]{:S(2)}, u32[]{:S(2)}) async-start(s32[4,1,512]{2,1,0:T(1,128)} %bitcast.11), calls=%async_computation | async-start | bytes 16384 | tf_op jit(solution)/shard_map/all_to_all | solution.py:135
  24.6 6.6 %scatter_custom_fusion.1 = f32[32,2048]{0,1:T(8,128)S(1)} fusion(s32[1024]{0:T(1024)S(1)} %bitcast.90, f32[]{:T(128)} %constant.22.clone.1, f32[1024]{0:T(1024)S(1)} %fusion.112, f32[32,256]{0,1:T(8,128)S(1)} %copy.119, s32[1024]{0:T(1024)S(1)} %get-tuple-element.36), kind=kCustom, calls=%fused_computation.155 | custom fusion | flops 32768 | bytes 401412 | tf_op jit(solution)/shard_map/scatter | solution.py:141
  31.2 1.0 copy.125
  32.2 5.1 %all-to-all-start.1 = ((f32[32,4,512]{2,0,1:T(8,128)}), f32[32,4,512]{2,0,1:T(8,128)S(1)}, u32[]{:S(2)}, u32[]{:S(2)}) async-start(f32[32,4,512]{2,0,1:T(8,128)} %copy.125), calls=%async_computation.1 | async-start | bytes 524288 | tf_op jit(solution)/shard_map/all_to_all | solution.py:144
  37.3 7.9 %all-to-all-done.1 = f32[32,4,512]{2,0,1:T(8,128)S(1)} async-done(((f32[32,4,512]{2,0,1:T(8,128)}), f32[32,4,512]{2,0,1:T(8,128)S(1)}, u32[]{:S(2)}, u32[]{:S(2)}) %all-to-all-start.1) | async-done | bytes 262176 | tf_op jit(solution)/shard_map/all_to_all | solution.py:144
  45.6 15.6 %scatter_custom_fusion.2 = f32[32,8192]{0,1:T(8,128)} fusion(s32[2048]{0:T(1024)S(1)} %bitcast.86, f32[2048,32]{1,0:T(8,128)S(1)} %copy.127, f32[]{:T(128)} %constant.22.clone.1), kind=kCustom, calls=%fused_computation.46 | custom fusion | flops 65536 | bytes 1048580 | tf_op jit(solution)/shard_map/scatter-add | solution.py:150
  61.2 1.7 fusion.118
  63.7 2.7 %collective-permute-start.3 = (f32[32,2,8,128]{3,2,1,0:T(8,128)S(1)}, f32[32,2,8,128]{3,2,1,0:T(8,128)S(1)}, u32[]{:S(2)}, u32[]{:S(2)}) collective-permute-start(f32[32,2,8,128]{3,2,1,0:T(8,128)S(1)} %copy.154), channel_id=1, source_target_pairs={{4,0},{8,4},{12,8},{16,12},{20,16},{24,20},{28,24},{0,28},{5,1},{9... | collective-permute-start | bytes 786440 | tf_op jit(solution)/shard_map/ppermute | solution.py:32
  66.4 2.8 %copy.131 = f32[32,8,8,128]{3,0,2,1:T(8,128)S(1)} copy(f32[32,8,8,128]{0,3,2,1:T(8,128)} %bitcast.75) | data formatting | bytes 2097152 | tf_op jit(solution)/shard_map/reshape | solution.py:151
  69.2 1.1 collective-permute-done.2
  71.3 1.3 collective-permute-start.4
  72.6 1.5 collective-permute-start.5
  74.1 6.7 %collective-permute-done.4 = f32[32,12,2,128]{3,0,2,1:T(8,128)S(1)} collective-permute-done((f32[32,12,2,128]{3,0,2,1:T(8,128)S(1)}, f32[32,12,2,128]{3,0,2,1:T(8,128)S(1)}, u32[]{:S(2)}, u32[]{:S(2)}) %collective-permute-start.4) | collective-permute-done | bytes 393248 | tf_op jit(solution)/shard_map/ppermute | solution.py:29
  80.8 4.7 %collective-permute-done.5 = f32[32,12,2,128]{3,0,2,1:T(8,128)S(1)} collective-permute-done((f32[32,12,2,128]{3,0,2,1:T(8,128)S(1)}, f32[32,12,2,128]{3,0,2,1:T(8,128)S(1)}, u32[]{:S(2)}, u32[]{:S(2)}) %collective-permute-start.5) | collective-permute-done | bytes 393248 | tf_op jit(solution)/shard_map/ppermute | solution.py:32
  85.5 1.9 pad_maximum_fusion
  87.4 9.0 %slice_add_fusion = (f32[32,10,10,128]{3,0,2,1:T(8,128)S(1)}, f32[32,10,10,128]{3,0,2,1:T(8,128)S(1)}) fusion(f32[32,12,12,128]{3,0,2,1:T(8,128)S(1)} %get-tuple-element.33, f32[10]{0:T(128)S(1)} %and_convert_fusion, f32[32,12,12,128]{3,0,2,1:T(8,128)} %get-tuple-element.32), kind=kLoop, calls=%fused_computation.98 | loop fusion | flops 21708800 | bytes 22020608 | tf_op jit(solution)/shard_map/add | solution.py:77
  96.5 5.9 %fusion.91 = f32[32,8,8,128]{3,0,2,1:T(8,128)} fusion(f32[32,8,8,128]{3,0,2,1:T(8,128)S(1)} %copy.131, f32[32,10,10,128]{3,0,2,1:T(8,128)S(1)} %get-tuple-element.28, f32[32,10,10,128]{3,0,2,1:T(8,128)S(1)} %get-tuple-element.29), kind=kLoop, calls=%fused_computation.145 | loop fusion | flops 13631488 | bytes 14221312 | tf_op jit(solution)/shard_map/add | solution.py:82
  102.3 3.6 %copy.134 = f32[32,8,8,128]{0,3,2,1:T(8,128)} copy(f32[32,8,8,128]{3,0,2,1:T(8,128)} %fusion.91) | data formatting | bytes 2097152 | tf_op jit(solution)/shard_map/add | solution.py:82
  105.9 7.7 %gather_fusion.1 = f32[2048,32]{1,0:T(8,128)S(1)} fusion(f32[32,8192]{0,1:T(8,128)} %bitcast.76, s32[2048]{0:T(1024)S(1)} %broadcast_clamp_fusion), kind=kCustom, calls=%fused_computation.2 | custom fusion | bytes 532480 | tf_op jit(solution)/shard_map/gather | solution.py:154
  113.6 1.0 copy.135
  114.6 4.7 %all-to-all-start.2 = ((f32[32,4,512]{2,0,1:T(8,128)}), f32[32,4,512]{2,0,1:T(8,128)S(1)}, u32[]{:S(2)}, u32[]{:S(2)}) async-start(f32[32,4,512]{2,0,1:T(8,128)} %copy.135), calls=%async_computation.2 | async-start | bytes 524288 | tf_op jit(solution)/shard_map/all_to_all | solution.py:155
  120.6 8.0 %all-to-all-done.2 = f32[32,4,512]{2,0,1:T(8,128)S(1)} async-done(((f32[32,4,512]{2,0,1:T(8,128)}), f32[32,4,512]{2,0,1:T(8,128)S(1)}, u32[]{:S(2)}, u32[]{:S(2)}) %all-to-all-start.2) | async-done | bytes 262176 | tf_op jit(solution)/shard_map/all_to_all | solution.py:155
  128.8 9.3 %scatter_custom_fusion.3 = f32[32,256]{0,1:T(8,128)S(1)} fusion(f32[32,256]{0,1:T(8,128)S(1)} %copy.137, s32[1024]{0:T(1024)S(1)} %get-tuple-element.37, f32[1024]{0:T(1024)S(1)} %fusion.112, f32[32,2048]{0,1:T(8,128)S(1)} %bitcast.77, s32[1024]{0:T(1024)S(1)} %broadcast_clamp_fusion.1), kind=kCustom, calls=%fused_computation.153 | custom fusion | flops 65536 | bytes 1089536 | tf_op jit(solution)/shard_map/scatter-add | solution.py:161
  138.3 37.8 %all-reduce.3 = (f32[32]{0:T(128)S(1)}, f32[32]{0:T(128)S(1)}) all-reduce(f32[32]{0:T(128)S(1)} %get-tuple-element.22, f32[32]{0:T(128)S(1)} %get-tuple-element.21), channel_id=1, replica_groups=mesh['passage'=8,'sub'=4] {'passage','sub'}, use_global_device_ids=true, to_apply=%region_1.2 | all-reduce | flops 64 | bytes 512 | tf_op jit(solution)/shard_map/psum | solution.py:162
  176.2 3.9 %collective-permute-start.6 = (f32[32,256]{0,1:T(8,128)S(1)}, f32[32,256]{0,1:T(8,128)S(1)}, u32[]{:S(2)}, u32[]{:S(2)}) collective-permute-start(f32[32,256]{0,1:T(8,128)S(1)} %multiply_subtract_fusion), channel_id=1, source_target_pairs={{0,1},{1,2},{2,3},{4,5},{5,6},{6,7},{8,9},{9,10},{10,11},{12,13},{... | collective-permute-start | bytes 98312 | tf_op jit(solution)/shard_map/ppermute | solution.py:29
  180.1 1.3 collective-permute-start.7
  182.7 4.3 %collective-permute-done.7 = f32[32,256]{0,1:T(8,128)S(1)} collective-permute-done((f32[32,256]{0,1:T(8,128)S(1)}, f32[32,256]{0,1:T(8,128)S(1)}, u32[]{:S(2)}, u32[]{:S(2)}) %collective-permute-start.7) | collective-permute-done | bytes 32800 | tf_op jit(solution)/shard_map/ppermute | solution.py:32
  188.7 40.3 %all-reduce.2 = (f32[64,64]{1,0:T(8,128)S(1)}, f32[64,64]{1,0:T(8,128)S(1)}) all-reduce(f32[64,64]{1,0:T(8,128)S(1)} %fusion.101, f32[64,64]{1,0:T(8,128)S(1)} %fusion.105), channel_id=1, replica_groups=mesh['passage'=8,'sub'=4] {'passage','sub'}, use_global_device_ids=true, to_apply=%region_11.12 | all-reduce | flops 8192 | bytes 65536 | tf_op jit(solution)/shard_map/psum | solution.py:171
  (62 shorter events, 12.2 us)
Async XLA Ops:
  0.6 119.4 %copy-start = (f32[2,4,128,128]{3,2,1,0:T(8,128)S(1)}, f32[2,4,128,128]{3,2,1,0:T(8,128)}, u32[]{:S(2)}) copy-start(f32[2,4,128,128]{3,2,1,0:T(8,128)} %param.13) | copy-start | bytes 1572868
  0.6 118.8 %collective-permute-start = (f32[32,256]{1,0:T(8,128)}, f32[32,256]{1,0:T(8,128)S(1)}, u32[]{:S(2)}, u32[]{:S(2)}) collective-permute-start(f32[32,256]{1,0:T(8,128)} %param.10), channel_id=1, source_target_pairs={{0,1},{1,2},{2,3},{4,5},{5,6},{6,7},{8,9},{9,10},{10,11},{12,13},{... | collective-permute-start | bytes 98312 | tf_op jit(solution)/shard_map/ppermute | solution.py:29
  5.7 113.7 %collective-permute-start.1 = (f32[32,256]{1,0:T(8,128)}, f32[32,256]{1,0:T(8,128)S(1)}, u32[]{:S(2)}, u32[]{:S(2)}) collective-permute-start(f32[32,256]{1,0:T(8,128)} %param.10), channel_id=1, source_target_pairs={{1,0},{2,1},{3,2},{5,4},{6,5},{7,6},{9,8},{10,9},{11,10},{13,12},{... | collective-permute-start | bytes 98312 | tf_op jit(solution)/shard_map/ppermute | solution.py:32
  15.8 16.4 %all-to-all-start = ((s32[4,1,512]{2,1,0:T(1,128)}), s32[4,1,512]{2,1,0:T(1,128)S(1)}, u32[]{:S(2)}, u32[]{:S(2)}) async-start(s32[4,1,512]{2,1,0:T(1,128)} %bitcast.11), calls=%async_computation | async-start | bytes 16384 | tf_op jit(solution)/shard_map/all_to_all | solution.py:135
  32.2 13.0 %all-to-all-start.1 = ((f32[32,4,512]{2,0,1:T(8,128)}), f32[32,4,512]{2,0,1:T(8,128)S(1)}, u32[]{:S(2)}, u32[]{:S(2)}) async-start(f32[32,4,512]{2,0,1:T(8,128)} %copy.125), calls=%async_computation.1 | async-start | bytes 524288 | tf_op jit(solution)/shard_map/all_to_all | solution.py:144
  62.9 3.5 %copy-start.1 = (f32[32,256]{1,0:T(8,128)S(1)}, f32[32,256]{1,0:T(8,128)}, u32[]{:S(2)}) copy-start(f32[32,256]{1,0:T(8,128)} %param.10) | copy-start | bytes 98308
  62.9 3.4 %copy-start.4 = (f32[256]{0:T(256)S(1)}, f32[256]{0:T(256)}, u32[]{:S(2)}) copy-start(f32[256]{0:T(256)} %param.12) | copy-start | bytes 3076
  63.3 7.1 %collective-permute-start.2 = (f32[32,2,8,128]{3,2,1,0:T(8,128)S(1)}, f32[32,2,8,128]{3,2,1,0:T(8,128)S(1)}, u32[]{:S(2)}, u32[]{:S(2)}) collective-permute-start(f32[32,2,8,128]{3,2,1,0:T(8,128)S(1)} %copy.153), channel_id=1, source_target_pairs={{0,4},{4,8},{8,12},{12,16},{16,20},{20,24},{24,28},{28,0},{1,5},{5... | collective-permute-start | bytes 786440 | tf_op jit(solution)/shard_map/ppermute | solution.py:29
  63.7 7.5 %collective-permute-start.3 = (f32[32,2,8,128]{3,2,1,0:T(8,128)S(1)}, f32[32,2,8,128]{3,2,1,0:T(8,128)S(1)}, u32[]{:S(2)}, u32[]{:S(2)}) collective-permute-start(f32[32,2,8,128]{3,2,1,0:T(8,128)S(1)} %copy.154), channel_id=1, source_target_pairs={{4,0},{8,4},{12,8},{16,12},{20,16},{24,20},{28,24},{0,28},{5,1},{9... | collective-permute-start | bytes 786440 | tf_op jit(solution)/shard_map/ppermute | solution.py:32
  71.3 9.5 %collective-permute-start.4 = (f32[32,12,2,128]{3,0,2,1:T(8,128)S(1)}, f32[32,12,2,128]{3,0,2,1:T(8,128)S(1)}, u32[]{:S(2)}, u32[]{:S(2)}) collective-permute-start(f32[32,12,2,128]{3,0,2,1:T(8,128)S(1)} %get-tuple-element.34), channel_id=1, source_target_pairs={{0,1},{1,2},{2,3},{4,5},{5,6},{6,7},{8,9},{9,10},{10,11},{12,13},{... | collective-permute-start | bytes 1179656 | tf_op jit(solution)/shard_map/ppermute | solution.py:29
  72.6 12.9 %collective-permute-start.5 = (f32[32,12,2,128]{3,0,2,1:T(8,128)S(1)}, f32[32,12,2,128]{3,0,2,1:T(8,128)S(1)}, u32[]{:S(2)}, u32[]{:S(2)}) collective-permute-start(f32[32,12,2,128]{3,0,2,1:T(8,128)S(1)} %get-tuple-element.35), channel_id=1, source_target_pairs={{1,0},{2,1},{3,2},{5,4},{6,5},{7,6},{9,8},{10,9},{11,10},{13,12},{... | collective-permute-start | bytes 1179656 | tf_op jit(solution)/shard_map/ppermute | solution.py:32
  105.9 13.3 %copy-start.5 = (s32[2,4]{1,0:T(2,128)S(1)}, s32[2,4]{1,0:T(2,128)}, u32[]{:S(2)}) copy-start(s32[2,4]{1,0:T(2,128)} %param.14) | copy-start | bytes 100
  114.6 13.9 %all-to-all-start.2 = ((f32[32,4,512]{2,0,1:T(8,128)}), f32[32,4,512]{2,0,1:T(8,128)S(1)}, u32[]{:S(2)}, u32[]{:S(2)}) async-start(f32[32,4,512]{2,0,1:T(8,128)} %copy.135), calls=%async_computation.2 | async-start | bytes 524288 | tf_op jit(solution)/shard_map/all_to_all | solution.py:155
  120.0 18.2 %copy-start.3 = (f32[256]{0:T(256)S(1)}, f32[256]{0:T(256)}, u32[]{:S(2)}) copy-start(f32[256]{0:T(256)} %param.11) | copy-start | bytes 3076
  176.2 6.4 %collective-permute-start.6 = (f32[32,256]{0,1:T(8,128)S(1)}, f32[32,256]{0,1:T(8,128)S(1)}, u32[]{:S(2)}, u32[]{:S(2)}) collective-permute-start(f32[32,256]{0,1:T(8,128)S(1)} %multiply_subtract_fusion), channel_id=1, source_target_pairs={{0,1},{1,2},{2,3},{4,5},{5,6},{6,7},{8,9},{9,10},{10,11},{12,13},{... | collective-permute-start | bytes 98312 | tf_op jit(solution)/shard_map/ppermute | solution.py:29
  180.1 6.9 %collective-permute-start.7 = (f32[32,256]{0,1:T(8,128)S(1)}, f32[32,256]{0,1:T(8,128)S(1)}, u32[]{:S(2)}, u32[]{:S(2)}) collective-permute-start(f32[32,256]{0,1:T(8,128)S(1)} %multiply_subtract_fusion), channel_id=1, source_target_pairs={{1,0},{2,1},{3,2},{5,4},{6,5},{7,6},{9,8},{10,9},{11,10},{13,12},{... | collective-permute-start | bytes 98312 | tf_op jit(solution)/shard_map/ppermute | solution.py:32
  182.0 47.7 %copy-start.2 = (f32[32,256]{1,0:T(8,128)}, f32[32,256]{1,0:T(8,128)S(1)}, u32[]{:S(2)}) copy-start(f32[32,256]{1,0:T(8,128)S(1)} %copy.146) | copy-start | bytes 98308
where the time goes:
time: 231 us; the launch traced here: 230 us
  blocking collectives  78.1 us (34%)
  other arithmetic  54.2 us (23%)
  waiting for transfers between devices  34.1 us (15%)
  starting transfers between devices  32.8 us (14%)
  local copies, waits for them, and re-layouts  27.1 us (12%)
    psum x1, blocking collectives, body(): lax.psum((inner(search, image), inner(search, search)), ('passage', 'sub'))  40.3 us
    psum x1, blocking collectives, body(): lax.psum((jnp.sum(block_vectors * stiff_image, axis=1), jnp.sum(block_vec...  37.8 us
    scatter-add x1, other arithmetic, body(): source = jnp.zeros((modes, CX * CY * CZ), jnp.float32).at[:, cells_in].ad...  15.6 us
    ppermute x4, starting transfers between devices, padded_2(): lax.ppermute(lax.slice_in_dim(block, block.shape[dim] - width, None, axis...  10.4 us
    ppermute x4, waiting for transfers between devices, padded_2(): lax.ppermute(lax.slice_in_dim(block, 0, width, axis=dim), axis, backward)  9.71 us
    scatter-add x1, other arithmetic, body(): mass_image = mass_diag[None, :] * block_vectors + jnp.zeros((modes, local...  9.34 us
    add x1, other arithmetic, pressure_solve(): second = first[:, 1:-1, 1:-1] + second_step  9.01 us
    ppermute x4, waiting for transfers between devices, padded_2(): lax.ppermute(lax.slice_in_dim(block, block.shape[dim] - width, None, axis...  8.5 us
  transfers between devices with their start and end apart: 11, of which 8 were waited for; matrix products, arithmetic and copies ran while one was open for 31% of the time, Pallas kernels for 0%

commit v1 on v0

v1 whole, which is shorter than its diff:
```python
import functools
import jax
import jax.numpy as jnp
from jax import lax
from jax.experimental import pallas as pl
from jax.experimental.pallas import tpu as pltpu
from jax.sharding import PartitionSpec as P

CX = 8
CY = 8
CZ = 128
HALO = 2

center_weight = 15.0
lower_bound = 1.0 / 15.0
upper_bound = 17.0 / 15.0
middle = (upper_bound + lower_bound) / 2.0
radius = (upper_bound - lower_bound) / 2.0
sigma_ratio = middle / radius
first_rho = 1.0 / sigma_ratio
second_rho = 1.0 / (2.0 * sigma_ratio - first_rho)
third_rho = 1.0 / (2.0 * sigma_ratio - second_rho)

FIRST = 1.0 / (center_weight * middle)
GAIN2 = 2.0 * second_rho / (radius * center_weight)
SEC_U = FIRST * (1.0 + second_rho * first_rho) + GAIN2 * (1.0 - 17.0 * FIRST)
SEC_T = GAIN2 * 2.0 * FIRST
STEP3 = third_rho * second_rho
GAIN3 = 2.0 * third_rho / (radius * center_weight)
PRE_SRC = GAIN3 - STEP3 * FIRST
PRE_SEC = 1.0 + STEP3 - 17.0 * GAIN3
PRE_T = 2.0 * GAIN3

BF = jnp.bfloat16
F32 = jnp.float32
NB1 = (CY + 2 * HALO) // 2
CELLS = CX * CY * CZ


def log2(n):
    return n.bit_length() - 1


def split(x):
    hi = x.astype(BF)
    return hi, (x - hi.astype(F32)).astype(BF)


def decode(row):
    flat = row.astype(jnp.int32)
    a = lax.shift_right_logical(flat, log2(CY * CZ)) & (CX - 1)
    owner = lax.shift_right_logical(flat, log2(CELLS))
    b = lax.shift_right_logical(flat, log2(CZ)) & (CY - 1)
    return a, owner, b, flat & (CZ - 1)


def lanes_from(x, index):
    index = jnp.broadcast_to(index, x.shape)
    return jnp.take_along_axis(x, index, axis=1, mode="promise_in_bounds")


def onehot(values, height):
    shape = (height, values.shape[1])
    rows = lax.broadcasted_iota(jnp.int32, shape, 0)
    return jnp.where(rows == values, 1.0, 0.0).astype(BF)


def add_source(blk, sub, a_first, a_count, out, lhs, rhs, modes, slots, fresh):
    local = blk.shape[1]
    top = modes + 1
    count = slots // local
    for j in range(count):
        a, owner, b, c = decode(blk[top + j : top + j + 1, :])
        node = blk[top + count + j : top + count + j + 1, :].astype(jnp.int32)
        weight = blk[top + 2 * count + j : top + 2 * count + j + 1, :]
        bext = owner * CY + b - (sub * CY - HALO)
        aloc = a - a_first
        valid = (bext >= 0) & (bext < CY + 2 * HALO) & (aloc >= 0) & (aloc < a_count)
        pair = jnp.where(valid, aloc * NB1 + lax.shift_right_arithmetic(bext, 1), -1)
        place = (bext & 1) * CZ + c
        pieces = []
        for h in range(local // 128):
            idx = node[:, h * 128 : (h + 1) * 128]
            got = jnp.zeros((modes, 128), F32)
            for g in range(local // 128):
                part = lanes_from(blk[0:modes, g * 128 : (g + 1) * 128], idx & 127)
                got = jnp.where(lax.shift_right_logical(idx, 7) == g, part, got)
            pieces.append(got)
        vals = jnp.concatenate(pieces, axis=1) * weight
        hi, lo = split(vals)
        wide = jnp.broadcast_to(pair.astype(F32), (modes, local)).astype(BF)
        zero = jnp.zeros((modes, local), BF)
        at = 2 * j * local
        for r in range(a_count * NB1):
            mask = wide == jnp.asarray(r, BF)
            lhs[r * modes : (r + 1) * modes, at : at + local] = jnp.where(mask, hi, zero)
            lhs[r * modes : (r + 1) * modes, at + local : at + 2 * local] = jnp.where(mask, lo, zero)
        hot = onehot(place, 2 * CZ)
        rhs[:, at : at + local] = hot
        rhs[:, at + local : at + 2 * local] = hot
    total = a_count * NB1 * modes
    step = min(total, 384)

    def rows(i, carry):
        at = pl.ds(pl.multiple_of(i * step, step), step)
        got = lax.dot_general(
            lhs[at, :], rhs[...], (((1,), (1,)), ((), ())), preferred_element_type=F32
        )
        if fresh:
            out[at, :] = got
        else:
            out[at, :] = out[at, :] + got
        return carry

    lax.fori_loop(0, total // step, rows, 0)


def own_source_kernel(slots, modes, count, sub_ref, *refs):
    blks, out, lhs, rhs = refs[:count], refs[count], refs[count + 1], refs[count + 2]
    for k in range(count):
        add_source(blks[k], sub_ref[0], 0, CX, out, lhs, rhs, modes, slots, k == 0)


def t_b(plane_e, plane_o, modes, low, high):
    e, o = plane_e, plane_o
    return e, o


def shift_sum(x):
    lane = lax.broadcasted_iota(jnp.int32, x.shape, 1)
    left = jnp.where(lane == 0, 0.0, pltpu.roll(x, 1, 1))
    right = jnp.where(lane == CZ - 1, 0.0, pltpu.roll(x, CZ - 1, 1))
    return x + 0.5 * (left + right)


def fluid_kernel(slots, modes, count, groups, sub_ref, *refs):
    own = refs[:count]
    low, high, src_own, out, edge, second, press, lhs, rhs, force = refs[count:]
    sub = sub_ref[0]
    local = own[0].shape[1]
    top = modes + 1
    per = slots // local
    plane = NB1 * modes
    for k in range(count):
        add_source(low.at[k], sub, CX - HALO, HALO, edge.at[0], lhs, rhs, modes, slots, k == 0)
        add_source(high.at[k], sub, 0, HALO, edge.at[1], lhs, rhs, modes, slots, k == 0)

    def src(a, b):
        rows = slice((b // 2) * modes, (b // 2 + 1) * modes)
        lanes = slice((b % 2) * CZ, (b % 2 + 1) * CZ)
        if a < HALO:
            return edge[0, a * plane + rows.start : a * plane + rows.stop, lanes]
        if a >= CX + HALO:
            at = (a - CX - HALO) * plane
            return edge[1, at + rows.start : at + rows.stop, lanes]
        at = (a - HALO) * plane
        return src_own[at + rows.start : at + rows.stop, lanes]

    for a in range(1, CX + 2 * HALO - 1):
        cols = [
            src(a, b) + 0.5 * (src(a - 1, b) + src(a + 1, b)) for b in range(CY + 2 * HALO)
        ]
        for b in range(1, CY + 2 * HALO - 1):
            t = shift_sum(cols[b] + 0.5 * (cols[b - 1] + cols[b + 1]))
            sec = SEC_U * src(a, b) + SEC_T * t
            if b < HALO:
                sec = sec * jnp.where(sub == 0, 0.0, 1.0)
            if b >= CY + HALO:
                sec = sec * jnp.where(sub == groups - 1, 0.0, 1.0)
            second[a - 1, b - 1] = sec
    for a in range(CX):
        cols = [
            second[a + 1, b] + 0.5 * (second[a, b] + second[a + 2, b]) for b in range(CY + 2)
        ]
        for b in range(CY):
            t = shift_sum(cols[b + 1] + 0.5 * (cols[b] + cols[b + 2]))
            press[a * CY + b] = (
                PRE_SRC * src(a + HALO, b + HALO) + PRE_SEC * second[a + 1, b + 1] + PRE_T * t
            )
    for k in range(count):
        total = jnp.zeros((2 * modes, local), F32)
        for j in range(per):
            a, owner, b, c = decode(own[k][top + j : top + j + 1, :])
            node = own[k][top + per + j : top + per + j + 1, :].astype(jnp.int32)
            weight = own[k][top + 2 * per + j : top + 2 * per + j + 1, :]
            row = jnp.where(owner == sub, a * CY + b, -1)
            halves = local // 128
            idx = [
                jnp.broadcast_to(c[:, h * 128 : (h + 1) * 128], (modes, 128)) for h in range(halves)
            ]
            row_w = [
                jnp.broadcast_to(row[:, h * 128 : (h + 1) * 128], (modes, 128))
                for h in range(halves)
            ]

            def pick(i, accs):
                accs = list(accs)
                for u in range(4):
                    r = i * 4 + u
                    cell = press[r]
                    for h in range(halves):
                        got = jnp.take_along_axis(cell, idx[h], axis=1, mode="promise_in_bounds")
                        accs[h] = jnp.where(row_w[h] == r, got, accs[h])
                return tuple(accs)

            accs = lax.fori_loop(
                0, CX * CY // 4, pick, tuple(jnp.zeros((modes, 128), F32) for _ in range(halves))
            )
            picked = jnp.concatenate(accs, axis=1) * weight
            hi, lo = split(picked)
            hot = onehot(node, local)
            total = total + lax.dot_general(
                jnp.concatenate([hi, lo], axis=0),
                hot,
                (((1,), (1,)), ((), ())),
                preferred_element_type=F32,
            )
        force[k] = total[:modes] + total[modes:]
    for k in range(count):
        for w in range(3):
            out[k, w] = force[(1 - k - w) % count]


def apply_blocks(window, cols_ref, kb_ref, sub, groups, diag, field):
    rb, nb, bs, _ = kb_ref.shape
    pieces = []
    for q in range(rb):
        acc = None
        for n in range(nb):
            j = cols_ref[q, n]
            where = sub + j // rb - 1
            inside = jnp.where((where >= 0) & (where < groups), 1.0, 0.0)
            part = lax.dot_general(
                window[j] * inside,
                kb_ref[q, n],
                (((1,), (0,)), ((), ())),
                precision=lax.Precision.HIGHEST,
                preferred_element_type=F32,
            )
            acc = part if acc is None else acc + part
        pieces.append(acc)
    return diag * field + jnp.concatenate(pieces, axis=1)


def fill_window(win, blocks, bs):
    at = 0
    for blk in blocks:
        for i in range(blk.shape[1] // bs):
            win[at] = blk[:, i * bs : (i + 1) * bs]
            at += 1


def stiff_kernel(modes, groups, sub_ref, cols_ref, prev, own, nxt, diag, kb, out, win):
    bs = kb.shape[2]
    fill_window(win, [prev[0:modes, :], own[0:modes, :], nxt[0:modes, :]], bs)
    out[...] = apply_blocks(win, cols_ref, kb, sub_ref[0], groups, diag[...], own[0:modes, :])


def gram_kernel(modes, groups, count, sub_ref, cols_ref, *refs):
    packs, parts = refs[:3], refs[3 : 3 + count]
    stiff, kstiff, diag, kb, gram, mass, win = refs[3 + count :]
    bs = kb.shape[2]
    fields = []
    for w in range(3):
        blk = packs[w]
        m = blk[modes : modes + 1, :] * blk[0:modes, :]
        for part in parts:
            m = m + part[w]
        fields.append(m)
    fill_window(win, fields, bs)
    own = fields[1]
    mass[...] = own
    km = apply_blocks(win, cols_ref, kb, sub_ref[0], groups, diag[...], own)
    v = packs[1][0:modes, :]
    s = stiff[...]
    left = jnp.concatenate([v, s, own], axis=0)
    right = jnp.concatenate([s, kstiff[...], km, own], axis=0)

    def inner(x, y):
        return lax.dot_general(
            x,
            y,
            (((1,), (1,)), ((), ())),
            precision=lax.Precision.HIGHEST,
            preferred_element_type=F32,
        )

    gram[...] = inner(left, right)
    gram[2 * modes : 3 * modes, 0:modes] = inner(v, v)


def final_kernel(modes, total, gram, stiff, mass, residual, g_stiff, g_plain):
    m = modes
    blocks = [
        [gram[i * m : (i + 1) * m, j * m : (j + 1) * m] for j in range(4)] for i in range(3)
    ]
    (vs, vks, vkm, vm), (ss, sks, skm, sm), (vv, mks, mkm, mm) = blocks
    rows = lax.broadcasted_iota(jnp.int32, (m, m), 0)
    lanes = lax.broadcasted_iota(jnp.int32, (m, m), 1)
    eye = rows == lanes

    def column(x):
        return jnp.sum(jnp.where(eye, x, 0.0), axis=1, keepdims=True)

    def line(x):
        return jnp.sum(jnp.where(eye, x, 0.0), axis=0, keepdims=True)

    tc = column(vs) / column(vm)
    tl = line(vs) / line(vm)
    residual[...] = stiff[...] - tc * mass[...]
    ms = sm.T
    scale = 1.0 / total
    vr = vs - vm * tl
    g_plain[0:m, 0:m] = vv * scale
    g_plain[0:m, m : 2 * m] = vr * scale
    g_plain[m : 2 * m, 0:m] = vr.T * scale
    g_plain[m : 2 * m, m : 2 * m] = (ss - sm * tl - tc * (ms - mm * tl)) * scale
    g_stiff[0:m, 0:m] = vs * scale
    g_stiff[0:m, m : 2 * m] = (vks - vkm * tl) * scale
    g_stiff[m : 2 * m, 0:m] = (ss - tc * ms) * scale
    g_stiff[m : 2 * m, m : 2 * m] = (sks - skm * tl - tc * (mks - mkm * tl)) * scale


def shifted(x, axis, k):
    n = lax.axis_size(axis)
    return lax.ppermute(x, axis, [(i, (i + k) % n) for i in range(n)])


def swapped(x, axis, k):
    n = lax.axis_size(axis)
    return lax.ppermute(x, axis, [(i, i ^ k) for i in range(n)])


def summed(x, axis, bit):
    n = lax.axis_size(axis)
    while (1 << bit) < n:
        if (4 << bit) <= n:
            one, two, three = [swapped(x, axis, k << bit) for k in (1, 2, 3)]
            x = (x + one) + (two + three)
            bit += 2
        else:
            x = x + swapped(x, axis, 1 << bit)
            bit += 1
    return x


def smem():
    return pl.BlockSpec(memory_space=pltpu.SMEM)


def vmem():
    return pl.BlockSpec(memory_space=pltpu.VMEM)


def call(kernel, name, out_shape, scalars, arrays, scratch, flops):
    return pl.pallas_call(
        kernel,
        name=name,
        out_shape=out_shape,
        in_specs=[smem()] * len(scalars) + [vmem()] * len(arrays),
        out_specs=jax.tree.map(lambda _: vmem(), out_shape),
        scratch_shapes=scratch,
        cost_estimate=pl.CostEstimate(flops=flops, transcendentals=0, bytes_accessed=1 << 20),
    )(*scalars, *arrays)


def body(
    block_vectors,
    stiffness,
    mass_diag,
    kblocks,
    block_cols,
    slot_node,
    slot_owner,
    slot_cell,
    slot_weight,
    live_slots,
):
    modes, local = block_vectors.shape
    groups = lax.axis_size("sub")
    slots = slot_node.shape[0]
    per = slots // local
    bs = kblocks.shape[2]
    total = local * lax.axis_size("passage") * groups
    sub = lax.axis_index("sub").astype(jnp.int32).reshape(1)
    live = jnp.arange(slots, dtype=jnp.int32) < live_slots[0]
    weight = jnp.where(live, slot_weight, 0.0)
    flat = (slot_owner[:, 0] * CELLS + slot_cell).astype(F32)
    pieces = [
        block_vectors,
        mass_diag[None, :],
        flat.reshape(per, local),
        slot_node.astype(F32).reshape(per, local),
        weight.reshape(per, local),
    ]
    height = modes + 1 + 3 * per
    padded = -(-height // 8) * 8
    pieces.append(jnp.zeros((padded - height, local), F32))
    pack = jnp.concatenate(pieces, axis=0)
    packs = [pack] + [shifted(pack, "sub", k) for k in range(1, groups)]
    both = jnp.stack(packs)
    low = shifted(both, "passage", 1)
    high = shifted(both, "passage", -1)
    diag = stiffness[None, :]
    window = [packs[1], packs[0], packs[groups - 1]]
    nwin = 3 * local // bs
    stiff = call(
        functools.partial(stiff_kernel, modes, groups),
        "stiff",
        jax.ShapeDtypeStruct((modes, local), F32),
        [sub, block_cols],
        [*window, diag, kblocks],
        [pltpu.VMEM((nwin, modes, bs), F32)],
        1 << 29,
    )
    stiff_prev = shifted(stiff, "sub", 1)
    stiff_next = shifted(stiff, "sub", -1)
    kstiff = call(
        functools.partial(stiff_kernel, modes, groups),
        "stiff_image",
        jax.ShapeDtypeStruct((modes, local), F32),
        [sub, block_cols],
        [stiff_prev, stiff, stiff_next, diag, kblocks],
        [pltpu.VMEM((nwin, modes, bs), F32)],
        1 << 29,
    )
    own_rows = CX * NB1 * modes
    source = call(
        functools.partial(own_source_kernel, slots, modes, groups),
        "own_source",
        jax.ShapeDtypeStruct((own_rows, 2 * CZ), F32),
        [sub],
        packs,
        [pltpu.VMEM((own_rows, 2 * slots), BF), pltpu.VMEM((2 * CZ, 2 * slots), BF)],
        1 << 33,
    )
    edge_rows = HALO * NB1 * modes
    force = call(
        functools.partial(fluid_kernel, slots, modes, groups, groups),
        "fluid",
        jax.ShapeDtypeStruct((groups, 3, modes, local), F32),
        [sub],
        [*packs, low, high, source],
        [
            pltpu.VMEM((2, edge_rows, 2 * CZ), F32),
            pltpu.VMEM((CX + 2, CY + 2, modes, CZ), F32),
            pltpu.VMEM((CX * CY, modes, CZ), F32),
            pltpu.VMEM((edge_rows, 2 * slots), BF),
            pltpu.VMEM((2 * CZ, 2 * slots), BF),
            pltpu.VMEM((groups, modes, local), F32),
        ],
        1 << 33,
    )
    parts = [force[0]] + [shifted(force[k], "sub", k) for k in range(1, groups)]
    gram, mass = call(
        functools.partial(gram_kernel, modes, groups, groups),
        "gram",
        (
            jax.ShapeDtypeStruct((3 * modes, 4 * modes), F32),
            jax.ShapeDtypeStruct((modes, local), F32),
        ),
        [sub, block_cols],
        [*window, *parts, stiff, kstiff, diag, kblocks],
        [pltpu.VMEM((nwin, modes, bs), F32)],
        1 << 29,
    )
    gram = gram + swapped(gram, "passage", 1)
    gram = summed(gram, "passage", 1)
    gram = summed(gram, "sub", 0)
    return call(
        functools.partial(final_kernel, modes, float(total)),
        "final",
        (
            jax.ShapeDtypeStruct((modes, local), F32),
            jax.ShapeDtypeStruct((2 * modes, 2 * modes), F32),
            jax.ShapeDtypeStruct((2 * modes, 2 * modes), F32),
        ),
        [],
        [gram, stiff, mass],
        [],
        1 << 20,
    )


def solution(mesh):
    return jax.shard_map(
        body,
        mesh=mesh,
        in_specs=(
            P(None, ("passage", "sub")),
            P(("passage", "sub")),
            P(("passage", "sub")),
            P(("passage", "sub"), None, None, None),
            P(("passage", "sub"), None),
            P(("passage", "sub")),
            P(("passage", "sub"), None),
            P(("passage", "sub")),
            P(("passage", "sub")),
            P(("passage", "sub")),
        ),
        out_specs=(P(None, ("passage", "sub")), P(), P()),
        check_vma=False,
    )
```

time: 231 us -> 120 us (0.52)
  blocking collectives: 78.1 us -> 0 us
  Pallas kernels: 0 us -> 66.5 us
  other arithmetic: 54.2 us -> 4.22 us
  local copies, waits for them, and re-layouts: 27.1 us -> 6.53 us
  waiting for transfers between devices: 34.1 us -> 16.6 us
  starting transfers between devices: 32.8 us -> 24.4 us
    psum x2 -> x0, blocking collectives: 78.1 us -> none  [the longest x1 40.3 us: body(): lax.psum((inner(search, image), inner(search, search)), ('passage', 'sub'))]
    pallas_call x0 -> x6, Pallas kernels: none -> 66.5 us  [call(): pl.pallas_call(kernel, name=name, out_shape=out_shape, in_specs=[smem()]...]
    scatter-add x2 -> x0, other arithmetic: 24.9 us -> none  [the longest x1 15.6 us: body(): source = jnp.zeros((modes, CX * CY * CZ), jnp.float32).at[:, cells_in].ad...]
    all_to_all x3 -> x0, waiting for transfers between devices: 15.9 us -> none  [the longest x1 7.95 us: body(): lax.all_to_all(picked, 'sub', split_axis=1, concat_axis=1, tiled=True)]
    all_to_all x3 -> x0, starting transfers between devices: 15.7 us -> none  [the longest x1 5.94 us: body(): lax.all_to_all(cells_out, 'sub', split_axis=0, concat_axis=0, tiled=True)]
    add x3, other arithmetic: 15 us -> 1.44 us  [the longest x1 0.81 us: body(): gram = gram + swapped(gram, 'passage', 1)]
    gather x3 -> x0, local copies, waits for them, and re-layouts: 8.77 us -> none  [the longest x1 7.65 us: body(): picked = press[:, cells_in].reshape(modes, groups, capacity)]
    ppermute x8 -> x17, starting transfers between devices: 17.1 us -> 24.4 us  [the longest x10 16.5 us: shifted(): return lax.ppermute(x, axis, [(i, (i + k) % n) for i in range(n)])]
  transfers between devices with their start and end apart: 11 -> 17, of which waited for: 8 -> 10; matrix products, arithmetic and copies ran while one was open for 31% -> 0% of each run, Pallas kernels for 0% -> 17%
where the time goes in v1:
time: 120 us
  Pallas kernels  66.5 us (55%)
  starting transfers between devices  24.4 us (20%)
  waiting for transfers between devices  16.6 us (14%)
  local copies, waits for them, and re-layouts  6.53 us (5%)
  other arithmetic  4.22 us (4%)
  between operations  1.37 us (1%)
    pallas_call x6, Pallas kernels, call(): pl.pallas_call(kernel, name=name, out_shape=out_shape, in_specs=[smem()]...  66.5 us
    ppermute x10, starting transfers between devices, shifted(): return lax.ppermute(x, axis, [(i, (i + k) % n) for i in range(n)])  16.5 us
    ppermute x7, waiting for transfers between devices, swapped(): return lax.ppermute(x, axis, [(i, i ^ k) for i in range(n)])  10.3 us
    ppermute x7, starting transfers between devices, swapped(): return lax.ppermute(x, axis, [(i, i ^ k) for i in range(n)])  7.94 us
    ppermute x10, waiting for transfers between devices, shifted(): return lax.ppermute(x, axis, [(i, (i + k) % n) for i in range(n)])  6.29 us
    unnamed x22, local copies, waits for them, and re-layouts  3.27 us
  transfers between devices with their start and end apart: 17, of which 10 were waited for; matrix products, arithmetic and copies ran while one was open for 0% of the time, Pallas kernels for 17%

profile of v1, /device:TPU:0, one launch (start us, length us, event | category | flops | bytes accessed | tf_op | source)
XLA Modules:
  0.0 119.7 jit_solution(12091199456072413519)
XLA Ops:
  0.6 0.7 broadcast_multiply_fusion
  1.3 0.7 add_convert_fusion
  2.7 0.7 fusion
  4.1 1.5 %concatenate.3.refs_0_.own.refs_1_ = f32[48,256]{1,0:T(8,128)S(1)} concatenate(f32[32,256]{1,0:T(8,128)} %param.10, f32[1,256]{1,0:T(1,128)} %bitcast.23, f32[4,256]{1,0:T(4,128)S(1)} %reshape.21, f32[4,256]{1,0:T(4,128)S(1)} %reshape.22, f32[4,256]{1,0:T(4,128)S(1)} %reshape.23, f32[3,256]{1,0:T(4,128)S(1)} %broadcast_in_dim.15), dimensions={0} | concatenate | bytes 98304 | tf_op jit(solution)/shard_map/concatenate | solution.py:399
  5.6 3.1 %collective-permute-start = (f32[48,256]{1,0:T(8,128)S(1)}, f32[48,256]{1,0:T(8,128)S(1)}, u32[]{:S(2)}, u32[]{:S(2)}) collective-permute-start(f32[48,256]{1,0:T(8,128)S(1)} %concatenate.3.refs_0_.own.refs_1_), channel_id=1, source_target_pairs={{0,1},{1,2},{2,3},{3,0},{4,5},{5,6},{6,7},{7,4},{8,9},{9,10},{10,1... | collective-permute-start | bytes 147464 | tf_op jit(solution)/shard_map/ppermute | solution.py:326
  8.7 2.1 %collective-permute-start.1 = (f32[48,256]{1,0:T(8,128)S(1)}, f32[48,256]{1,0:T(8,128)S(1)}, u32[]{:S(2)}, u32[]{:S(2)}) collective-permute-start(f32[48,256]{1,0:T(8,128)S(1)} %concatenate.3.refs_0_.own.refs_1_), channel_id=1, source_target_pairs={{0,3},{1,0},{2,1},{3,2},{4,7},{5,4},{6,5},{7,6},{8,11},{9,8},{10,9... | collective-permute-start | bytes 147464 | tf_op jit(solution)/shard_map/ppermute | solution.py:326
  10.8 0.9 collective-permute-start.2
  11.8 1.2 collective-permute-done.refs_1_.prev.refs_0_
  13.3 2.6 %collective-permute-done.2.refs_2_ = f32[48,256]{1,0:T(8,128)S(1)} collective-permute-done((f32[48,256]{1,0:T(8,128)S(1)}, f32[48,256]{1,0:T(8,128)S(1)}, u32[]{:S(2)}, u32[]{:S(2)}) %collective-permute-start.2) | collective-permute-done | bytes 49184 | tf_op jit(solution)/shard_map/ppermute | solution.py:326
  16.0 2.6 %collective-permute-start.4 = (f32[4,48,256]{2,1,0:T(8,128)S(1)}, f32[4,48,256]{2,1,0:T(8,128)S(1)}, u32[]{:S(2)}, u32[]{:S(2)}) collective-permute-start(f32[4,48,256]{2,1,0:T(8,128)S(1)} %pad_maximum_fusion), channel_id=1, source_target_pairs={{0,28},{4,0},{8,4},{12,8},{16,12},{20,16},{24,20},{28,24},{1,29},{... | collective-permute-start | bytes 589832 | tf_op jit(solution)/shard_map/ppermute | solution.py:326
  18.7 15.7 %own_source.1.refs_6_ = f32[1536,256]{1,0:T(8,128)} custom-call(s32[1]{0:T(128)} %bitcast.sub_ref, f32[48,256]{1,0:T(8,128)} %copy-done, f32[48,256]{1,0:T(8,128)} %copy-done.1, f32[48,256]{1,0:T(8,128)} %copy-done.3, f32[48,256]{1,0:T(8,128)} %copy-done.2), custom_call_target="tpu_custom_call" | custom-call | flops 8589934592 | bytes 1048576 | tf_op jit(solution)/shard_map/own_source/pallas_call | solution.py:356
  35.7 41.5 %fluid.1 = f32[4,3,32,256]{3,2,1,0:T(8,128)} custom-call(s32[1]{0:T(128)} %bitcast.sub_ref, f32[48,256]{1,0:T(8,128)} %copy-done, f32[48,256]{1,0:T(8,128)} %copy-done.1, f32[48,256]{1,0:T(8,128)} %copy-done.3, f32[48,256]{1,0:T(8,128)} %copy-done.2, f32[4,48,256]{2,1,0:T(8,128)} %copy-done.4, f32[4,48,256]{2,1,0:T(8,128)} %copy-done.5, ...), custom_call_target="tpu_custom_call" | custom-call | flops 8589934592 | bytes 1048576 | tf_op jit(solution)/shard_map/fluid/pallas_call | solution.py:356
  77.3 1.7 %slice_bitcast_fusion = (f32[3,32,256]{2,1,0:T(8,128)S(1)}, f32[3,32,256]{2,1,0:T(8,128)S(1)}, f32[3,32,256]{2,1,0:T(8,128)S(1)}, f32[3,32,256]{2,1,0:T(8,128)}) fusion(f32[4,3,32,256]{3,2,1,0:T(8,128)} %fluid.1), kind=kLoop, calls=%fused_computation.1 | loop fusion | bytes 786432 | tf_op jit(solution)/shard_map/squeeze | solution.py:454
  79.1 2.8 %collective-permute-start.6 = (f32[3,32,256]{2,1,0:T(8,128)S(1)}, f32[3,32,256]{2,1,0:T(8,128)S(1)}, u32[]{:S(2)}, u32[]{:S(2)}) collective-permute-start(f32[3,32,256]{2,1,0:T(8,128)S(1)} %get-tuple-element.8), channel_id=1, source_target_pairs={{0,2},{1,3},{2,0},{3,1},{4,6},{5,7},{6,4},{7,5},{8,10},{9,11},{10,... | collective-permute-start | bytes 294920 | tf_op jit(solution)/shard_map/ppermute | solution.py:326
  81.8 1.0 collective-permute-start.7
  82.8 2.3 %stiff.1.own.refs_7_ = f32[32,256]{1,0:T(8,128)} custom-call(s32[1]{0:T(128)} %bitcast.sub_ref, s32[2,4]{1,0:T(2,128)} %cols_ref.5, f32[48,256]{1,0:T(8,128)} %copy-done.1, f32[48,256]{1,0:T(8,128)} %copy-done, f32[48,256]{1,0:T(8,128)} %copy-done.2, f32[1,256]{1,0:T(1,128)} %bitcast.24, f32[2,4,128,128]{3,2,1,0:T(8,128)} %refs_10_.1), custom_call_target="tpu_custom_call" | custom-call | flops 536870912 | bytes 1048576 | tf_op jit(solution)/shard_map/stiff/pallas_call | solution.py:356
  85.1 1.0 collective-permute-start.8
  86.2 2.8 %collective-permute-start.9 = (f32[32,256]{1,0:T(8,128)}, f32[32,256]{1,0:T(8,128)S(1)}, u32[]{:S(2)}, u32[]{:S(2)}) collective-permute-start(f32[32,256]{1,0:T(8,128)} %stiff.1.own.refs_7_), channel_id=1, source_target_pairs={{0,3},{1,0},{2,1},{3,2},{4,7},{5,4},{6,5},{7,6},{8,11},{9,8},{10,9... | collective-permute-start | bytes 98312 | tf_op jit(solution)/shard_map/ppermute | solution.py:326
  89.0 2.1 %collective-permute-done.8.prev = f32[32,256]{1,0:T(8,128)S(1)} collective-permute-done((f32[32,256]{1,0:T(8,128)}, f32[32,256]{1,0:T(8,128)S(1)}, u32[]{:S(2)}, u32[]{:S(2)}) %collective-permute-start.8) | collective-permute-done | bytes 32800 | tf_op jit(solution)/shard_map/ppermute | solution.py:326
  92.3 2.3 %stiff_image.1.refs_8_ = f32[32,256]{1,0:T(8,128)} custom-call(s32[1]{0:T(128)} %bitcast.sub_ref, s32[2,4]{1,0:T(2,128)} %cols_ref.5, f32[32,256]{1,0:T(8,128)} %copy-done.9, f32[32,256]{1,0:T(8,128)} %stiff.1.own.refs_7_, f32[32,256]{1,0:T(8,128)} %copy-done.10, f32[1,256]{1,0:T(1,128)} %bitcast.25, f32[2,4,128,128]{3,2,1,0:T(8,128)} %refs_10_.1), custom_call_target="tpu_custom_call" | custom-call | flops 536870912 | bytes 1048576 | tf_op jit(solution)/shard_map/stiff_image/pallas_call | solution.py:356
  95.3 2.8 %gram.1 = (f32[96,128]{1,0:T(8,128)}, f32[32,256]{1,0:T(8,128)}) custom-call(s32[1]{0:T(128)} %bitcast.sub_ref, s32[2,4]{1,0:T(2,128)} %cols_ref.5, f32[48,256]{1,0:T(8,128)} %copy-done.1, f32[48,256]{1,0:T(8,128)} %copy-done, f32[48,256]{1,0:T(8,128)} %copy-done.2, f32[3,32,256]{2,1,0:T(8,128)} %get-tuple-element.10.refs_3_, f32[3,32,256]{2,1,0:T(8,128)} %copy-done.6, ...), custom_call_target="tpu_custom_call" | custom-call | flops 536870912 | bytes 1048576 | tf_op jit(solution)/shard_map/gram/pallas_call | solution.py:356
  98.1 1.4 %collective-permute-done.10 = f32[96,128]{1,0:T(8,128)S(1)} collective-permute-done((f32[96,128]{1,0:T(8,128)}, f32[96,128]{1,0:T(8,128)S(1)}, u32[]{:S(2)}, u32[]{:S(2)}) %collective-permute-start.10) | collective-permute-done | bytes 49184 | tf_op jit(solution)/shard_map/ppermute | solution.py:331
  99.6 0.8 add.25
  100.4 0.7 collective-permute-start.11
  101.1 1.4 %collective-permute-start.12 = (f32[96,128]{1,0:T(8,128)S(1)}, f32[96,128]{1,0:T(8,128)S(1)}, u32[]{:S(2)}, u32[]{:S(2)}) collective-permute-start(f32[96,128]{1,0:T(8,128)S(1)} %add.25), channel_id=1, source_target_pairs={{0,16},{4,20},{8,24},{12,28},{16,0},{20,4},{24,8},{28,12},{1,17},{... | collective-permute-start | bytes 147464 | tf_op jit(solution)/shard_map/ppermute | solution.py:331
  102.5 1.3 %collective-permute-start.13 = (f32[96,128]{1,0:T(8,128)S(1)}, f32[96,128]{1,0:T(8,128)S(1)}, u32[]{:S(2)}, u32[]{:S(2)}) collective-permute-start(f32[96,128]{1,0:T(8,128)S(1)} %add.25), channel_id=1, source_target_pairs={{0,24},{4,28},{8,16},{12,20},{16,8},{20,12},{24,0},{28,4},{1,25},{... | collective-permute-start | bytes 147464 | tf_op jit(solution)/shard_map/ppermute | solution.py:331
  104.5 0.7 collective-permute-done.12
  105.2 2.3 %collective-permute-done.13 = f32[96,128]{1,0:T(8,128)S(1)} collective-permute-done((f32[96,128]{1,0:T(8,128)S(1)}, f32[96,128]{1,0:T(8,128)S(1)}, u32[]{:S(2)}, u32[]{:S(2)}) %collective-permute-start.13) | collective-permute-done | bytes 49184 | tf_op jit(solution)/shard_map/ppermute | solution.py:331
  107.9 3.5 %collective-permute-start.15 = (f32[96,128]{1,0:T(8,128)S(1)}, f32[96,128]{1,0:T(8,128)S(1)}, u32[]{:S(2)}, u32[]{:S(2)}) collective-permute-start(f32[96,128]{1,0:T(8,128)S(1)} %add_add_fusion.1), channel_id=1, source_target_pairs={{0,2},{1,3},{2,0},{3,1},{4,6},{5,7},{6,4},{7,5},{8,10},{9,11},{10,... | collective-permute-start | bytes 147464 | tf_op jit(solution)/shard_map/ppermute | solution.py:331
  112.0 1.4 %collective-permute-done.15 = f32[96,128]{1,0:T(8,128)S(1)} collective-permute-done((f32[96,128]{1,0:T(8,128)S(1)}, f32[96,128]{1,0:T(8,128)S(1)}, u32[]{:S(2)}, u32[]{:S(2)}) %collective-permute-start.15) | collective-permute-done | bytes 49184 | tf_op jit(solution)/shard_map/ppermute | solution.py:331
  113.4 3.8 %collective-permute-done.16 = f32[96,128]{1,0:T(8,128)S(1)} collective-permute-done((f32[96,128]{1,0:T(8,128)S(1)}, f32[96,128]{1,0:T(8,128)S(1)}, u32[]{:S(2)}, u32[]{:S(2)}) %collective-permute-start.16) | collective-permute-done | bytes 49184 | tf_op jit(solution)/shard_map/ppermute | solution.py:331
  117.9 1.8 %final.1 = (f32[32,256]{1,0:T(8,128)}, f32[64,64]{1,0:T(8,128)}, f32[64,64]{1,0:T(8,128)}) custom-call(f32[96,128]{1,0:T(8,128)} %add_add_fusion.gram, f32[32,256]{1,0:T(8,128)} %stiff.1.own.refs_7_, f32[32,256]{1,0:T(8,128)} %get-tuple-element.6.mass), custom_call_target="tpu_custom_call" | custom-call | flops 1048576 | bytes 1048576 | tf_op jit(solution)/shard_map/final/pallas_call | solution.py:356
  (44 shorter events, 6.8 us)
Async XLA Ops:
  5.6 13.0 %copy-start = (f32[48,256]{1,0:T(8,128)}, f32[48,256]{1,0:T(8,128)S(1)}, u32[]{:S(2)}) copy-start(f32[48,256]{1,0:T(8,128)S(1)} %concatenate.3.refs_0_.own.refs_1_) | copy-start | bytes 147460
  5.6 7.3 %collective-permute-start = (f32[48,256]{1,0:T(8,128)S(1)}, f32[48,256]{1,0:T(8,128)S(1)}, u32[]{:S(2)}, u32[]{:S(2)}) collective-permute-start(f32[48,256]{1,0:T(8,128)S(1)} %concatenate.3.refs_0_.own.refs_1_), channel_id=1, source_target_pairs={{0,1},{1,2},{2,3},{3,0},{4,5},{5,6},{6,7},{7,4},{8,9},{9,10},{10,1... | collective-permute-start | bytes 147464 | tf_op jit(solution)/shard_map/ppermute | solution.py:326
  8.7 4.6 %collective-permute-start.1 = (f32[48,256]{1,0:T(8,128)S(1)}, f32[48,256]{1,0:T(8,128)S(1)}, u32[]{:S(2)}, u32[]{:S(2)}) collective-permute-start(f32[48,256]{1,0:T(8,128)S(1)} %concatenate.3.refs_0_.own.refs_1_), channel_id=1, source_target_pairs={{0,3},{1,0},{2,1},{3,2},{4,7},{5,4},{6,5},{7,6},{8,11},{9,8},{10,9... | collective-permute-start | bytes 147464 | tf_op jit(solution)/shard_map/ppermute | solution.py:326
  10.8 5.1 %collective-permute-start.2 = (f32[48,256]{1,0:T(8,128)S(1)}, f32[48,256]{1,0:T(8,128)S(1)}, u32[]{:S(2)}, u32[]{:S(2)}) collective-permute-start(f32[48,256]{1,0:T(8,128)S(1)} %concatenate.3.refs_0_.own.refs_1_), channel_id=1, source_target_pairs={{0,2},{1,3},{2,0},{3,1},{4,6},{5,7},{6,4},{7,5},{8,10},{9,11},{10,... | collective-permute-start | bytes 147464 | tf_op jit(solution)/shard_map/ppermute | solution.py:326
  12.9 5.7 %copy-start.1 = (f32[48,256]{1,0:T(8,128)}, f32[48,256]{1,0:T(8,128)S(1)}, u32[]{:S(2)}) copy-start(f32[48,256]{1,0:T(8,128)S(1)} %collective-permute-done.refs_1_.prev.refs_0_) | copy-start | bytes 147460
  13.3 5.3 %copy-start.2 = (f32[48,256]{1,0:T(8,128)}, f32[48,256]{1,0:T(8,128)S(1)}, u32[]{:S(2)}) copy-start(f32[48,256]{1,0:T(8,128)S(1)} %collective-permute-done.1.refs_3_.nxt.refs_2_) | copy-start | bytes 147460
  15.9 2.7 %copy-start.3 = (f32[48,256]{1,0:T(8,128)}, f32[48,256]{1,0:T(8,128)S(1)}, u32[]{:S(2)}) copy-start(f32[48,256]{1,0:T(8,128)S(1)} %collective-permute-done.2.refs_2_) | copy-start | bytes 147460
  16.0 18.4 %collective-permute-start.3 = (f32[4,48,256]{2,1,0:T(8,128)S(1)}, f32[4,48,256]{2,1,0:T(8,128)S(1)}, u32[]{:S(2)}, u32[]{:S(2)}) collective-permute-start(f32[4,48,256]{2,1,0:T(8,128)S(1)} %pad_maximum_fusion), channel_id=1, source_target_pairs={{0,4},{4,8},{8,12},{12,16},{16,20},{20,24},{24,28},{28,0},{1,5},{5... | collective-permute-start | bytes 589832 | tf_op jit(solution)/shard_map/ppermute | solution.py:326
  16.0 18.4 %collective-permute-start.4 = (f32[4,48,256]{2,1,0:T(8,128)S(1)}, f32[4,48,256]{2,1,0:T(8,128)S(1)}, u32[]{:S(2)}, u32[]{:S(2)}) collective-permute-start(f32[4,48,256]{2,1,0:T(8,128)S(1)} %pad_maximum_fusion), channel_id=1, source_target_pairs={{0,28},{4,0},{8,4},{12,8},{16,12},{20,16},{24,20},{28,24},{1,29},{... | collective-permute-start | bytes 589832 | tf_op jit(solution)/shard_map/ppermute | solution.py:326
  34.4 0.7 copy-start.4
  35.1 0.7 copy-start.5
  79.0 15.6 %collective-permute-start.5 = (f32[3,32,256]{2,1,0:T(8,128)S(1)}, f32[3,32,256]{2,1,0:T(8,128)S(1)}, u32[]{:S(2)}, u32[]{:S(2)}) collective-permute-start(f32[3,32,256]{2,1,0:T(8,128)S(1)} %get-tuple-element.9), channel_id=1, source_target_pairs={{0,1},{1,2},{2,3},{3,0},{4,5},{5,6},{6,7},{7,4},{8,9},{9,10},{10,1... | collective-permute-start | bytes 294920 | tf_op jit(solution)/shard_map/ppermute | solution.py:326
  79.1 15.5 %collective-permute-start.6 = (f32[3,32,256]{2,1,0:T(8,128)S(1)}, f32[3,32,256]{2,1,0:T(8,128)S(1)}, u32[]{:S(2)}, u32[]{:S(2)}) collective-permute-start(f32[3,32,256]{2,1,0:T(8,128)S(1)} %get-tuple-element.8), channel_id=1, source_target_pairs={{0,2},{1,3},{2,0},{3,1},{4,6},{5,7},{6,4},{7,5},{8,10},{9,11},{10,... | collective-permute-start | bytes 294920 | tf_op jit(solution)/shard_map/ppermute | solution.py:326
  81.8 12.8 %collective-permute-start.7 = (f32[3,32,256]{2,1,0:T(8,128)S(1)}, f32[3,32,256]{2,1,0:T(8,128)S(1)}, u32[]{:S(2)}, u32[]{:S(2)}) collective-permute-start(f32[3,32,256]{2,1,0:T(8,128)S(1)} %get-tuple-element.7), channel_id=1, source_target_pairs={{0,3},{1,0},{2,1},{3,2},{4,7},{5,4},{6,5},{7,6},{8,11},{9,8},{10,9... | collective-permute-start | bytes 294920 | tf_op jit(solution)/shard_map/ppermute | solution.py:326
  85.1 5.9 %collective-permute-start.8 = (f32[32,256]{1,0:T(8,128)}, f32[32,256]{1,0:T(8,128)S(1)}, u32[]{:S(2)}, u32[]{:S(2)}) collective-permute-start(f32[32,256]{1,0:T(8,128)} %stiff.1.own.refs_7_), channel_id=1, source_target_pairs={{0,1},{1,2},{2,3},{3,0},{4,5},{5,6},{6,7},{7,4},{8,9},{9,10},{10,1... | collective-permute-start | bytes 98312 | tf_op jit(solution)/shard_map/ppermute | solution.py:326
  86.2 4.9 %collective-permute-start.9 = (f32[32,256]{1,0:T(8,128)}, f32[32,256]{1,0:T(8,128)S(1)}, u32[]{:S(2)}, u32[]{:S(2)}) collective-permute-start(f32[32,256]{1,0:T(8,128)} %stiff.1.own.refs_7_), channel_id=1, source_target_pairs={{0,3},{1,0},{2,1},{3,2},{4,7},{5,4},{6,5},{7,6},{8,11},{9,8},{10,9... | collective-permute-start | bytes 98312 | tf_op jit(solution)/shard_map/ppermute | solution.py:326
  91.1 0.6 copy-start.9
  91.7 0.6 copy-start.10
  94.6 0.6 copy-start.6
  94.6 0.7 copy-start.7
  94.6 0.7 copy-start.8
  98.1 1.4 %collective-permute-start.10 = (f32[96,128]{1,0:T(8,128)}, f32[96,128]{1,0:T(8,128)S(1)}, u32[]{:S(2)}, u32[]{:S(2)}) collective-permute-start(f32[96,128]{1,0:T(8,128)} %get-tuple-element.5), channel_id=1, source_target_pairs={{0,4},{4,0},{8,12},{12,8},{16,20},{20,16},{24,28},{28,24},{1,5},{5... | collective-permute-start | bytes 147464 | tf_op jit(solution)/shard_map/ppermute | solution.py:331
  100.4 4.1 %collective-permute-start.11 = (f32[96,128]{1,0:T(8,128)S(1)}, f32[96,128]{1,0:T(8,128)S(1)}, u32[]{:S(2)}, u32[]{:S(2)}) collective-permute-start(f32[96,128]{1,0:T(8,128)S(1)} %add.25), channel_id=1, source_target_pairs={{0,8},{4,12},{8,0},{12,4},{16,24},{20,28},{24,16},{28,20},{1,9},{5... | collective-permute-start | bytes 147464 | tf_op jit(solution)/shard_map/ppermute | solution.py:331
  101.1 4.1 %collective-permute-start.12 = (f32[96,128]{1,0:T(8,128)S(1)}, f32[96,128]{1,0:T(8,128)S(1)}, u32[]{:S(2)}, u32[]{:S(2)}) collective-permute-start(f32[96,128]{1,0:T(8,128)S(1)} %add.25), channel_id=1, source_target_pairs={{0,16},{4,20},{8,24},{12,28},{16,0},{20,4},{24,8},{28,12},{1,17},{... | collective-permute-start | bytes 147464 | tf_op jit(solution)/shard_map/ppermute | solution.py:331
  102.5 5.0 %collective-permute-start.13 = (f32[96,128]{1,0:T(8,128)S(1)}, f32[96,128]{1,0:T(8,128)S(1)}, u32[]{:S(2)}, u32[]{:S(2)}) collective-permute-start(f32[96,128]{1,0:T(8,128)S(1)} %add.25), channel_id=1, source_target_pairs={{0,24},{4,28},{8,16},{12,20},{16,8},{20,12},{24,0},{28,4},{1,25},{... | collective-permute-start | bytes 147464 | tf_op jit(solution)/shard_map/ppermute | solution.py:331
  107.5 4.5 %collective-permute-start.14 = (f32[96,128]{1,0:T(8,128)S(1)}, f32[96,128]{1,0:T(8,128)S(1)}, u32[]{:S(2)}, u32[]{:S(2)}) collective-permute-start(f32[96,128]{1,0:T(8,128)S(1)} %add_add_fusion.1), channel_id=1, source_target_pairs={{0,1},{1,0},{2,3},{3,2},{4,5},{5,4},{6,7},{7,6},{8,9},{9,8},{10,11... | collective-permute-start | bytes 147464 | tf_op jit(solution)/shard_map/ppermute | solution.py:331
  107.9 5.5 %collective-permute-start.15 = (f32[96,128]{1,0:T(8,128)S(1)}, f32[96,128]{1,0:T(8,128)S(1)}, u32[]{:S(2)}, u32[]{:S(2)}) collective-permute-start(f32[96,128]{1,0:T(8,128)S(1)} %add_add_fusion.1), channel_id=1, source_target_pairs={{0,2},{1,3},{2,0},{3,1},{4,6},{5,7},{6,4},{7,5},{8,10},{9,11},{10,... | collective-permute-start | bytes 147464 | tf_op jit(solution)/shard_map/ppermute | solution.py:331
  111.4 5.9 %collective-permute-start.16 = (f32[96,128]{1,0:T(8,128)S(1)}, f32[96,128]{1,0:T(8,128)S(1)}, u32[]{:S(2)}, u32[]{:S(2)}) collective-permute-start(f32[96,128]{1,0:T(8,128)S(1)} %add_add_fusion.1), channel_id=1, source_target_pairs={{0,3},{1,2},{2,1},{3,0},{4,7},{5,6},{6,5},{7,4},{8,11},{9,10},{10,... | collective-permute-start | bytes 147464 | tf_op jit(solution)/shard_map/ppermute | solution.py:331

commit v2 on v1

v2 whole, which is shorter than its diff:
```python
import functools
import jax
import jax.numpy as jnp
from jax import lax
from jax.experimental import pallas as pl
from jax.experimental.pallas import tpu as pltpu
from jax.sharding import PartitionSpec as P

CX = 8
CY = 8
CZ = 128
HALO = 2

center_weight = 15.0
lower_bound = 1.0 / 15.0
upper_bound = 17.0 / 15.0
middle = (upper_bound + lower_bound) / 2.0
radius = (upper_bound - lower_bound) / 2.0
sigma_ratio = middle / radius
first_rho = 1.0 / sigma_ratio
second_rho = 1.0 / (2.0 * sigma_ratio - first_rho)
third_rho = 1.0 / (2.0 * sigma_ratio - second_rho)

FIRST = 1.0 / (center_weight * middle)
GAIN2 = 2.0 * second_rho / (radius * center_weight)
SEC_U = FIRST * (1.0 + second_rho * first_rho) + GAIN2 * (1.0 - 17.0 * FIRST)
SEC_T = GAIN2 * 2.0 * FIRST
STEP3 = third_rho * second_rho
GAIN3 = 2.0 * third_rho / (radius * center_weight)
PRE_SRC = GAIN3 - STEP3 * FIRST
PRE_SEC = 1.0 + STEP3 - 17.0 * GAIN3
PRE_T = 2.0 * GAIN3

BF = jnp.bfloat16
F32 = jnp.float32
CELLS = CX * CY * CZ


def log2(n):
    return n.bit_length() - 1


def split(x):
    hi = x.astype(BF)
    return hi, (x - hi.astype(F32)).astype(BF)


def lanes_from(x, index):
    return jnp.take_along_axis(
        x, jnp.broadcast_to(index, x.shape), axis=1, mode="promise_in_bounds"
    )


def onehot(values, height):
    shape = (height, values.shape[1])
    rows = lax.broadcasted_iota(jnp.int32, shape, 0)
    return jnp.where(rows == values, 1.0, 0.0).astype(BF)


def dot_t(x, y):
    return lax.dot_general(x, y, (((1,), (1,)), ((), ())), preferred_element_type=F32)


def dot(x, y):
    return lax.dot_general(x, y, (((1,), (0,)), ((), ())), preferred_element_type=F32)


def pack_kernel(modes, groups, live_ref, v_ref, owner_ref, cell_ref, node_ref, weight_ref, out):
    deep, wide = owner_ref.shape
    capacity = 2 * deep * wide // groups
    keys = groups * CX
    owner, cell, weight = owner_ref[...], cell_ref[...], weight_ref[...]
    shape = (deep, wide)
    place = lax.broadcasted_iota(jnp.int32, shape, 0) * wide + lax.broadcasted_iota(
        jnp.int32, shape, 1
    )
    live = place < live_ref[0]
    a = lax.shift_right_logical(cell, log2(CY * CZ))
    key = jnp.where(live, owner * CX + ((a + HALO) & (CX - 1)), -1)
    hots = jnp.concatenate([jnp.where(key == k, 1.0, 0.0) for k in range(keys)], axis=0).astype(BF)
    rows = lax.broadcasted_iota(jnp.int32, (wide, wide), 0)
    lanes = lax.broadcasted_iota(jnp.int32, (wide, wide), 1)
    within = dot(hots, jnp.where(rows <= lanes, 1.0, 0.0).astype(BF))
    size = keys * deep
    rows = lax.broadcasted_iota(jnp.int32, (size, size), 0)
    lanes = lax.broadcasted_iota(jnp.int32, (size, size), 1)
    shift = log2(CX * deep)
    same = lax.shift_right_logical(rows, shift) == lax.shift_right_logical(lanes, shift)
    earlier = jnp.where(same & (lanes < rows), 1.0, 0.0).astype(BF)
    ahead = dot(dot(earlier, hots).astype(BF), jnp.ones((wide, wide), BF))
    order = within + ahead - 1.0
    pos = jnp.zeros(shape, F32)
    for k in range(keys):
        pos = jnp.where(key == k, order[k * deep : (k + 1) * deep], pos)
    target = owner * capacity + pos.astype(jnp.int32)
    line = lax.shift_right_logical(target, log2(wide))
    half = deep
    line = jnp.where(live, lax.shift_right_logical(line, 1) + (line & 1) * half, -1)
    lane = target & (wide - 1)
    w1 = weight.astype(BF).astype(F32)
    w2 = (weight - w1).astype(BF).astype(F32)
    values = [
        lax.shift_right_logical(cell, 8).astype(F32),
        (cell & 255).astype(F32),
        node_ref[...].astype(F32),
        w1,
        w2,
        weight - w1 - w2,
    ]
    lefts, rights = [], []
    for r in range(deep):
        into = lax.broadcasted_iota(jnp.int32, (2 * half, wide), 0) == line[r : r + 1]
        lefts.append(
            jnp.concatenate([jnp.where(into, v[r : r + 1], 0.0) for v in values], axis=0).astype(BF)
        )
        rights.append(onehot(lane[r : r + 1], wide))
    listed = dot_t(jnp.concatenate(lefts, axis=1), jnp.concatenate(rights, axis=1))
    part = [listed[i * 2 * half : (i + 1) * 2 * half] for i in range(6)]
    lists = [256.0 * part[0] + part[1], part[2], part[3] + part[4] + part[5]]
    out[0:modes, :] = v_ref[...]
    for i, x in enumerate(lists):
        at = modes + i * half
        out[at : at + half, 0:wide] = x[:half]
        out[at : at + half, wide : 2 * wide] = x[half:]


class Lists:
    def __init__(self, blk, modes, capacity):
        self.blk, self.modes = blk, modes
        self.local = blk.shape[1]
        self.lines = (blk.shape[0] - modes) // 3
        self.width = min(self.local, capacity)
        self.capacity = capacity
        self.chunks = capacity // self.width

    def row(self, kind, owner, chunk):
        at = owner * self.capacity + chunk * self.width
        line = lax.shift_right_logical(at, log2(self.local))
        x = self.blk[pl.ds(self.modes + kind * self.lines + line, 1), :]
        if self.width < self.local:
            group = lax.shift_right_logical(at, log2(self.width)) & (self.local // self.width - 1)
            got = x[:, : self.width]
            for g in range(1, self.local // self.width):
                got = jnp.where(group == g, x[:, g * self.width : (g + 1) * self.width], got)
            x = got
        return x

    def load(self, owner, chunk):
        cell = self.row(0, owner, chunk).astype(jnp.int32)
        node = self.row(1, owner, chunk).astype(jnp.int32)
        weight = self.row(2, owner, chunk)
        a = lax.shift_right_logical(cell, log2(CY * CZ))
        b = lax.shift_right_logical(cell, log2(CZ)) & (CY - 1)
        return a, b, cell & (CZ - 1), node, weight


def fill(lists, owner, chunk, a_first, a_count, b_first, b_count, inside, lhs, rhs, at, side):
    modes, width = lists.modes, lists.width
    a, b, c, node, weight = lists.load(owner, chunk)
    if inside is not None:
        weight = weight * inside
    aloc, bloc = a - a_first, b - b_first
    valid = (aloc >= 0) & (aloc < a_count) & (bloc >= 0) & (bloc < 2 * b_count)
    pair = jnp.where(valid, aloc * b_count + lax.shift_right_arithmetic(bloc, 1), -1)
    place = (b & 1) * CZ + c
    pieces = []
    for h in range(width // 128):
        idx = node[:, h * 128 : (h + 1) * 128]
        got = None
        for g in range(lists.local // 128):
            part = lanes_from(lists.blk[0:modes, g * 128 : (g + 1) * 128], idx & 127)
            got = part if g == 0 else jnp.where(lax.shift_right_logical(idx, 7) == g, part, got)
        pieces.append(got)
    hi, lo = split(jnp.concatenate(pieces, axis=1) * weight)
    wide = jnp.broadcast_to(pair.astype(F32), (modes, width)).astype(BF)
    zero = jnp.zeros((modes, width), BF)
    for r in range(a_count * b_count):
        mask = wide == jnp.asarray(r, BF)
        lhs[r * modes : (r + 1) * modes, at : at + width] = jnp.where(mask, hi, zero)
        lhs[r * modes : (r + 1) * modes, at + width : at + 2 * width] = jnp.where(mask, lo, zero)
    hot = onehot(place, 2 * CZ)
    rhs[:, at : at + width] = hot
    rhs[:, at + width : at + 2 * width] = hot


def scatter(blks, modes, capacity, owner, inside, a_first, a_count, b_first, b_count, out, lhs, rhs):
    every = [Lists(blk, modes, capacity) for blk in blks]
    width = every[0].width
    rows = a_count * b_count * modes
    spec = (a_first, a_count, b_first, b_count, inside)
    left = lhs.at[0:rows, :]
    for k, lists in enumerate(every):
        fill(lists, owner, 0, *spec, left, rhs, 2 * k * width, None)
    deep = 2 * width * len(every)
    out[...] = dot_t(lhs[0:rows, 0:deep], rhs[:, 0:deep])
    for lists in every:
        for chunk in range(1, lists.chunks):
            a, b, c, node, weight = lists.load(owner, chunk)
            needed = jnp.where((a >= a_first) & (a < a_first + a_count), weight, 0.0)

            @pl.when(jnp.max(needed) > 0.0)
            def _():
                fill(lists, owner, chunk, *spec, left, rhs, 0, None)
                out[...] += dot_t(lhs[0:rows, 0 : 2 * width], rhs[:, 0 : 2 * width])


def around(sub, groups):
    below = jnp.maximum(sub - 1, 0), jnp.where(sub > 0, 1.0, 0.0)
    above = jnp.minimum(sub + 1, groups - 1), jnp.where(sub < groups - 1, 1.0, 0.0)
    return below, above


def own_source_kernel(modes, groups, capacity, sub_ref, *refs):
    blks = refs[:groups]
    own, below, above, lhs, rhs = refs[groups:]
    sub = sub_ref[0]
    (lo_owner, lo_in), (hi_owner, hi_in) = around(sub, groups)
    scatter(blks, modes, capacity, sub, None, 0, CX, 0, CY // 2, own, lhs, rhs)
    scatter(blks, modes, capacity, lo_owner, lo_in, 0, CX, CY - HALO, HALO // 2, below, lhs, rhs)
    scatter(blks, modes, capacity, hi_owner, hi_in, 0, CX, 0, HALO // 2, above, lhs, rhs)


def shift_sum(x):
    lane = lax.broadcasted_iota(jnp.int32, x.shape, 1)
    left = jnp.where(lane == 0, 0.0, pltpu.roll(x, 1, 1))
    right = jnp.where(lane == CZ - 1, 0.0, pltpu.roll(x, CZ - 1, 1))
    return x + 0.5 * (left + right)


def fluid_kernel(modes, groups, capacity, sub_ref, *refs):
    blks = refs[:groups]
    low, high, mid, below, above, mdiag = refs[groups : groups + 6]
    outs = refs[groups + 6 : 2 * groups + 6]
    edge, corner, second, press, lhs, rhs, force = refs[2 * groups + 6 :]
    sub = sub_ref[0]
    local = blks[0].shape[1]
    half = HALO // 2
    (lo_owner, lo_in), (hi_owner, hi_in) = around(sub, groups)
    for side, both in enumerate((low, high)):
        there = [both.at[k] for k in range(groups)]
        a_first = CX - HALO if side == 0 else 0
        args = (there, modes, capacity)
        scatter(*args, sub, None, a_first, HALO, 0, CY // 2, edge.at[side], lhs, rhs)
        scatter(
            *args, lo_owner, lo_in, a_first, HALO, CY - HALO, half, corner.at[2 * side], lhs, rhs
        )
        scatter(*args, hi_owner, hi_in, a_first, HALO, 0, half, corner.at[2 * side + 1], lhs, rhs)

    def src(a, b):
        lanes = slice((b % 2) * CZ, (b % 2 + 1) * CZ)
        outer = -1
        if a < HALO:
            outer, a = 0, a
        elif a >= CX + HALO:
            outer, a = 1, a - CX - HALO
        else:
            a = a - HALO
        if b < HALO:
            ref, at = (below if outer < 0 else corner.at[2 * outer]), a * half + b // 2
        elif b >= CY + HALO:
            ref = above if outer < 0 else corner.at[2 * outer + 1]
            at = a * half + (b - CY - HALO) // 2
        else:
            ref, at = (mid if outer < 0 else edge.at[outer]), a * (CY // 2) + (b - HALO) // 2
        return ref[at * modes : (at + 1) * modes, lanes]

    for a in range(1, CX + 2 * HALO - 1):
        cols = [
            src(a, b) + 0.5 * (src(a - 1, b) + src(a + 1, b)) for b in range(CY + 2 * HALO)
        ]
        for b in range(1, CY + 2 * HALO - 1):
            t = shift_sum(cols[b] + 0.5 * (cols[b - 1] + cols[b + 1]))
            sec = SEC_U * src(a, b) + SEC_T * t
            if b < HALO:
                sec = sec * lo_in
            if b >= CY + HALO:
                sec = sec * hi_in
            second[a - 1, b - 1] = sec
    for a in range(CX):
        cols = [
            second[a + 1, b] + 0.5 * (second[a, b] + second[a + 2, b]) for b in range(CY + 2)
        ]
        for b in range(CY):
            t = shift_sum(cols[b + 1] + 0.5 * (cols[b] + cols[b + 2]))
            p = PRE_SRC * src(a + HALO, b + HALO) + PRE_SEC * second[a + 1, b + 1] + PRE_T * t
            hi, lo = split(p)
            at = (a * (CY // 2) + b // 2) * modes
            lanes = (b % 2) * CZ
            press[at : at + modes, lanes : lanes + CZ] = hi
            press[at : at + modes, 2 * CZ + lanes : 3 * CZ + lanes] = lo

    def collect(lists, chunk):
        a, b, c, node, weight = lists.load(sub, chunk)
        hot = onehot((b & 1) * CZ + c, 2 * CZ)
        got = dot(press[...], jnp.concatenate([hot, hot], axis=0))
        pair = a * (CY // 2) + lax.shift_right_logical(b, 1)
        wide = jnp.broadcast_to(pair, (modes, lists.width))
        picked = jnp.zeros((modes, lists.width), F32)
        for r in range(CX * CY // 2):
            picked = jnp.where(wide == r, got[r * modes : (r + 1) * modes], picked)
        hi, lo = split(picked * weight)
        both = dot_t(jnp.concatenate([hi, lo], axis=0), onehot(node, local))
        return both[:modes] + both[modes:]

    every = [Lists(blk, modes, capacity) for blk in blks]
    for k, lists in enumerate(every):
        add = collect(lists, 0)
        force[k] = add + mdiag[...] * blks[0][0:modes, :] if k == 0 else add
        for chunk in range(1, lists.chunks):

            @pl.when(jnp.max(lists.row(2, sub, chunk)) > 0.0)
            def _():
                force[k] += collect(lists, chunk)

    for k in range(groups):
        for w in range(3):
            outs[k][w] = force[(1 - k - w) % groups]


def apply_blocks(window, cols_ref, kb_ref, sub, groups, diag, field):
    rb, nb, bs, _ = kb_ref.shape
    pieces = []
    for q in range(rb):
        acc = None
        for n in range(nb):
            j = cols_ref[q, n]
            where = sub + j // rb - 1
            inside = jnp.where((where >= 0) & (where < groups), 1.0, 0.0)
            part = lax.dot_general(
                window[j] * inside,
                kb_ref[q, n],
                (((1,), (0,)), ((), ())),
                precision=lax.Precision.HIGHEST,
                preferred_element_type=F32,
            )
            acc = part if acc is None else acc + part
        pieces.append(acc)
    return diag * field + jnp.concatenate(pieces, axis=1)


def fill_window(win, blocks, bs):
    at = 0
    for blk in blocks:
        for i in range(blk.shape[1] // bs):
            win[at] = blk[:, i * bs : (i + 1) * bs]
            at += 1


def stiff_kernel(modes, groups, sub_ref, cols_ref, prev, own, nxt, diag, kb, out, win):
    bs = kb.shape[2]
    fill_window(win, [prev[0:modes, :], own[0:modes, :], nxt[0:modes, :]], bs)
    out[...] = apply_blocks(win, cols_ref, kb, sub_ref[0], groups, diag[...], own[0:modes, :])


def gram_kernel(modes, groups, sub_ref, cols_ref, v_ref, *refs):
    parts = refs[:groups]
    stiff, kstiff, diag, kb, gram, mass, win = refs[groups:]
    bs = kb.shape[2]
    fields = []
    for w in range(3):
        m = parts[0][w]
        for part in parts[1:]:
            m = m + part[w]
        fields.append(m)
    fill_window(win, fields, bs)
    own = fields[1]
    mass[...] = own
    km = apply_blocks(win, cols_ref, kb, sub_ref[0], groups, diag[...], own)
    v = v_ref[...]
    s = stiff[...]
    left = jnp.concatenate([v, s, own], axis=0)
    right = jnp.concatenate([s, kstiff[...], km, own], axis=0)

    def inner(x, y):
        return lax.dot_general(
            x,
            y,
            (((1,), (1,)), ((), ())),
            precision=lax.Precision.HIGHEST,
            preferred_element_type=F32,
        )

    gram[...] = inner(left, right)
    gram[2 * modes : 3 * modes, 0:modes] = inner(v, v)


def final_kernel(modes, total, gram, stiff, mass, residual, g_stiff, g_plain):
    m = modes
    blocks = [
        [gram[i * m : (i + 1) * m, j * m : (j + 1) * m] for j in range(4)] for i in range(3)
    ]
    (vs, vks, vkm, vm), (ss, sks, skm, sm), (vv, mks, mkm, mm) = blocks
    rows = lax.broadcasted_iota(jnp.int32, (m, m), 0)
    lanes = lax.broadcasted_iota(jnp.int32, (m, m), 1)
    eye = rows == lanes

    def column(x):
        return jnp.sum(jnp.where(eye, x, 0.0), axis=1, keepdims=True)

    def line(x):
        return jnp.sum(jnp.where(eye, x, 0.0), axis=0, keepdims=True)

    tc = column(vs) / column(vm)
    tl = line(vs) / line(vm)
    residual[...] = stiff[...] - tc * mass[...]
    ms = sm.T
    scale = 1.0 / total
    vr = vs - vm * tl
    g_plain[0:m, 0:m] = vv * scale
    g_plain[0:m, m : 2 * m] = vr * scale
    g_plain[m : 2 * m, 0:m] = vr.T * scale
    g_plain[m : 2 * m, m : 2 * m] = (ss - sm * tl - tc * (ms - mm * tl)) * scale
    g_stiff[0:m, 0:m] = vs * scale
    g_stiff[0:m, m : 2 * m] = (vks - vkm * tl) * scale
    g_stiff[m : 2 * m, 0:m] = (ss - tc * ms) * scale
    g_stiff[m : 2 * m, m : 2 * m] = (sks - skm * tl - tc * (mks - mkm * tl)) * scale


def shifted(x, axis, k):
    n = lax.axis_size(axis)
    return lax.ppermute(x, axis, [(i, (i + k) % n) for i in range(n)])


def swapped(x, axis, k):
    n = lax.axis_size(axis)
    return lax.ppermute(x, axis, [(i, i ^ k) for i in range(n)])


def summed(x, axis, bit):
    n = lax.axis_size(axis)
    while (1 << bit) < n:
        if (4 << bit) <= n:
            one, two, three = [swapped(x, axis, k << bit) for k in (1, 2, 3)]
            x = (x + one) + (two + three)
            bit += 2
        else:
            x = x + swapped(x, axis, 1 << bit)
            bit += 1
    return x


def smem():
    return pl.BlockSpec(memory_space=pltpu.SMEM)


def vmem():
    return pl.BlockSpec(memory_space=pltpu.VMEM)


def call(kernel, name, out_shape, scalars, arrays, scratch, flops):
    return pl.pallas_call(
        kernel,
        name=name,
        out_shape=out_shape,
        in_specs=[smem()] * len(scalars) + [vmem()] * len(arrays),
        out_specs=jax.tree.map(lambda _: vmem(), out_shape),
        scratch_shapes=scratch,
        cost_estimate=pl.CostEstimate(flops=flops, transcendentals=0, bytes_accessed=1 << 20),
    )(*scalars, *arrays)


def body(
    block_vectors,
    stiffness,
    mass_diag,
    kblocks,
    block_cols,
    slot_node,
    slot_owner,
    slot_cell,
    slot_weight,
    live_slots,
):
    modes, local = block_vectors.shape
    groups = lax.axis_size("sub")
    slots = slot_node.shape[0]
    bs = kblocks.shape[2]
    total = local * lax.axis_size("passage") * groups
    sub = lax.axis_index("sub").astype(jnp.int32).reshape(1)
    deep, wide = slots // 128, 128
    capacity = 2 * slots // groups
    pack = call(
        functools.partial(pack_kernel, modes, groups),
        "pack",
        jax.ShapeDtypeStruct((modes + 3 * deep, local), F32),
        [live_slots],
        [block_vectors]
        + [x.reshape(deep, wide) for x in (slot_owner, slot_cell, slot_node, slot_weight)],
        [],
        1 << 28,
    )
    packs = [pack] + [shifted(pack, "sub", k) for k in range(1, groups)]
    both = jnp.stack(packs)
    low = shifted(both, "passage", 1)
    high = shifted(both, "passage", -1)
    diag = stiffness[None, :]
    window = [packs[1], packs[0], packs[groups - 1]]
    nwin = 3 * local // bs
    stiff = call(
        functools.partial(stiff_kernel, modes, groups),
        "stiff",
        jax.ShapeDtypeStruct((modes, local), F32),
        [sub, block_cols],
        [*window, diag, kblocks],
        [pltpu.VMEM((nwin, modes, bs), F32)],
        1 << 29,
    )
    stiff_prev = shifted(stiff, "sub", 1)
    stiff_next = shifted(stiff, "sub", -1)
    kstiff = call(
        functools.partial(stiff_kernel, modes, groups),
        "stiff_image",
        jax.ShapeDtypeStruct((modes, local), F32),
        [sub, block_cols],
        [stiff_prev, stiff, stiff_next, diag, kblocks],
        [pltpu.VMEM((nwin, modes, bs), F32)],
        1 << 29,
    )
    pairs = CY // 2
    half = HALO // 2
    width = min(local, capacity)
    rhs = pltpu.VMEM((2 * CZ, 2 * width * groups), BF)

    def field(*shape):
        return jax.ShapeDtypeStruct(shape, F32)

    source = call(
        functools.partial(own_source_kernel, modes, groups, capacity),
        "own_source",
        (
            field(CX * pairs * modes, 2 * CZ),
            field(CX * half * modes, 2 * CZ),
            field(CX * half * modes, 2 * CZ),
        ),
        [sub],
        packs,
        [pltpu.VMEM((CX * pairs * modes, 2 * width * groups), BF), rhs],
        1 << 32,
    )
    force = call(
        functools.partial(fluid_kernel, modes, groups, capacity),
        "fluid",
        tuple(field(3, modes, local) for _ in range(groups)),
        [sub],
        [*packs, low, high, *source, mass_diag[None, :]],
        [
            pltpu.VMEM((2, HALO * pairs * modes, 2 * CZ), F32),
            pltpu.VMEM((4, HALO * half * modes, 2 * CZ), F32),
            pltpu.VMEM((CX + 2, CY + 2, modes, CZ), F32),
            pltpu.VMEM((CX * pairs * modes, 4 * CZ), BF),
            pltpu.VMEM((HALO * pairs * modes, 2 * width * groups), BF),
            rhs,
            pltpu.VMEM((groups, modes, local), F32),
        ],
        1 << 32,
    )
    parts = [force[0]] + [shifted(force[k], "sub", k) for k in range(1, groups)]
    gram, mass = call(
        functools.partial(gram_kernel, modes, groups),
        "gram",
        (field(3 * modes, 4 * modes), field(modes, local)),
        [sub, block_cols],
        [block_vectors, *parts, stiff, kstiff, diag, kblocks],
        [pltpu.VMEM((nwin, modes, bs), F32)],
        1 << 29,
    )
    gram = gram + swapped(gram, "passage", 1)
    gram = summed(gram, "passage", 1)
    gram = summed(gram, "sub", 0)
    return call(
        functools.partial(final_kernel, modes, float(total)),
        "final",
        (
            jax.ShapeDtypeStruct((modes, local), F32),
            jax.ShapeDtypeStruct((2 * modes, 2 * modes), F32),
            jax.ShapeDtypeStruct((2 * modes, 2 * modes), F32),
        ),
        [],
        [gram, stiff, mass],
        [],
        1 << 20,
    )


def solution(mesh):
    return jax.shard_map(
        body,
        mesh=mesh,
        in_specs=(
            P(None, ("passage", "sub")),
            P(("passage", "sub")),
            P(("passage", "sub")),
            P(("passage", "sub"), None, None, None),
            P(("passage", "sub"), None),
            P(("passage", "sub")),
            P(("passage", "sub"), None),
            P(("passage", "sub")),
            P(("passage", "sub")),
            P(("passage", "sub")),
        ),
        out_specs=(P(None, ("passage", "sub")), P(), P()),
        check_vma=False,
    )
```

time: 120 us -> 81.9 us (0.68)
  Pallas kernels: 66.5 us -> 29.1 us
  starting transfers between devices: 24.4 us -> 28.5 us
  local copies, waits for them, and re-layouts: 6.53 us -> 2.69 us
  other arithmetic: 4.22 us -> 2.3 us
    pallas_call x6 -> x7, Pallas kernels: 66.5 us -> 29.1 us  [call(): pl.pallas_call(kernel, name=name, out_shape=out_shape, in_specs=[smem()]...]
    ppermute x10, starting transfers between devices: 16.5 us -> 20.6 us  [shifted(): return lax.ppermute(x, axis, [(i, (i + k) % n) for i in range(n)])]
    squeeze x1 -> x0, local copies, waits for them, and re-layouts: 1.7 us -> none  [body(): parts = [force[0]] + [shifted(force[k], 'sub', k) for k in range(1, groups)]]
    concatenate x1 -> x0, local copies, waits for them, and re-layouts: 1.53 us -> none  [body(): pack = jnp.concatenate(pieces, axis=0)]
    convert_element_type x2 -> x0, other arithmetic: 1.38 us -> none  [the longest x1 0.69 us: body(): flat = (slot_owner[:, 0] * CELLS + slot_cell).astype(F32)]
    unnamed x22 -> x20, local copies, waits for them, and re-layouts: 3.27 us -> 2.69 us
  transfers between devices with their start and end apart: 17 -> 17, of which waited for: 10 -> 10; matrix products, arithmetic and copies ran while one was open for 0% -> 0% of each run, Pallas kernels for 17% -> 13%
where the time goes in v2:
time: 81.9 us; the launch traced here: 81.5 us
  Pallas kernels  29.1 us (36%)
  starting transfers between devices  28.5 us (35%)
  waiting for transfers between devices  17.5 us (21%)
  local copies, waits for them, and re-layouts  2.69 us (3%)
  other arithmetic  2.3 us (3%)
  between operations  1.39 us (2%)
    pallas_call x7, Pallas kernels, call(): pl.pallas_call(kernel, name=name, out_shape=out_shape, in_specs=[smem()]...  29.1 us
    ppermute x10, starting transfers between devices, shifted(): return lax.ppermute(x, axis, [(i, (i + k) % n) for i in range(n)])  20.6 us
    ppermute x7, waiting for transfers between devices, swapped(): return lax.ppermute(x, axis, [(i, i ^ k) for i in range(n)])  10.6 us
    ppermute x7, starting transfers between devices, swapped(): return lax.ppermute(x, axis, [(i, i ^ k) for i in range(n)])  7.94 us
    ppermute x10, waiting for transfers between devices, shifted(): return lax.ppermute(x, axis, [(i, (i + k) % n) for i in range(n)])  6.93 us
    unnamed x20, local copies, waits for them, and re-layouts  2.69 us
  transfers between devices with their start and end apart: 17, of which 10 were waited for; matrix products, arithmetic and copies ran while one was open for 0% of the time, Pallas kernels for 13%

profile of v2, /device:TPU:0, one launch (start us, length us, event | category | flops | bytes accessed | tf_op | source)
XLA Modules:
  0.0 81.5 jit_solution(16335725580941884983)
XLA Ops:
  1.3 2.0 %pack.1.refs_0_.own = f32[56,256]{1,0:T(8,128)} custom-call(s32[1]{0:T(128)S(6)} %copy.13.live_ref, f32[32,256]{1,0:T(8,128)} %v_ref.3, s32[8,128]{1,0:T(8,128)} %bitcast.15, s32[8,128]{1,0:T(8,128)} %bitcast.16, s32[8,128]{1,0:T(8,128)} %bitcast.17, f32[8,128]{1,0:T(8,128)} %bitcast.18), custom_call_target="tpu_custom_call" | custom-call | flops 268435456 | bytes 1048576 | tf_op jit(solution)/shard_map/pack/pallas_call | solution.py:451
  3.3 3.1 %collective-permute-start = (f32[56,256]{1,0:T(8,128)}, f32[56,256]{1,0:T(8,128)S(1)}, u32[]{:S(2)}, u32[]{:S(2)}) collective-permute-start(f32[56,256]{1,0:T(8,128)} %pack.1.refs_0_.own), channel_id=1, source_target_pairs={{0,1},{1,2},{2,3},{3,0},{4,5},{5,6},{6,7},{7,4},{8,9},{9,10},{10,1... | collective-permute-start | bytes 172040 | tf_op jit(solution)/shard_map/ppermute | solution.py:421
  6.4 2.0 %collective-permute-start.2 = (f32[56,256]{1,0:T(8,128)}, f32[56,256]{1,0:T(8,128)S(1)}, u32[]{:S(2)}, u32[]{:S(2)}) collective-permute-start(f32[56,256]{1,0:T(8,128)} %pack.1.refs_0_.own), channel_id=1, source_target_pairs={{0,3},{1,0},{2,1},{3,2},{4,7},{5,4},{6,5},{7,6},{8,11},{9,8},{10,9... | collective-permute-start | bytes 172040 | tf_op jit(solution)/shard_map/ppermute | solution.py:421
  8.4 1.0 %collective-permute-start.1 = (f32[56,256]{1,0:T(8,128)}, f32[56,256]{1,0:T(8,128)S(1)}, u32[]{:S(2)}, u32[]{:S(2)}) collective-permute-start(f32[56,256]{1,0:T(8,128)} %pack.1.refs_0_.own), channel_id=1, source_target_pairs={{0,2},{1,3},{2,0},{3,1},{4,6},{5,7},{6,4},{7,5},{8,10},{9,11},{10,... | collective-permute-start | bytes 172040 | tf_op jit(solution)/shard_map/ppermute | solution.py:421
  9.4 1.4 %collective-permute-done.refs_1_.prev = f32[56,256]{1,0:T(8,128)S(1)} collective-permute-done((f32[56,256]{1,0:T(8,128)}, f32[56,256]{1,0:T(8,128)S(1)}, u32[]{:S(2)}, u32[]{:S(2)}) %collective-permute-start) | collective-permute-done | bytes 57376 | tf_op jit(solution)/shard_map/ppermute | solution.py:421
  11.4 2.9 %collective-permute-done.1.refs_2_ = f32[56,256]{1,0:T(8,128)S(1)} collective-permute-done((f32[56,256]{1,0:T(8,128)}, f32[56,256]{1,0:T(8,128)S(1)}, u32[]{:S(2)}, u32[]{:S(2)}) %collective-permute-start.1) | collective-permute-done | bytes 57376 | tf_op jit(solution)/shard_map/ppermute | solution.py:421
  14.2 0.9 %pad_maximum_fusion = f32[4,56,256]{2,1,0:T(8,128)S(1)} fusion(f32[1,56,256]{2,1,0:T(8,128)S(1)} %bitcast.13, f32[1,56,256]{2,1,0:T(8,128)S(1)} %bitcast.14, f32[1,56,256]{2,1,0:T(8,128)S(1)} %bitcast.12, f32[1,56,256]{2,1,0:T(8,128)} %bitcast.11), kind=kLoop, calls=%fused_computation | loop fusion | flops 172032 | bytes 458752 | tf_op jit(solution)/shard_map/stack | solution.py:493
  15.2 2.6 %collective-permute-start.4 = (f32[4,56,256]{2,1,0:T(8,128)S(1)}, f32[4,56,256]{2,1,0:T(8,128)S(1)}, u32[]{:S(2)}, u32[]{:S(2)}) collective-permute-start(f32[4,56,256]{2,1,0:T(8,128)S(1)} %pad_maximum_fusion), channel_id=1, source_target_pairs={{0,28},{4,0},{8,4},{12,8},{16,12},{20,16},{24,20},{28,24},{1,29},{... | collective-permute-start | bytes 688136 | tf_op jit(solution)/shard_map/ppermute | solution.py:421
  17.8 5.7 %own_source.1 = (f32[1024,256]{1,0:T(8,128)}, f32[256,256]{1,0:T(8,128)}, f32[256,256]{1,0:T(8,128)}) custom-call(s32[1]{0:T(128)} %bitcast.sub_ref, f32[56,256]{1,0:T(8,128)} %pack.1.refs_0_.own, f32[56,256]{1,0:T(8,128)} %copy-done, f32[56,256]{1,0:T(8,128)} %copy-done.2, f32[56,256]{1,0:T(8,128)} %copy-done.1), custom_call_target="tpu_custom_call" | custom-call | flops 4294967296 | bytes 1048576 | tf_op jit(solution)/shard_map/own_source/pallas_call | solution.py:451
  23.6 0.7 copy-done.3
  24.3 12.1 %fluid.1 = (f32[3,32,256]{2,1,0:T(8,128)}, f32[3,32,256]{2,1,0:T(8,128)}, f32[3,32,256]{2,1,0:T(8,128)}, f32[3,32,256]{2,1,0:T(8,128)}) custom-call(s32[1]{0:T(128)} %bitcast.sub_ref, f32[56,256]{1,0:T(8,128)} %pack.1.refs_0_.own, f32[56,256]{1,0:T(8,128)} %copy-done, f32[56,256]{1,0:T(8,128)} %copy-done.2, f32[56,256]{1,0:T(8,128)} %copy-done.1, ...), custom_call_target="tpu_custom_call" | custom-call | flops 4294967296 | bytes 1048576 | tf_op jit(solution)/shard_map/fluid/pallas_call | solution.py:451
  36.5 1.0 %collective-permute-start.5 = (f32[3,32,256]{2,1,0:T(8,128)}, f32[3,32,256]{2,1,0:T(8,128)S(1)}, u32[]{:S(2)}, u32[]{:S(2)}) collective-permute-start(f32[3,32,256]{2,1,0:T(8,128)} %get-tuple-element.16), channel_id=1, source_target_pairs={{0,1},{1,2},{2,3},{3,0},{4,5},{5,6},{6,7},{7,4},{8,9},{9,10},{10,1... | collective-permute-start | bytes 294920 | tf_op jit(solution)/shard_map/ppermute | solution.py:421
  37.4 4.1 %collective-permute-start.6 = (f32[3,32,256]{2,1,0:T(8,128)}, f32[3,32,256]{2,1,0:T(8,128)S(1)}, u32[]{:S(2)}, u32[]{:S(2)}) collective-permute-start(f32[3,32,256]{2,1,0:T(8,128)} %get-tuple-element.17), channel_id=1, source_target_pairs={{0,2},{1,3},{2,0},{3,1},{4,6},{5,7},{6,4},{7,5},{8,10},{9,11},{10,... | collective-permute-start | bytes 294920 | tf_op jit(solution)/shard_map/ppermute | solution.py:421
  41.5 2.9 %collective-permute-start.7 = (f32[3,32,256]{2,1,0:T(8,128)}, f32[3,32,256]{2,1,0:T(8,128)S(1)}, u32[]{:S(2)}, u32[]{:S(2)}) collective-permute-start(f32[3,32,256]{2,1,0:T(8,128)} %get-tuple-element.18), channel_id=1, source_target_pairs={{0,3},{1,0},{2,1},{3,2},{4,7},{5,4},{6,5},{7,6},{8,11},{9,8},{10,9... | collective-permute-start | bytes 294920 | tf_op jit(solution)/shard_map/ppermute | solution.py:421
  44.4 2.3 %stiff.1.own.refs_4_ = f32[32,256]{1,0:T(8,128)} custom-call(s32[1]{0:T(128)} %bitcast.sub_ref, s32[2,4]{1,0:T(2,128)} %cols_ref.5, f32[56,256]{1,0:T(8,128)} %copy-done, f32[56,256]{1,0:T(8,128)} %pack.1.refs_0_.own, f32[56,256]{1,0:T(8,128)} %copy-done.1, f32[1,256]{1,0:T(1,128)} %bitcast.20, f32[2,4,128,128]{3,2,1,0:T(8,128)} %refs_7_.1), custom_call_target="tpu_custom_call" | custom-call | flops 536870912 | bytes 1048576 | tf_op jit(solution)/shard_map/stiff/pallas_call | solution.py:451
  46.7 3.8 %collective-permute-start.9 = (f32[32,256]{1,0:T(8,128)}, f32[32,256]{1,0:T(8,128)S(1)}, u32[]{:S(2)}, u32[]{:S(2)}) collective-permute-start(f32[32,256]{1,0:T(8,128)} %stiff.1.own.refs_4_), channel_id=1, source_target_pairs={{0,3},{1,0},{2,1},{3,2},{4,7},{5,4},{6,5},{7,6},{8,11},{9,8},{10,9... | collective-permute-start | bytes 98312 | tf_op jit(solution)/shard_map/ppermute | solution.py:421
  50.6 2.1 %collective-permute-done.8.prev = f32[32,256]{1,0:T(8,128)S(1)} collective-permute-done((f32[32,256]{1,0:T(8,128)}, f32[32,256]{1,0:T(8,128)S(1)}, u32[]{:S(2)}, u32[]{:S(2)}) %collective-permute-start.8) | collective-permute-done | bytes 32800 | tf_op jit(solution)/shard_map/ppermute | solution.py:421
  53.3 0.6 copy-done.9
  53.9 2.3 %stiff_image.1.refs_5_ = f32[32,256]{1,0:T(8,128)} custom-call(s32[1]{0:T(128)} %bitcast.sub_ref, s32[2,4]{1,0:T(2,128)} %cols_ref.5, f32[32,256]{1,0:T(8,128)} %copy-done.8, f32[32,256]{1,0:T(8,128)} %stiff.1.own.refs_4_, f32[32,256]{1,0:T(8,128)} %copy-done.9, f32[1,256]{1,0:T(1,128)} %bitcast.21, f32[2,4,128,128]{3,2,1,0:T(8,128)} %refs_7_.1), custom_call_target="tpu_custom_call" | custom-call | flops 536870912 | bytes 1048576 | tf_op jit(solution)/shard_map/stiff_image/pallas_call | solution.py:451
  56.9 2.8 %gram.1 = (f32[96,128]{1,0:T(8,128)}, f32[32,256]{1,0:T(8,128)}) custom-call(s32[1]{0:T(128)} %bitcast.sub_ref, s32[2,4]{1,0:T(2,128)} %cols_ref.5, f32[32,256]{1,0:T(8,128)} %v_ref.3, f32[3,32,256]{2,1,0:T(8,128)} %get-tuple-element.15.refs_0_, f32[3,32,256]{2,1,0:T(8,128)} %copy-done.5, f32[3,32,256]{2,1,0:T(8,128)} %copy-done.6, f32[3,32,256]{2,1,0:T(8,128)} %copy-done.7, ...), custom_call_target="tpu_custom_call" | custom-call | flops 536870912 | bytes 1048576 | tf_op jit(solution)/shard_map/gram/pallas_call | solution.py:451
  59.7 1.4 %collective-permute-done.10 = f32[96,128]{1,0:T(8,128)S(1)} collective-permute-done((f32[96,128]{1,0:T(8,128)}, f32[96,128]{1,0:T(8,128)S(1)}, u32[]{:S(2)}, u32[]{:S(2)}) %collective-permute-start.10) | collective-permute-done | bytes 49184 | tf_op jit(solution)/shard_map/ppermute | solution.py:426
  61.1 0.8 add.21
  61.9 0.9 %collective-permute-start.11 = (f32[96,128]{1,0:T(8,128)S(1)}, f32[96,128]{1,0:T(8,128)S(1)}, u32[]{:S(2)}, u32[]{:S(2)}) collective-permute-start(f32[96,128]{1,0:T(8,128)S(1)} %add.21), channel_id=1, source_target_pairs={{0,8},{4,12},{8,0},{12,4},{16,24},{20,28},{24,16},{28,20},{1,9},{5... | collective-permute-start | bytes 147464 | tf_op jit(solution)/shard_map/ppermute | solution.py:426
  62.8 1.5 %collective-permute-start.12 = (f32[96,128]{1,0:T(8,128)S(1)}, f32[96,128]{1,0:T(8,128)S(1)}, u32[]{:S(2)}, u32[]{:S(2)}) collective-permute-start(f32[96,128]{1,0:T(8,128)S(1)} %add.21), channel_id=1, source_target_pairs={{0,16},{4,20},{8,24},{12,28},{16,0},{20,4},{24,8},{28,12},{1,17},{... | collective-permute-start | bytes 147464 | tf_op jit(solution)/shard_map/ppermute | solution.py:426
  64.3 1.1 %collective-permute-start.13 = (f32[96,128]{1,0:T(8,128)S(1)}, f32[96,128]{1,0:T(8,128)S(1)}, u32[]{:S(2)}, u32[]{:S(2)}) collective-permute-start(f32[96,128]{1,0:T(8,128)S(1)} %add.21), channel_id=1, source_target_pairs={{0,24},{4,28},{8,16},{12,20},{16,8},{20,12},{24,0},{28,4},{1,25},{... | collective-permute-start | bytes 147464 | tf_op jit(solution)/shard_map/ppermute | solution.py:426
  66.0 0.9 %collective-permute-done.12 = f32[96,128]{1,0:T(8,128)S(1)} collective-permute-done((f32[96,128]{1,0:T(8,128)S(1)}, f32[96,128]{1,0:T(8,128)S(1)}, u32[]{:S(2)}, u32[]{:S(2)}) %collective-permute-start.12) | collective-permute-done | bytes 49184 | tf_op jit(solution)/shard_map/ppermute | solution.py:426
  66.9 2.4 %collective-permute-done.13 = f32[96,128]{1,0:T(8,128)S(1)} collective-permute-done((f32[96,128]{1,0:T(8,128)S(1)}, f32[96,128]{1,0:T(8,128)S(1)}, u32[]{:S(2)}, u32[]{:S(2)}) %collective-permute-start.13) | collective-permute-done | bytes 49184 | tf_op jit(solution)/shard_map/ppermute | solution.py:426
  69.4 3.8 %collective-permute-start.15 = (f32[96,128]{1,0:T(8,128)S(1)}, f32[96,128]{1,0:T(8,128)S(1)}, u32[]{:S(2)}, u32[]{:S(2)}) collective-permute-start(f32[96,128]{1,0:T(8,128)S(1)} %add_add_fusion.1), channel_id=1, source_target_pairs={{0,2},{1,3},{2,0},{3,1},{4,6},{5,7},{6,4},{7,5},{8,10},{9,11},{10,... | collective-permute-start | bytes 147464 | tf_op jit(solution)/shard_map/ppermute | solution.py:426
  73.8 1.5 %collective-permute-done.15 = f32[96,128]{1,0:T(8,128)S(1)} collective-permute-done((f32[96,128]{1,0:T(8,128)S(1)}, f32[96,128]{1,0:T(8,128)S(1)}, u32[]{:S(2)}, u32[]{:S(2)}) %collective-permute-start.15) | collective-permute-done | bytes 49184 | tf_op jit(solution)/shard_map/ppermute | solution.py:426
  75.2 3.8 %collective-permute-done.16 = f32[96,128]{1,0:T(8,128)S(1)} collective-permute-done((f32[96,128]{1,0:T(8,128)S(1)}, f32[96,128]{1,0:T(8,128)S(1)}, u32[]{:S(2)}, u32[]{:S(2)}) %collective-permute-start.16) | collective-permute-done | bytes 49184 | tf_op jit(solution)/shard_map/ppermute | solution.py:426
  79.1 0.6 add_add_fusion.gram
  79.7 1.8 %final.1 = (f32[32,256]{1,0:T(8,128)}, f32[64,64]{1,0:T(8,128)}, f32[64,64]{1,0:T(8,128)}) custom-call(f32[96,128]{1,0:T(8,128)} %add_add_fusion.gram, f32[32,256]{1,0:T(8,128)} %stiff.1.own.refs_4_, f32[32,256]{1,0:T(8,128)} %get-tuple-element.20.mass), custom_call_target="tpu_custom_call" | custom-call | flops 1048576 | bytes 1048576 | tf_op jit(solution)/shard_map/final/pallas_call | solution.py:451
  (33 shorter events, 3.3 us)
Async XLA Ops:
  3.3 7.5 %collective-permute-start = (f32[56,256]{1,0:T(8,128)}, f32[56,256]{1,0:T(8,128)S(1)}, u32[]{:S(2)}, u32[]{:S(2)}) collective-permute-start(f32[56,256]{1,0:T(8,128)} %pack.1.refs_0_.own), channel_id=1, source_target_pairs={{0,1},{1,2},{2,3},{3,0},{4,5},{5,6},{6,7},{7,4},{8,9},{9,10},{10,1... | collective-permute-start | bytes 172040 | tf_op jit(solution)/shard_map/ppermute | solution.py:421
  6.4 5.0 %collective-permute-start.2 = (f32[56,256]{1,0:T(8,128)}, f32[56,256]{1,0:T(8,128)S(1)}, u32[]{:S(2)}, u32[]{:S(2)}) collective-permute-start(f32[56,256]{1,0:T(8,128)} %pack.1.refs_0_.own), channel_id=1, source_target_pairs={{0,3},{1,0},{2,1},{3,2},{4,7},{5,4},{6,5},{7,6},{8,11},{9,8},{10,9... | collective-permute-start | bytes 172040 | tf_op jit(solution)/shard_map/ppermute | solution.py:421
  8.4 5.8 %collective-permute-start.1 = (f32[56,256]{1,0:T(8,128)}, f32[56,256]{1,0:T(8,128)S(1)}, u32[]{:S(2)}, u32[]{:S(2)}) collective-permute-start(f32[56,256]{1,0:T(8,128)} %pack.1.refs_0_.own), channel_id=1, source_target_pairs={{0,2},{1,3},{2,0},{3,1},{4,6},{5,7},{6,4},{7,5},{8,10},{9,11},{10,... | collective-permute-start | bytes 172040 | tf_op jit(solution)/shard_map/ppermute | solution.py:421
  10.8 4.3 %copy-start = (f32[56,256]{1,0:T(8,128)}, f32[56,256]{1,0:T(8,128)S(1)}, u32[]{:S(2)}) copy-start(f32[56,256]{1,0:T(8,128)S(1)} %collective-permute-done.refs_1_.prev) | copy-start | bytes 172036
  11.4 3.7 %copy-start.1 = (f32[56,256]{1,0:T(8,128)}, f32[56,256]{1,0:T(8,128)S(1)}, u32[]{:S(2)}) copy-start(f32[56,256]{1,0:T(8,128)S(1)} %collective-permute-done.2.refs_3_.nxt) | copy-start | bytes 172036
  14.2 0.9 %copy-start.2 = (f32[56,256]{1,0:T(8,128)}, f32[56,256]{1,0:T(8,128)S(1)}, u32[]{:S(2)}) copy-start(f32[56,256]{1,0:T(8,128)S(1)} %collective-permute-done.1.refs_2_) | copy-start | bytes 172036
  15.1 8.4 %collective-permute-start.3 = (f32[4,56,256]{2,1,0:T(8,128)S(1)}, f32[4,56,256]{2,1,0:T(8,128)S(1)}, u32[]{:S(2)}, u32[]{:S(2)}) collective-permute-start(f32[4,56,256]{2,1,0:T(8,128)S(1)} %pad_maximum_fusion), channel_id=1, source_target_pairs={{0,4},{4,8},{8,12},{12,16},{16,20},{20,24},{24,28},{28,0},{1,5},{5... | collective-permute-start | bytes 688136 | tf_op jit(solution)/shard_map/ppermute | solution.py:421
  15.2 8.4 %collective-permute-start.4 = (f32[4,56,256]{2,1,0:T(8,128)S(1)}, f32[4,56,256]{2,1,0:T(8,128)S(1)}, u32[]{:S(2)}, u32[]{:S(2)}) collective-permute-start(f32[4,56,256]{2,1,0:T(8,128)S(1)} %pad_maximum_fusion), channel_id=1, source_target_pairs={{0,28},{4,0},{8,4},{12,8},{16,12},{20,16},{24,20},{28,24},{1,29},{... | collective-permute-start | bytes 688136 | tf_op jit(solution)/shard_map/ppermute | solution.py:421
  23.6 0.7 copy-start.3
  23.6 0.8 copy-start.4
  36.5 19.7 %collective-permute-start.5 = (f32[3,32,256]{2,1,0:T(8,128)}, f32[3,32,256]{2,1,0:T(8,128)S(1)}, u32[]{:S(2)}, u32[]{:S(2)}) collective-permute-start(f32[3,32,256]{2,1,0:T(8,128)} %get-tuple-element.16), channel_id=1, source_target_pairs={{0,1},{1,2},{2,3},{3,0},{4,5},{5,6},{6,7},{7,4},{8,9},{9,10},{10,1... | collective-permute-start | bytes 294920 | tf_op jit(solution)/shard_map/ppermute | solution.py:421
  37.4 18.8 %collective-permute-start.6 = (f32[3,32,256]{2,1,0:T(8,128)}, f32[3,32,256]{2,1,0:T(8,128)S(1)}, u32[]{:S(2)}, u32[]{:S(2)}) collective-permute-start(f32[3,32,256]{2,1,0:T(8,128)} %get-tuple-element.17), channel_id=1, source_target_pairs={{0,2},{1,3},{2,0},{3,1},{4,6},{5,7},{6,4},{7,5},{8,10},{9,11},{10,... | collective-permute-start | bytes 294920 | tf_op jit(solution)/shard_map/ppermute | solution.py:421
  41.5 14.7 %collective-permute-start.7 = (f32[3,32,256]{2,1,0:T(8,128)}, f32[3,32,256]{2,1,0:T(8,128)S(1)}, u32[]{:S(2)}, u32[]{:S(2)}) collective-permute-start(f32[3,32,256]{2,1,0:T(8,128)} %get-tuple-element.18), channel_id=1, source_target_pairs={{0,3},{1,0},{2,1},{3,2},{4,7},{5,4},{6,5},{7,6},{8,11},{9,8},{10,9... | collective-permute-start | bytes 294920 | tf_op jit(solution)/shard_map/ppermute | solution.py:421
  46.7 5.9 %collective-permute-start.8 = (f32[32,256]{1,0:T(8,128)}, f32[32,256]{1,0:T(8,128)S(1)}, u32[]{:S(2)}, u32[]{:S(2)}) collective-permute-start(f32[32,256]{1,0:T(8,128)} %stiff.1.own.refs_4_), channel_id=1, source_target_pairs={{0,1},{1,2},{2,3},{3,0},{4,5},{5,6},{6,7},{7,4},{8,9},{9,10},{10,1... | collective-permute-start | bytes 98312 | tf_op jit(solution)/shard_map/ppermute | solution.py:421
  46.7 5.9 %collective-permute-start.9 = (f32[32,256]{1,0:T(8,128)}, f32[32,256]{1,0:T(8,128)S(1)}, u32[]{:S(2)}, u32[]{:S(2)}) collective-permute-start(f32[32,256]{1,0:T(8,128)} %stiff.1.own.refs_4_), channel_id=1, source_target_pairs={{0,3},{1,0},{2,1},{3,2},{4,7},{5,4},{6,5},{7,6},{8,11},{9,8},{10,9... | collective-permute-start | bytes 98312 | tf_op jit(solution)/shard_map/ppermute | solution.py:421
  52.7 0.6 copy-start.8
  53.3 0.6 copy-start.9
  56.2 0.6 copy-start.5
  56.2 0.7 copy-start.6
  56.2 0.7 copy-start.7
  59.7 1.4 %collective-permute-start.10 = (f32[96,128]{1,0:T(8,128)}, f32[96,128]{1,0:T(8,128)S(1)}, u32[]{:S(2)}, u32[]{:S(2)}) collective-permute-start(f32[96,128]{1,0:T(8,128)} %get-tuple-element.19), channel_id=1, source_target_pairs={{0,4},{4,0},{8,12},{12,8},{16,20},{20,16},{24,28},{28,24},{1,5},{5... | collective-permute-start | bytes 147464 | tf_op jit(solution)/shard_map/ppermute | solution.py:426
  61.9 4.1 %collective-permute-start.11 = (f32[96,128]{1,0:T(8,128)S(1)}, f32[96,128]{1,0:T(8,128)S(1)}, u32[]{:S(2)}, u32[]{:S(2)}) collective-permute-start(f32[96,128]{1,0:T(8,128)S(1)} %add.21), channel_id=1, source_target_pairs={{0,8},{4,12},{8,0},{12,4},{16,24},{20,28},{24,16},{28,20},{1,9},{5... | collective-permute-start | bytes 147464 | tf_op jit(solution)/shard_map/ppermute | solution.py:426
  62.8 4.1 %collective-permute-start.12 = (f32[96,128]{1,0:T(8,128)S(1)}, f32[96,128]{1,0:T(8,128)S(1)}, u32[]{:S(2)}, u32[]{:S(2)}) collective-permute-start(f32[96,128]{1,0:T(8,128)S(1)} %add.21), channel_id=1, source_target_pairs={{0,16},{4,20},{8,24},{12,28},{16,0},{20,4},{24,8},{28,12},{1,17},{... | collective-permute-start | bytes 147464 | tf_op jit(solution)/shard_map/ppermute | solution.py:426
  64.3 5.0 %collective-permute-start.13 = (f32[96,128]{1,0:T(8,128)S(1)}, f32[96,128]{1,0:T(8,128)S(1)}, u32[]{:S(2)}, u32[]{:S(2)}) collective-permute-start(f32[96,128]{1,0:T(8,128)S(1)} %add.21), channel_id=1, source_target_pairs={{0,24},{4,28},{8,16},{12,20},{16,8},{20,12},{24,0},{28,4},{1,25},{... | collective-permute-start | bytes 147464 | tf_op jit(solution)/shard_map/ppermute | solution.py:426
  69.3 4.5 %collective-permute-start.14 = (f32[96,128]{1,0:T(8,128)S(1)}, f32[96,128]{1,0:T(8,128)S(1)}, u32[]{:S(2)}, u32[]{:S(2)}) collective-permute-start(f32[96,128]{1,0:T(8,128)S(1)} %add_add_fusion.1), channel_id=1, source_target_pairs={{0,1},{1,0},{2,3},{3,2},{4,5},{5,4},{6,7},{7,6},{8,9},{9,8},{10,11... | collective-permute-start | bytes 147464 | tf_op jit(solution)/shard_map/ppermute | solution.py:426
  69.4 5.8 %collective-permute-start.15 = (f32[96,128]{1,0:T(8,128)S(1)}, f32[96,128]{1,0:T(8,128)S(1)}, u32[]{:S(2)}, u32[]{:S(2)}) collective-permute-start(f32[96,128]{1,0:T(8,128)S(1)} %add_add_fusion.1), channel_id=1, source_target_pairs={{0,2},{1,3},{2,0},{3,1},{4,6},{5,7},{6,4},{7,5},{8,10},{9,11},{10,... | collective-permute-start | bytes 147464 | tf_op jit(solution)/shard_map/ppermute | solution.py:426
  73.2 5.9 %collective-permute-start.16 = (f32[96,128]{1,0:T(8,128)S(1)}, f32[96,128]{1,0:T(8,128)S(1)}, u32[]{:S(2)}, u32[]{:S(2)}) collective-permute-start(f32[96,128]{1,0:T(8,128)S(1)} %add_add_fusion.1), channel_id=1, source_target_pairs={{0,3},{1,2},{2,1},{3,0},{4,7},{5,6},{6,5},{7,4},{8,11},{9,10},{10,... | collective-permute-start | bytes 147464 | tf_op jit(solution)/shard_map/ppermute | solution.py:426

commit v3 on v2

--- a/solution.py
+++ b/solution.py
@@ -65,7 +65,18 @@
     return lax.dot_general(x, y, (((1,), (0,)), ((), ())), preferred_element_type=F32)
 
 
-def pack_kernel(modes, groups, live_ref, v_ref, owner_ref, cell_ref, node_ref, weight_ref, out):
+def pack_kernel(modes, groups, live_ref, *refs):
+    sources, (out, mdiag, diag, cols) = refs[:8], refs[8:12]
+    owner_ref, cell_ref, node_ref, weight_ref, sems = refs[12:]
+    targets = [owner_ref, cell_ref, node_ref, weight_ref]
+    targets += [out.at[0:modes, :], mdiag, diag, cols]
+    copies = [
+        pltpu.make_async_copy(x, y, sems.at[i]) for i, (x, y) in enumerate(zip(sources, targets))
+    ]
+    for copy in copies:
+        copy.start()
+    for copy in copies[:4]:
+        copy.wait()
     deep, wide = owner_ref.shape
     capacity = 2 * deep * wide // groups
     keys = groups * CX
@@ -117,19 +128,20 @@
     listed = dot_t(jnp.concatenate(lefts, axis=1), jnp.concatenate(rights, axis=1))
     part = [listed[i * 2 * half : (i + 1) * 2 * half] for i in range(6)]
     lists = [256.0 * part[0] + part[1], part[2], part[3] + part[4] + part[5]]
-    out[0:modes, :] = v_ref[...]
     for i, x in enumerate(lists):
         at = modes + i * half
         out[at : at + half, 0:wide] = x[:half]
         out[at : at + half, wide : 2 * wide] = x[half:]
+    for copy in copies[4:]:
+        copy.wait()
 
 
 class Lists:
-    def __init__(self, blk, modes, capacity):
+    def __init__(self, blk, modes, capacity, width=None):
         self.blk, self.modes = blk, modes
         self.local = blk.shape[1]
         self.lines = (blk.shape[0] - modes) // 3
-        self.width = min(self.local, capacity)
+        self.width = min(width or self.local, capacity)
         self.capacity = capacity
         self.chunks = capacity // self.width
 
@@ -183,25 +195,35 @@
     rhs[:, at + width : at + 2 * width] = hot
 
 
-def scatter(blks, modes, capacity, owner, inside, a_first, a_count, b_first, b_count, out, lhs, rhs):
-    every = [Lists(blk, modes, capacity) for blk in blks]
+def scatter(
+    blks, modes, capacity, owner, inside, a_first, a_count, b_first, b_count, out, lhs, rhs, width=None
+):
+    every = [Lists(blk, modes, capacity, width) for blk in blks]
     width = every[0].width
     rows = a_count * b_count * modes
     spec = (a_first, a_count, b_first, b_count, inside)
     left = lhs.at[0:rows, :]
+    counts = []
     for k, lists in enumerate(every):
+        last = jnp.zeros((1, width), jnp.int32)
+        for chunk in range(1, lists.chunks):
+            a, b, c, node, weight = lists.load(owner, chunk)
+            needed = (weight > 0.0) & (a >= a_first) & (a < a_first + a_count)
+            last = jnp.where(needed, chunk + 1, last)
+        counts.append(jnp.max(last))
         fill(lists, owner, 0, *spec, left, rhs, 2 * k * width, None)
     deep = 2 * width * len(every)
     out[...] = dot_t(lhs[0:rows, 0:deep], rhs[:, 0:deep])
-    for lists in every:
-        for chunk in range(1, lists.chunks):
-            a, b, c, node, weight = lists.load(owner, chunk)
-            needed = jnp.where((a >= a_first) & (a < a_first + a_count), weight, 0.0)
-
-            @pl.when(jnp.max(needed) > 0.0)
-            def _():
-                fill(lists, owner, chunk, *spec, left, rhs, 0, None)
-                out[...] += dot_t(lhs[0:rows, 0 : 2 * width], rhs[:, 0 : 2 * width])
+    if every[0].chunks == 1:
+        return
+    for lists, count in zip(every, counts):
+
+        def more(chunk, carry):
+            fill(lists, owner, chunk, *spec, left, rhs, 0, None)
+            out[...] += dot_t(lhs[0:rows, 0 : 2 * width], rhs[:, 0 : 2 * width])
+            return carry
+
+        lax.fori_loop(1, count, more, 0)
 
 
 def around(sub, groups):
@@ -212,7 +234,7 @@
 
 def own_source_kernel(modes, groups, capacity, sub_ref, *refs):
     blks = refs[:groups]
-    own, below, above, lhs, rhs = refs[groups:]
+    own, below, above, lhs, rhs = refs[groups + 1 :]
     sub = sub_ref[0]
     (lo_owner, lo_in), (hi_owner, hi_in) = around(sub, groups)
     scatter(blks, modes, capacity, sub, None, 0, CX, 0, CY // 2, own, lhs, rhs)
@@ -229,9 +251,9 @@
 
 def fluid_kernel(modes, groups, capacity, sub_ref, *refs):
     blks = refs[:groups]
-    low, high, mid, below, above, mdiag = refs[groups : groups + 6]
-    outs = refs[groups + 6 : 2 * groups + 6]
-    edge, corner, second, press, lhs, rhs, force = refs[2 * groups + 6 :]
+    low, high, mid, below, above, mdiag, stiff = refs[groups : groups + 7]
+    outs = refs[groups + 7 : 2 * groups + 7]
+    edge, corner, second, press, lhs, rhs, force = refs[2 * groups + 7 :]
     sub = sub_ref[0]
     local = blks[0].shape[1]
     half = HALO // 2
@@ -239,12 +261,12 @@
     for side, both in enumerate((low, high)):
         there = [both.at[k] for k in range(groups)]
         a_first = CX - HALO if side == 0 else 0
+        wide = 128 if side == 0 else 256
         args = (there, modes, capacity)
-        scatter(*args, sub, None, a_first, HALO, 0, CY // 2, edge.at[side], lhs, rhs)
-        scatter(
-            *args, lo_owner, lo_in, a_first, HALO, CY - HALO, half, corner.at[2 * side], lhs, rhs
-        )
-        scatter(*args, hi_owner, hi_in, a_first, HALO, 0, half, corner.at[2 * side + 1], lhs, rhs)
+        scatter(*args, sub, None, a_first, HALO, 0, CY // 2, edge.at[side], lhs, rhs, wide)
+        spec = (a_first, HALO, CY - HALO, half)
+        scatter(*args, lo_owner, lo_in, *spec, corner.at[2 * side], lhs, rhs, wide)
+        scatter(*args, hi_owner, hi_in, a_first, HALO, 0, half, corner.at[2 * side + 1], lhs, rhs, wide)
 
     def src(a, b):
         lanes = slice((b % 2) * CZ, (b % 2 + 1) * CZ)
@@ -315,6 +337,8 @@
     for k in range(groups):
         for w in range(3):
             outs[k][w] = force[(1 - k - w) % groups]
+        if k in (1, groups - 1):
+            outs[k][3] = stiff[...]
 
 
 def apply_blocks(window, cols_ref, kb_ref, sub, groups, diag, field):
@@ -352,9 +376,9 @@
     out[...] = apply_blocks(win, cols_ref, kb, sub_ref[0], groups, diag[...], own[0:modes, :])
 
 
-def gram_kernel(modes, groups, sub_ref, cols_ref, v_ref, *refs):
+def gram_kernel(modes, groups, sub_ref, cols_ref, pack, *refs):
     parts = refs[:groups]
-    stiff, kstiff, diag, kb, gram, mass, win = refs[groups:]
+    stiff, diag, kb, keep, send, mass, win, gram = refs[groups:]
     bs = kb.shape[2]
     fields = []
     for w in range(3):
@@ -362,14 +386,16 @@
         for part in parts[1:]:
             m = m + part[w]
         fields.append(m)
-    fill_window(win, fields, bs)
     own = fields[1]
     mass[...] = own
-    km = apply_blocks(win, cols_ref, kb, sub_ref[0], groups, diag[...], own)
-    v = v_ref[...]
     s = stiff[...]
+    ends = [parts[1][3], s, parts[groups - 1][3]]
+    both = [jnp.concatenate([x, y], axis=0) for x, y in zip(ends, fields)]
+    fill_window(win, both, bs)
+    image = apply_blocks(win, cols_ref, kb, sub_ref[0], groups, diag[...], both[1])
+    v = pack[0:modes, :]
     left = jnp.concatenate([v, s, own], axis=0)
-    right = jnp.concatenate([s, kstiff[...], km, own], axis=0)
+    right = jnp.concatenate([s, image, own], axis=0)
 
     def inner(x, y):
         return lax.dot_general(
@@ -380,12 +406,22 @@
             preferred_element_type=F32,
         )
 
-    gram[...] = inner(left, right)
-    gram[2 * modes : 3 * modes, 0:modes] = inner(v, v)
-
-
-def final_kernel(modes, total, gram, stiff, mass, residual, g_stiff, g_plain):
+    whole = inner(left, right)
+    half = 3 * modes // 2
+    gram[0] = whole[:half]
+    gram[1] = whole[half:]
+    gram[1, 2 * modes - half : 3 * modes - half, 0:modes] = inner(v, v)
+    core = sub_ref[1]
+    keep[...] = gram[core]
+    send[...] = gram[1 - core]
+
+
+def final_kernel(modes, total, sub_ref, mine, other, stiff, mass, residual, g_stiff, g_plain, gram):
     m = modes
+    core = sub_ref[1]
+    half = 3 * m // 2
+    gram[pl.ds(pl.multiple_of(core * half, half), half), :] = mine[...]
+    gram[pl.ds(pl.multiple_of((1 - core) * half, half), half), :] = other[...]
     blocks = [
         [gram[i * m : (i + 1) * m, j * m : (j + 1) * m] for j in range(4)] for i in range(3)
     ]
@@ -447,7 +483,7 @@
     return pl.BlockSpec(memory_space=pltpu.VMEM)
 
 
-def call(kernel, name, out_shape, scalars, arrays, scratch, flops):
+def call(kernel, name, out_shape, scalars, arrays, scratch, flops, mib=4):
     return pl.pallas_call(
         kernel,
         name=name,
@@ -455,6 +491,7 @@
         in_specs=[smem()] * len(scalars) + [vmem()] * len(arrays),
         out_specs=jax.tree.map(lambda _: vmem(), out_shape),
         scratch_shapes=scratch,
+        compiler_params=pltpu.CompilerParams(vmem_limit_bytes=mib << 20),
         cost_estimate=pl.CostEstimate(flops=flops, transcendentals=0, bytes_accessed=1 << 20),
     )(*scalars, *arrays)
 
@@ -476,43 +513,50 @@
     slots = slot_node.shape[0]
     bs = kblocks.shape[2]
     total = local * lax.axis_size("passage") * groups
-    sub = lax.axis_index("sub").astype(jnp.int32).reshape(1)
+    sub = jnp.stack([lax.axis_index("sub"), lax.axis_index("passage") & 1]).astype(jnp.int32)
     deep, wide = slots // 128, 128
     capacity = 2 * slots // groups
-    pack = call(
+    slotted = [x.reshape(deep, wide) for x in (slot_owner, slot_cell, slot_node, slot_weight)]
+    pack, mdiag, diag, cols = pl.pallas_call(
         functools.partial(pack_kernel, modes, groups),
-        "pack",
-        jax.ShapeDtypeStruct((modes + 3 * deep, local), F32),
-        [live_slots],
-        [block_vectors]
-        + [x.reshape(deep, wide) for x in (slot_owner, slot_cell, slot_node, slot_weight)],
-        [],
-        1 << 28,
+        name="pack",
+        out_shape=(
+            jax.ShapeDtypeStruct((modes + 3 * deep, local), F32),
+            jax.ShapeDtypeStruct((1, local), F32),
+            jax.ShapeDtypeStruct((1, local), F32),
+            jax.ShapeDtypeStruct(block_cols.shape, jnp.int32),
+        ),
+        in_specs=[smem()] + [pl.BlockSpec(memory_space=pltpu.MemorySpace.HBM)] * 8,
+        out_specs=(vmem(), vmem(), vmem(), vmem()),
+        scratch_shapes=[pltpu.VMEM((deep, wide), x.dtype) for x in slotted]
+        + [pltpu.SemaphoreType.DMA((8,))],
+        compiler_params=pltpu.CompilerParams(vmem_limit_bytes=4 << 20),
+        cost_estimate=pl.CostEstimate(flops=1 << 28, transcendentals=0, bytes_accessed=1 << 20),
+    )(
+        live_slots,
+        *[
+            pltpu.with_memory_space_constraint(x, pltpu.MemorySpace.HBM)
+            for x in (
+                *slotted,
+                block_vectors,
+                mass_diag[None, :],
+                stiffness[None, :],
+                block_cols,
+            )
+        ]
     )
     packs = [pack] + [shifted(pack, "sub", k) for k in range(1, groups)]
     both = jnp.stack(packs)
     low = shifted(both, "passage", 1)
     high = shifted(both, "passage", -1)
-    diag = stiffness[None, :]
     window = [packs[1], packs[0], packs[groups - 1]]
     nwin = 3 * local // bs
     stiff = call(
         functools.partial(stiff_kernel, modes, groups),
         "stiff",
         jax.ShapeDtypeStruct((modes, local), F32),
-        [sub, block_cols],
+        [sub, cols],
         [*window, diag, kblocks],
-        [pltpu.VMEM((nwin, modes, bs), F32)],
-        1 << 29,
-    )
-    stiff_prev = shifted(stiff, "sub", 1)
-    stiff_next = shifted(stiff, "sub", -1)
-    kstiff = call(
-        functools.partial(stiff_kernel, modes, groups),
-        "stiff_image",
-        jax.ShapeDtypeStruct((modes, local), F32),
-        [sub, block_cols],
-        [stiff_prev, stiff, stiff_next, diag, kblocks],
         [pltpu.VMEM((nwin, modes, bs), F32)],
         1 << 29,
     )
@@ -533,16 +577,17 @@
             field(CX * half * modes, 2 * CZ),
         ),
         [sub],
-        packs,
+        [*packs, stiff],
         [pltpu.VMEM((CX * pairs * modes, 2 * width * groups), BF), rhs],
         1 << 32,
+        16,
     )
     force = call(
         functools.partial(fluid_kernel, modes, groups, capacity),
         "fluid",
-        tuple(field(3, modes, local) for _ in range(groups)),
+        tuple(field(4 if k in (1, groups - 1) else 3, modes, local) for k in range(groups)),
         [sub],
-        [*packs, low, high, *source, mass_diag[None, :]],
+        [*packs, low, high, *source, mdiag, stiff],
         [
             pltpu.VMEM((2, HALO * pairs * modes, 2 * CZ), F32),
             pltpu.VMEM((4, HALO * half * modes, 2 * CZ), F32),
@@ -553,31 +598,32 @@
             pltpu.VMEM((groups, modes, local), F32),
         ],
         1 << 32,
+        16,
     )
     parts = [force[0]] + [shifted(force[k], "sub", k) for k in range(1, groups)]
-    gram, mass = call(
+    keep, send, mass = call(
         functools.partial(gram_kernel, modes, groups),
         "gram",
-        (field(3 * modes, 4 * modes), field(modes, local)),
-        [sub, block_cols],
-        [block_vectors, *parts, stiff, kstiff, diag, kblocks],
-        [pltpu.VMEM((nwin, modes, bs), F32)],
+        (field(3 * modes // 2, 4 * modes), field(3 * modes // 2, 4 * modes), field(modes, local)),
+        [sub, cols],
+        [pack, *parts, stiff, diag, kblocks],
+        [
+            pltpu.VMEM((nwin, 2 * modes, bs), F32),
+            pltpu.VMEM((2, 3 * modes // 2, 4 * modes), F32),
+        ],
         1 << 29,
     )
-    gram = gram + swapped(gram, "passage", 1)
-    gram = summed(gram, "passage", 1)
-    gram = summed(gram, "sub", 0)
+    mine = keep + swapped(send, "passage", 1)
+    mine = summed(mine, "passage", 1)
+    mine = summed(mine, "sub", 0)
+    other = swapped(mine, "passage", 1)
     return call(
         functools.partial(final_kernel, modes, float(total)),
         "final",
-        (
-            jax.ShapeDtypeStruct((modes, local), F32),
-            jax.ShapeDtypeStruct((2 * modes, 2 * modes), F32),
-            jax.ShapeDtypeStruct((2 * modes, 2 * modes), F32),
-        ),
-        [],
-        [gram, stiff, mass],
-        [],
+        (field(modes, local), field(2 * modes, 2 * modes), field(2 * modes, 2 * modes)),
+        [sub],
+        [mine, other, stiff, mass],
+        [pltpu.VMEM((3 * modes, 4 * modes), F32)],
         1 << 20,
     )
 

time: 81.9 us -> 64 us (0.78)
  Pallas kernels: 29.1 us -> 17.6 us
  starting transfers between devices: 28.5 us -> 19.1 us
  waiting for transfers between devices: 17.5 us -> 24.9 us
  local copies, waits for them, and re-layouts: 2.69 us -> 0.01 us
  other arithmetic: 2.3 us -> 0.12 us
    pallas_call x7 -> x5, Pallas kernels: 29.1 us -> 16.1 us  [call(): pl.pallas_call(kernel, name=name, out_shape=out_shape, in_specs=[smem()]...]
    ppermute x10 -> x8, starting transfers between devices: 20.6 us -> 11 us  [shifted(): return lax.ppermute(x, axis, [(i, (i + k) % n) for i in range(n)])]
    ppermute x10 -> x8, waiting for transfers between devices: 6.93 us -> 16.3 us  [shifted(): return lax.ppermute(x, axis, [(i, (i + k) % n) for i in range(n)])]
    unnamed x20 -> x2, local copies, waits for them, and re-layouts: 2.69 us -> 0.01 us
    ppermute x7 -> x8, waiting for transfers between devices: 10.6 us -> 8.54 us  [swapped(): return lax.ppermute(x, axis, [(i, i ^ k) for i in range(n)])]
    pallas_call x0 -> x1, Pallas kernels: none -> 1.51 us  [body(): pl.pallas_call(functools.partial(pack_kernel, modes, groups), name='pack'...]
    another operation x1, other arithmetic: 0.86 us -> 0.02 us  [body(): both = jnp.stack(packs)]
    ppermute x7 -> x8, starting transfers between devices: 7.94 us -> 8.08 us  [swapped(): return lax.ppermute(x, axis, [(i, i ^ k) for i in range(n)])]
  transfers between devices with their start and end apart: 17 -> 16, of which waited for: 10 -> 12; matrix products, arithmetic and copies ran while one was open for 0% -> 0% of each run, Pallas kernels for 13% -> 9%
where the time goes in v3:
time: 64 us; the launch traced here: 63 us
  waiting for transfers between devices  24.9 us (39%)
  starting transfers between devices  19.1 us (30%)
  Pallas kernels  17.6 us (28%)
  between operations  1.36 us (2%)
    ppermute x8, waiting for transfers between devices, shifted(): return lax.ppermute(x, axis, [(i, (i + k) % n) for i in range(n)])  16.3 us
    pallas_call x5, Pallas kernels, call(): pl.pallas_call(kernel, name=name, out_shape=out_shape, in_specs=[smem()]...  16.1 us
    ppermute x8, starting transfers between devices, shifted(): return lax.ppermute(x, axis, [(i, (i + k) % n) for i in range(n)])  11 us
    ppermute x8, waiting for transfers between devices, swapped(): return lax.ppermute(x, axis, [(i, i ^ k) for i in range(n)])  8.54 us
    ppermute x8, starting transfers between devices, swapped(): return lax.ppermute(x, axis, [(i, i ^ k) for i in range(n)])  8.08 us
    pallas_call x1, Pallas kernels, body(): pl.pallas_call(functools.partial(pack_kernel, modes, groups), name='pack'...  1.51 us
  transfers between devices with their start and end apart: 16, of which 12 were waited for; matrix products, arithmetic and copies ran while one was open for 0% of the time, Pallas kernels for 9%

profile of v3, /device:TPU:0, one launch (start us, length us, event | category | flops | bytes accessed | tf_op | source)
XLA Modules:
  0.0 63.0 jit_solution(3569557073940628959)
XLA Ops:
  1.3 1.5 %pack.1 = (f32[56,256]{1,0:T(8,128)S(1)}, f32[1,256]{1,0:T(1,128)S(1)}, f32[1,256]{1,0:T(1,128)S(1)}, s32[2,4]{1,0:T(2,128)S(1)}) custom-call(s32[1]{0:T(128)S(6)} %copy.13.live_ref, s32[8,128]{1,0:T(8,128)} %bitcast.16, s32[8,128]{1,0:T(8,128)} %bitcast.17, s32[8,128]{1,0:T(8,128)} %bitcast.18, f32[8,128]{1,0:T(8,128)} %bitcast.19, f32[32,256]{1,0:T(8,128)} %refs_4_.1, ...), custom_call_target="tpu_custom_call" | custom-call | flops 268435456 | bytes 1048576 | tf_op jit(solution)/shard_map/pack/pallas_call | solution.py:520
  2.8 5.1 %collective-permute-start.2 = (f32[56,256]{1,0:T(8,128)S(1)}, f32[56,256]{1,0:T(8,128)S(1)}, u32[]{:S(2)}, u32[]{:S(2)}) collective-permute-start(f32[56,256]{1,0:T(8,128)S(1)} %get-tuple-element.18.own.refs_0_.pack), channel_id=1, source_target_pairs={{0,3},{1,0},{2,1},{3,2},{4,7},{5,4},{6,5},{7,6},{8,11},{9,8},{10,9... | collective-permute-start | bytes 172040 | tf_op jit(solution)/shard_map/ppermute | solution.py:457
  7.9 1.0 %collective-permute-start = (f32[56,256]{1,0:T(8,128)S(1)}, f32[56,256]{1,0:T(8,128)S(1)}, u32[]{:S(2)}, u32[]{:S(2)}) collective-permute-start(f32[56,256]{1,0:T(8,128)S(1)} %get-tuple-element.18.own.refs_0_.pack), channel_id=1, source_target_pairs={{0,1},{1,2},{2,3},{3,0},{4,5},{5,6},{6,7},{7,4},{8,9},{9,10},{10,1... | collective-permute-start | bytes 172040 | tf_op jit(solution)/shard_map/ppermute | solution.py:457
  8.9 0.1 pad_add_fusion.sub_ref
  9.0 1.2 %collective-permute-done.2.nxt.refs_3_ = f32[56,256]{1,0:T(8,128)S(1)} collective-permute-done((f32[56,256]{1,0:T(8,128)S(1)}, f32[56,256]{1,0:T(8,128)S(1)}, u32[]{:S(2)}, u32[]{:S(2)}) %collective-permute-start.2) | collective-permute-done | bytes 57376 | tf_op jit(solution)/shard_map/ppermute | solution.py:457
  10.2 2.9 %collective-permute-done.1.refs_2_ = f32[56,256]{1,0:T(8,128)S(1)} collective-permute-done((f32[56,256]{1,0:T(8,128)S(1)}, f32[56,256]{1,0:T(8,128)S(1)}, u32[]{:S(2)}, u32[]{:S(2)}) %collective-permute-start.1) | collective-permute-done | bytes 57376 | tf_op jit(solution)/shard_map/ppermute | solution.py:457
  13.1 0.8 %collective-permute-done.prev.refs_1_ = f32[56,256]{1,0:T(8,128)S(1)} collective-permute-done((f32[56,256]{1,0:T(8,128)S(1)}, f32[56,256]{1,0:T(8,128)S(1)}, u32[]{:S(2)}, u32[]{:S(2)}) %collective-permute-start) | collective-permute-done | bytes 57376 | tf_op jit(solution)/shard_map/ppermute | solution.py:457
  13.9 0.5 collective-permute-start.4
  14.5 1.1 %stiff.1.refs_4_.refs_10_ = f32[32,256]{1,0:T(8,128)S(1)} custom-call(s32[2]{0:T(128)S(1)} %pad_add_fusion.sub_ref, s32[2,4]{1,0:T(2,128)S(1)} %get-tuple-element.17.cols_ref, f32[56,256]{1,0:T(8,128)S(1)} %collective-permute-done.prev.refs_1_, f32[56,256]{1,0:T(8,128)S(1)} %get-tuple-element.18.own.refs_0_.pack, ...), custom_call_target="tpu_custom_call" | custom-call | flops 536870912 | bytes 1048576 | tf_op jit(solution)/shard_map/stiff/pallas_call | solution.py:487
  15.6 4.3 %own_source.1 = (f32[1024,256]{1,0:T(8,128)S(1)}, f32[256,256]{1,0:T(8,128)S(1)}, f32[256,256]{1,0:T(8,128)S(1)}) custom-call(s32[2]{0:T(128)S(1)} %pad_add_fusion.sub_ref, f32[56,256]{1,0:T(8,128)S(1)} %get-tuple-element.18.own.refs_0_.pack, f32[56,256]{1,0:T(8,128)S(1)} %collective-permute-done.prev.refs_1_, f32[56,256]{1,0:T(8,128)S(1)} %collective-permute-done.1.refs_2_, ...), custom_call_target="tpu_custom_call" | custom-call | flops 4294967296 | bytes 1048576 | tf_op jit(solution)/shard_map/own_source/pallas_call | solution.py:487
  19.9 3.0 %collective-permute-done.3.refs_4_ = f32[4,56,256]{2,1,0:T(8,128)S(1)} collective-permute-done((f32[4,56,256]{2,1,0:T(8,128)S(1)}, f32[4,56,256]{2,1,0:T(8,128)S(1)}, u32[]{:S(2)}, u32[]{:S(2)}) %collective-permute-start.3) | collective-permute-done | bytes 229408 | tf_op jit(solution)/shard_map/ppermute | solution.py:457
  22.9 7.8 %fluid.1 = (f32[3,32,256]{2,1,0:T(8,128)S(1)}, f32[4,32,256]{2,1,0:T(8,128)S(1)}, f32[3,32,256]{2,1,0:T(8,128)S(1)}, f32[4,32,256]{2,1,0:T(8,128)S(1)}) custom-call(s32[2]{0:T(128)S(1)} %pad_add_fusion.sub_ref, f32[56,256]{1,0:T(8,128)S(1)} %get-tuple-element.18.own.refs_0_.pack, f32[56,256]{1,0:T(8,128)S(1)} %collective-permute-done.prev.refs_1_, ...), custom_call_target="tpu_custom_call" | custom-call | flops 4294967296 | bytes 1048576 | tf_op jit(solution)/shard_map/fluid/pallas_call | solution.py:487
  30.7 2.7 %collective-permute-start.5 = (f32[4,32,256]{2,1,0:T(8,128)S(1)}, f32[4,32,256]{2,1,0:T(8,128)S(1)}, u32[]{:S(2)}, u32[]{:S(2)}) collective-permute-start(f32[4,32,256]{2,1,0:T(8,128)S(1)} %get-tuple-element.25), channel_id=1, source_target_pairs={{0,1},{1,2},{2,3},{3,0},{4,5},{5,6},{6,7},{7,4},{8,9},{9,10},{10,1... | collective-permute-start | bytes 393224 | tf_op jit(solution)/shard_map/ppermute | solution.py:457
  33.4 1.1 %collective-permute-start.7 = (f32[4,32,256]{2,1,0:T(8,128)S(1)}, f32[4,32,256]{2,1,0:T(8,128)S(1)}, u32[]{:S(2)}, u32[]{:S(2)}) collective-permute-start(f32[4,32,256]{2,1,0:T(8,128)S(1)} %get-tuple-element.27), channel_id=1, source_target_pairs={{0,3},{1,0},{2,1},{3,2},{4,7},{5,4},{6,5},{7,6},{8,11},{9,8},{10,9... | collective-permute-start | bytes 393224 | tf_op jit(solution)/shard_map/ppermute | solution.py:457
  34.5 0.4 collective-permute-start.6
  34.9 8.4 %collective-permute-done.6.refs_2_ = f32[3,32,256]{2,1,0:T(8,128)S(1)} collective-permute-done((f32[3,32,256]{2,1,0:T(8,128)S(1)}, f32[3,32,256]{2,1,0:T(8,128)S(1)}, u32[]{:S(2)}, u32[]{:S(2)}) %collective-permute-start.6) | collective-permute-done | bytes 98336 | tf_op jit(solution)/shard_map/ppermute | solution.py:457
  43.4 1.4 %gram.1 = (f32[48,128]{1,0:T(8,128)S(1)}, f32[48,128]{1,0:T(8,128)S(1)}, f32[32,256]{1,0:T(8,128)S(1)}) custom-call(s32[2]{0:T(128)S(1)} %pad_add_fusion.sub_ref, s32[2,4]{1,0:T(2,128)S(1)} %get-tuple-element.17.cols_ref, f32[56,256]{1,0:T(8,128)S(1)} %get-tuple-element.18.own.refs_0_.pack, f32[3,32,256]{2,1,0:T(8,128)S(1)} %get-tuple-element.24.refs_0_, ...), custom_call_target="tpu_custom_call" | custom-call | flops 536870912 | bytes 1048576 | tf_op jit(solution)/shard_map/gram/pallas_call | solution.py:487
  44.8 0.1 collective-permute-start.8
  44.9 1.2 %collective-permute-done.8 = f32[48,128]{1,0:T(8,128)S(1)} collective-permute-done((f32[48,128]{1,0:T(8,128)S(1)}, f32[48,128]{1,0:T(8,128)S(1)}, u32[]{:S(2)}, u32[]{:S(2)}) %collective-permute-start.8) | collective-permute-done | bytes 24608 | tf_op jit(solution)/shard_map/ppermute | solution.py:462
  46.0 1.9 %collective-permute-start.11 = (f32[48,128]{1,0:T(8,128)S(1)}, f32[48,128]{1,0:T(8,128)S(1)}, u32[]{:S(2)}, u32[]{:S(2)}) collective-permute-start(f32[48,128]{1,0:T(8,128)S(1)} %add.21), channel_id=1, source_target_pairs={{0,24},{4,28},{8,16},{12,20},{16,8},{20,12},{24,0},{28,4},{1,25},{... | collective-permute-start | bytes 73736 | tf_op jit(solution)/shard_map/ppermute | solution.py:462
  48.0 1.0 %collective-permute-start.10 = (f32[48,128]{1,0:T(8,128)S(1)}, f32[48,128]{1,0:T(8,128)S(1)}, u32[]{:S(2)}, u32[]{:S(2)}) collective-permute-start(f32[48,128]{1,0:T(8,128)S(1)} %add.21), channel_id=1, source_target_pairs={{0,16},{4,20},{8,24},{12,28},{16,0},{20,4},{24,8},{28,12},{1,17},{... | collective-permute-start | bytes 73736 | tf_op jit(solution)/shard_map/ppermute | solution.py:462
  49.0 0.5 collective-permute-start.9
  49.5 1.3 %collective-permute-done.11 = f32[48,128]{1,0:T(8,128)S(1)} collective-permute-done((f32[48,128]{1,0:T(8,128)S(1)}, f32[48,128]{1,0:T(8,128)S(1)}, u32[]{:S(2)}, u32[]{:S(2)}) %collective-permute-start.11) | collective-permute-done | bytes 24608 | tf_op jit(solution)/shard_map/ppermute | solution.py:462
  50.9 0.9 %collective-permute-done.10 = f32[48,128]{1,0:T(8,128)S(1)} collective-permute-done((f32[48,128]{1,0:T(8,128)S(1)}, f32[48,128]{1,0:T(8,128)S(1)}, u32[]{:S(2)}, u32[]{:S(2)}) %collective-permute-start.10) | collective-permute-done | bytes 24608 | tf_op jit(solution)/shard_map/ppermute | solution.py:462
  51.8 1.0 %collective-permute-done.9 = f32[48,128]{1,0:T(8,128)S(1)} collective-permute-done((f32[48,128]{1,0:T(8,128)S(1)}, f32[48,128]{1,0:T(8,128)S(1)}, u32[]{:S(2)}, u32[]{:S(2)}) %collective-permute-start.9) | collective-permute-done | bytes 24608 | tf_op jit(solution)/shard_map/ppermute | solution.py:462
  52.8 2.6 %collective-permute-start.14 = (f32[48,128]{1,0:T(8,128)S(1)}, f32[48,128]{1,0:T(8,128)S(1)}, u32[]{:S(2)}, u32[]{:S(2)}) collective-permute-start(f32[48,128]{1,0:T(8,128)S(1)} %add_add_fusion.1), channel_id=1, source_target_pairs={{0,3},{1,2},{2,1},{3,0},{4,7},{5,6},{6,5},{7,4},{8,11},{9,10},{10,... | collective-permute-start | bytes 73736 | tf_op jit(solution)/shard_map/ppermute | solution.py:462
  55.4 1.8 %collective-permute-start.12 = (f32[48,128]{1,0:T(8,128)S(1)}, f32[48,128]{1,0:T(8,128)S(1)}, u32[]{:S(2)}, u32[]{:S(2)}) collective-permute-start(f32[48,128]{1,0:T(8,128)S(1)} %add_add_fusion.1), channel_id=1, source_target_pairs={{0,1},{1,0},{2,3},{3,2},{4,5},{5,4},{6,7},{7,6},{8,9},{9,8},{10,11... | collective-permute-start | bytes 73736 | tf_op jit(solution)/shard_map/ppermute | solution.py:462
  57.3 1.2 %collective-permute-done.14 = f32[48,128]{1,0:T(8,128)S(1)} collective-permute-done((f32[48,128]{1,0:T(8,128)S(1)}, f32[48,128]{1,0:T(8,128)S(1)}, u32[]{:S(2)}, u32[]{:S(2)}) %collective-permute-start.14) | collective-permute-done | bytes 24608 | tf_op jit(solution)/shard_map/ppermute | solution.py:462
  58.5 1.6 %collective-permute-done.13 = f32[48,128]{1,0:T(8,128)S(1)} collective-permute-done((f32[48,128]{1,0:T(8,128)S(1)}, f32[48,128]{1,0:T(8,128)S(1)}, u32[]{:S(2)}, u32[]{:S(2)}) %collective-permute-start.13) | collective-permute-done | bytes 24608 | tf_op jit(solution)/shard_map/ppermute | solution.py:462
  60.2 0.1 collective-permute-start.15
  60.3 1.2 %collective-permute-done.15.other = f32[48,128]{1,0:T(8,128)S(1)} collective-permute-done((f32[48,128]{1,0:T(8,128)S(1)}, f32[48,128]{1,0:T(8,128)S(1)}, u32[]{:S(2)}, u32[]{:S(2)}) %collective-permute-start.15) | collective-permute-done | bytes 24608 | tf_op jit(solution)/shard_map/ppermute | solution.py:462
  61.4 1.5 %final.1 = (f32[32,256]{1,0:T(8,128)}, f32[64,64]{1,0:T(8,128)}, f32[64,64]{1,0:T(8,128)}) custom-call(s32[2]{0:T(128)S(1)} %pad_add_fusion.sub_ref, f32[48,128]{1,0:T(8,128)S(1)} %add_add_fusion.mine, f32[48,128]{1,0:T(8,128)S(1)} %collective-permute-done.15.other, f32[32,256]{1,0:T(8,128)S(1)} %stiff.1.refs_4_.refs_10_, f32[32,256]{1,0:T(8,128)S(1)} %get-tuple-element.30.mass), custom_call_target="tpu_custom_call" | custom-call | flops 1048576 | bytes 1048576 | tf_op jit(solution)/shard_map/final/pallas_call | solution.py:487
  (13 shorter events, 0.1 us)
Async XLA Ops:
  1.3 13.2 %copy-start = (f32[2,4,128,128]{3,2,1,0:T(8,128)S(1)}, f32[2,4,128,128]{3,2,1,0:T(8,128)}, u32[]{:S(2)}) copy-start(f32[2,4,128,128]{3,2,1,0:T(8,128)} %refs_6_.1) | copy-start | bytes 1572868
  2.8 7.4 %collective-permute-start.2 = (f32[56,256]{1,0:T(8,128)S(1)}, f32[56,256]{1,0:T(8,128)S(1)}, u32[]{:S(2)}, u32[]{:S(2)}) collective-permute-start(f32[56,256]{1,0:T(8,128)S(1)} %get-tuple-element.18.own.refs_0_.pack), channel_id=1, source_target_pairs={{0,3},{1,0},{2,1},{3,2},{4,7},{5,4},{6,5},{7,6},{8,11},{9,8},{10,9... | collective-permute-start | bytes 172040 | tf_op jit(solution)/shard_map/ppermute | solution.py:457
  7.9 5.2 %collective-permute-start.1 = (f32[56,256]{1,0:T(8,128)S(1)}, f32[56,256]{1,0:T(8,128)S(1)}, u32[]{:S(2)}, u32[]{:S(2)}) collective-permute-start(f32[56,256]{1,0:T(8,128)S(1)} %get-tuple-element.18.own.refs_0_.pack), channel_id=1, source_target_pairs={{0,2},{1,3},{2,0},{3,1},{4,6},{5,7},{6,4},{7,5},{8,10},{9,11},{10,... | collective-permute-start | bytes 172040 | tf_op jit(solution)/shard_map/ppermute | solution.py:457
  7.9 6.0 %collective-permute-start = (f32[56,256]{1,0:T(8,128)S(1)}, f32[56,256]{1,0:T(8,128)S(1)}, u32[]{:S(2)}, u32[]{:S(2)}) collective-permute-start(f32[56,256]{1,0:T(8,128)S(1)} %get-tuple-element.18.own.refs_0_.pack), channel_id=1, source_target_pairs={{0,1},{1,2},{2,3},{3,0},{4,5},{5,6},{6,7},{7,4},{8,9},{9,10},{10,1... | collective-permute-start | bytes 172040 | tf_op jit(solution)/shard_map/ppermute | solution.py:457
  13.9 6.0 %collective-permute-start.4 = (f32[4,56,256]{2,1,0:T(8,128)S(1)}, f32[4,56,256]{2,1,0:T(8,128)S(1)}, u32[]{:S(2)}, u32[]{:S(2)}) collective-permute-start(f32[4,56,256]{2,1,0:T(8,128)S(1)} %pad_maximum_fusion), channel_id=1, source_target_pairs={{0,28},{4,0},{8,4},{12,8},{16,12},{20,16},{24,20},{28,24},{1,29},{... | collective-permute-start | bytes 688136 | tf_op jit(solution)/shard_map/ppermute | solution.py:457
  14.4 8.4 %collective-permute-start.3 = (f32[4,56,256]{2,1,0:T(8,128)S(1)}, f32[4,56,256]{2,1,0:T(8,128)S(1)}, u32[]{:S(2)}, u32[]{:S(2)}) collective-permute-start(f32[4,56,256]{2,1,0:T(8,128)S(1)} %pad_maximum_fusion), channel_id=1, source_target_pairs={{0,4},{4,8},{8,12},{12,16},{16,20},{20,24},{24,28},{28,0},{1,5},{5... | collective-permute-start | bytes 688136 | tf_op jit(solution)/shard_map/ppermute | solution.py:457
  30.7 12.7 %collective-permute-start.5 = (f32[4,32,256]{2,1,0:T(8,128)S(1)}, f32[4,32,256]{2,1,0:T(8,128)S(1)}, u32[]{:S(2)}, u32[]{:S(2)}) collective-permute-start(f32[4,32,256]{2,1,0:T(8,128)S(1)} %get-tuple-element.25), channel_id=1, source_target_pairs={{0,1},{1,2},{2,3},{3,0},{4,5},{5,6},{6,7},{7,4},{8,9},{9,10},{10,1... | collective-permute-start | bytes 393224 | tf_op jit(solution)/shard_map/ppermute | solution.py:457
  33.4 10.0 %collective-permute-start.7 = (f32[4,32,256]{2,1,0:T(8,128)S(1)}, f32[4,32,256]{2,1,0:T(8,128)S(1)}, u32[]{:S(2)}, u32[]{:S(2)}) collective-permute-start(f32[4,32,256]{2,1,0:T(8,128)S(1)} %get-tuple-element.27), channel_id=1, source_target_pairs={{0,3},{1,0},{2,1},{3,2},{4,7},{5,4},{6,5},{7,6},{8,11},{9,8},{10,9... | collective-permute-start | bytes 393224 | tf_op jit(solution)/shard_map/ppermute | solution.py:457
  34.5 8.8 %collective-permute-start.6 = (f32[3,32,256]{2,1,0:T(8,128)S(1)}, f32[3,32,256]{2,1,0:T(8,128)S(1)}, u32[]{:S(2)}, u32[]{:S(2)}) collective-permute-start(f32[3,32,256]{2,1,0:T(8,128)S(1)} %get-tuple-element.26), channel_id=1, source_target_pairs={{0,2},{1,3},{2,0},{3,1},{4,6},{5,7},{6,4},{7,5},{8,10},{9,11},{10,... | collective-permute-start | bytes 294920 | tf_op jit(solution)/shard_map/ppermute | solution.py:457
  44.8 1.3 %collective-permute-start.8 = (f32[48,128]{1,0:T(8,128)S(1)}, f32[48,128]{1,0:T(8,128)S(1)}, u32[]{:S(2)}, u32[]{:S(2)}) collective-permute-start(f32[48,128]{1,0:T(8,128)S(1)} %get-tuple-element.29), channel_id=1, source_target_pairs={{0,4},{4,0},{8,12},{12,8},{16,20},{20,16},{24,28},{28,24},{1,5},{5... | collective-permute-start | bytes 73736 | tf_op jit(solution)/shard_map/ppermute | solution.py:462
  46.0 4.8 %collective-permute-start.11 = (f32[48,128]{1,0:T(8,128)S(1)}, f32[48,128]{1,0:T(8,128)S(1)}, u32[]{:S(2)}, u32[]{:S(2)}) collective-permute-start(f32[48,128]{1,0:T(8,128)S(1)} %add.21), channel_id=1, source_target_pairs={{0,24},{4,28},{8,16},{12,20},{16,8},{20,12},{24,0},{28,4},{1,25},{... | collective-permute-start | bytes 73736 | tf_op jit(solution)/shard_map/ppermute | solution.py:462
  48.0 3.8 %collective-permute-start.10 = (f32[48,128]{1,0:T(8,128)S(1)}, f32[48,128]{1,0:T(8,128)S(1)}, u32[]{:S(2)}, u32[]{:S(2)}) collective-permute-start(f32[48,128]{1,0:T(8,128)S(1)} %add.21), channel_id=1, source_target_pairs={{0,16},{4,20},{8,24},{12,28},{16,0},{20,4},{24,8},{28,12},{1,17},{... | collective-permute-start | bytes 73736 | tf_op jit(solution)/shard_map/ppermute | solution.py:462
  49.0 3.8 %collective-permute-start.9 = (f32[48,128]{1,0:T(8,128)S(1)}, f32[48,128]{1,0:T(8,128)S(1)}, u32[]{:S(2)}, u32[]{:S(2)}) collective-permute-start(f32[48,128]{1,0:T(8,128)S(1)} %add.21), channel_id=1, source_target_pairs={{0,8},{4,12},{8,0},{12,4},{16,24},{20,28},{24,16},{28,20},{1,9},{5... | collective-permute-start | bytes 73736 | tf_op jit(solution)/shard_map/ppermute | solution.py:462
  52.8 5.7 %collective-permute-start.14 = (f32[48,128]{1,0:T(8,128)S(1)}, f32[48,128]{1,0:T(8,128)S(1)}, u32[]{:S(2)}, u32[]{:S(2)}) collective-permute-start(f32[48,128]{1,0:T(8,128)S(1)} %add_add_fusion.1), channel_id=1, source_target_pairs={{0,3},{1,2},{2,1},{3,0},{4,7},{5,6},{6,5},{7,4},{8,11},{9,10},{10,... | collective-permute-start | bytes 73736 | tf_op jit(solution)/shard_map/ppermute | solution.py:462
  55.4 4.7 %collective-permute-start.13 = (f32[48,128]{1,0:T(8,128)S(1)}, f32[48,128]{1,0:T(8,128)S(1)}, u32[]{:S(2)}, u32[]{:S(2)}) collective-permute-start(f32[48,128]{1,0:T(8,128)S(1)} %add_add_fusion.1), channel_id=1, source_target_pairs={{0,2},{1,3},{2,0},{3,1},{4,6},{5,7},{6,4},{7,5},{8,10},{9,11},{10,... | collective-permute-start | bytes 73736 | tf_op jit(solution)/shard_map/ppermute | solution.py:462
  55.4 4.7 %collective-permute-start.12 = (f32[48,128]{1,0:T(8,128)S(1)}, f32[48,128]{1,0:T(8,128)S(1)}, u32[]{:S(2)}, u32[]{:S(2)}) collective-permute-start(f32[48,128]{1,0:T(8,128)S(1)} %add_add_fusion.1), channel_id=1, source_target_pairs={{0,1},{1,0},{2,3},{3,2},{4,5},{5,4},{6,7},{7,6},{8,9},{9,8},{10,11... | collective-permute-start | bytes 73736 | tf_op jit(solution)/shard_map/ppermute | solution.py:462
  60.2 1.3 %collective-permute-start.15 = (f32[48,128]{1,0:T(8,128)S(1)}, f32[48,128]{1,0:T(8,128)S(1)}, u32[]{:S(2)}, u32[]{:S(2)}) collective-permute-start(f32[48,128]{1,0:T(8,128)S(1)} %add_add_fusion.mine), channel_id=1, source_target_pairs={{0,4},{4,0},{8,12},{12,8},{16,20},{20,16},{24,28},{28,24},{1,5},{5... | collective-permute-start | bytes 73736 | tf_op jit(solution)/shard_map/ppermute | solution.py:462

commit v4 on v3

--- a/solution.py
+++ b/solution.py
@@ -200,9 +200,7 @@
 ):
     every = [Lists(blk, modes, capacity, width) for blk in blks]
     width = every[0].width
-    rows = a_count * b_count * modes
     spec = (a_first, a_count, b_first, b_count, inside)
-    left = lhs.at[0:rows, :]
     counts = []
     for k, lists in enumerate(every):
         last = jnp.zeros((1, width), jnp.int32)
@@ -210,36 +208,41 @@
             a, b, c, node, weight = lists.load(owner, chunk)
             needed = (weight > 0.0) & (a >= a_first) & (a < a_first + a_count)
             last = jnp.where(needed, chunk + 1, last)
-        counts.append(jnp.max(last))
-        fill(lists, owner, 0, *spec, left, rhs, 2 * k * width, None)
-    deep = 2 * width * len(every)
-    out[...] = dot_t(lhs[0:rows, 0:deep], rhs[:, 0:deep])
+        counts.append(last)
+        fill(lists, owner, 0, *spec, lhs, rhs, 2 * k * width, None)
+    out[...] = dot_t(lhs[...], rhs[...])
     if every[0].chunks == 1:
+        return []
+
+    def more(lists):
+        def one(chunk, carry):
+            fill(lists, owner, chunk, *spec, lhs, rhs, 0, None)
+            out[...] += dot_t(lhs[:, 0 : 2 * width], rhs[:, 0 : 2 * width])
+            return carry
+
+        return one
+
+    return [(count, more(lists)) for count, lists in zip(counts, every)]
+
+
+def later_chunks(jobs):
+    if not jobs:
         return
-    for lists, count in zip(every, counts):
-
-        def more(chunk, carry):
-            fill(lists, owner, chunk, *spec, left, rhs, 0, None)
-            out[...] += dot_t(lhs[0:rows, 0 : 2 * width], rhs[:, 0 : 2 * width])
-            return carry
-
-        lax.fori_loop(1, count, more, 0)
+    top = None
+    for count, _ in jobs:
+        most = jnp.max(count, axis=1, keepdims=True)
+        top = most if top is None else jnp.maximum(top, most)
+
+    @pl.when(jnp.max(top) > 0)
+    def _():
+        for last, (count, one) in zip([jnp.max(count) for count, _ in jobs], jobs):
+            lax.fori_loop(1, last, one, 0)
 
 
 def around(sub, groups):
     below = jnp.maximum(sub - 1, 0), jnp.where(sub > 0, 1.0, 0.0)
     above = jnp.minimum(sub + 1, groups - 1), jnp.where(sub < groups - 1, 1.0, 0.0)
     return below, above
-
-
-def own_source_kernel(modes, groups, capacity, sub_ref, *refs):
-    blks = refs[:groups]
-    own, below, above, lhs, rhs = refs[groups + 1 :]
-    sub = sub_ref[0]
-    (lo_owner, lo_in), (hi_owner, hi_in) = around(sub, groups)
-    scatter(blks, modes, capacity, sub, None, 0, CX, 0, CY // 2, own, lhs, rhs)
-    scatter(blks, modes, capacity, lo_owner, lo_in, 0, CX, CY - HALO, HALO // 2, below, lhs, rhs)
-    scatter(blks, modes, capacity, hi_owner, hi_in, 0, CX, 0, HALO // 2, above, lhs, rhs)
 
 
 def shift_sum(x):
@@ -249,62 +252,108 @@
     return x + 0.5 * (left + right)
 
 
+def plane_sum(src, a, b_range):
+    cols = [src(a, b) + 0.5 * (src(a - 1, b) + src(a + 1, b)) for b in b_range]
+    return [
+        shift_sum(cols[i] + 0.5 * (cols[i - 1] + cols[i + 1])) for i in range(1, len(cols) - 1)
+    ]
+
+
+def second_plane(src, a, lo_in, hi_in):
+    out = []
+    for i, t in enumerate(plane_sum(src, a, range(CY + 2 * HALO))):
+        sec = SEC_U * src(a, i + 1) + SEC_T * t
+        if i + 1 < HALO:
+            sec = sec * lo_in
+        if i + 1 >= CY + HALO:
+            sec = sec * hi_in
+        out.append(sec)
+    return out
+
+
+def source_reader(modes, mid, below, above, edge=None, corner=None):
+    half = HALO // 2
+
+    def src(a, b):
+        lanes = slice((b % 2) * CZ, (b % 2 + 1) * CZ)
+        outer = -1
+        if a < HALO:
+            outer = 0
+        elif a >= CX + HALO:
+            outer, a = 1, a - CX - HALO
+        else:
+            a = a - HALO
+        if b < HALO:
+            ref, at = (below if outer < 0 else corner[2 * outer]), a * half + b // 2
+        elif b >= CY + HALO:
+            ref = above if outer < 0 else corner[2 * outer + 1]
+            at = a * half + (b - CY - HALO) // 2
+        else:
+            ref, at = (mid if outer < 0 else edge[outer]), a * (CY // 2) + (b - HALO) // 2
+        return ref[at * modes : (at + 1) * modes, lanes]
+
+    return src
+
+
+def own_source_kernel(modes, groups, capacity, sub_ref, *refs):
+    blks = refs[:groups]
+    own, below, above, inner, *scratch = refs[groups + 1 :]
+    sub = sub_ref[0]
+    (lo_owner, lo_in), (hi_owner, hi_in) = around(sub, groups)
+    args = (blks, modes, capacity)
+    half = HALO // 2
+    jobs = scatter(*args, sub, None, 0, CX, 0, CY // 2, own, *scratch[0:2])
+    jobs += scatter(*args, lo_owner, lo_in, 0, CX, CY - HALO, half, below, *scratch[2:4])
+    jobs += scatter(*args, hi_owner, hi_in, 0, CX, 0, half, above, *scratch[4:6])
+    later_chunks(jobs)
+    src = source_reader(modes, own, below, above)
+    for a in range(HALO + 1, CX + HALO - 1):
+        for b, sec in enumerate(second_plane(src, a, lo_in, hi_in)):
+            inner[a - HALO - 1, b] = sec
+
+
 def fluid_kernel(modes, groups, capacity, sub_ref, *refs):
     blks = refs[:groups]
-    low, high, mid, below, above, mdiag, stiff = refs[groups : groups + 7]
-    outs = refs[groups + 7 : 2 * groups + 7]
-    edge, corner, second, press, lhs, rhs, force = refs[2 * groups + 7 :]
+    low, high, mid, below, above, inner, mdiag, stiff = refs[groups : groups + 8]
+    outs = refs[groups + 8 : 2 * groups + 8]
+    rest = refs[2 * groups + 8 :]
+    edge, corner, outer, press, force = rest[0:2], rest[2:6], rest[6], rest[7], rest[8]
+    scratch = rest[9:]
     sub = sub_ref[0]
     local = blks[0].shape[1]
     half = HALO // 2
     (lo_owner, lo_in), (hi_owner, hi_in) = around(sub, groups)
+    jobs = []
     for side, both in enumerate((low, high)):
         there = [both.at[k] for k in range(groups)]
         a_first = CX - HALO if side == 0 else 0
         wide = 128 if side == 0 else 256
         args = (there, modes, capacity)
-        scatter(*args, sub, None, a_first, HALO, 0, CY // 2, edge.at[side], lhs, rhs, wide)
-        spec = (a_first, HALO, CY - HALO, half)
-        scatter(*args, lo_owner, lo_in, *spec, corner.at[2 * side], lhs, rhs, wide)
-        scatter(*args, hi_owner, hi_in, a_first, HALO, 0, half, corner.at[2 * side + 1], lhs, rhs, wide)
-
-    def src(a, b):
-        lanes = slice((b % 2) * CZ, (b % 2 + 1) * CZ)
-        outer = -1
+        mem = scratch[6 * side : 6 * side + 6]
+        spec = (a_first, HALO)
+        jobs += scatter(*args, sub, None, *spec, 0, CY // 2, edge[side], *mem[0:2], wide)
+        jobs += scatter(
+            *args, lo_owner, lo_in, *spec, CY - HALO, half, corner[2 * side], *mem[2:4], wide
+        )
+        jobs += scatter(
+            *args, hi_owner, hi_in, *spec, 0, half, corner[2 * side + 1], *mem[4:6], wide
+        )
+    later_chunks(jobs)
+    src = source_reader(modes, mid, below, above, edge, corner)
+    for i, a in enumerate((1, 2, CX + HALO - 1, CX + HALO)):
+        for b, sec in enumerate(second_plane(src, a, lo_in, hi_in)):
+            outer[i, b] = sec
+
+    def second(a, b):
         if a < HALO:
-            outer, a = 0, a
-        elif a >= CX + HALO:
-            outer, a = 1, a - CX - HALO
-        else:
-            a = a - HALO
-        if b < HALO:
-            ref, at = (below if outer < 0 else corner.at[2 * outer]), a * half + b // 2
-        elif b >= CY + HALO:
-            ref = above if outer < 0 else corner.at[2 * outer + 1]
-            at = a * half + (b - CY - HALO) // 2
-        else:
-            ref, at = (mid if outer < 0 else edge.at[outer]), a * (CY // 2) + (b - HALO) // 2
-        return ref[at * modes : (at + 1) * modes, lanes]
-
-    for a in range(1, CX + 2 * HALO - 1):
-        cols = [
-            src(a, b) + 0.5 * (src(a - 1, b) + src(a + 1, b)) for b in range(CY + 2 * HALO)
-        ]
-        for b in range(1, CY + 2 * HALO - 1):
-            t = shift_sum(cols[b] + 0.5 * (cols[b - 1] + cols[b + 1]))
-            sec = SEC_U * src(a, b) + SEC_T * t
-            if b < HALO:
-                sec = sec * lo_in
-            if b >= CY + HALO:
-                sec = sec * hi_in
-            second[a - 1, b - 1] = sec
+            return outer[a, b]
+        if a >= CX:
+            return outer[a - CX + HALO, b]
+        return inner[a - HALO, b]
+
     for a in range(CX):
-        cols = [
-            second[a + 1, b] + 0.5 * (second[a, b] + second[a + 2, b]) for b in range(CY + 2)
-        ]
-        for b in range(CY):
-            t = shift_sum(cols[b + 1] + 0.5 * (cols[b] + cols[b + 2]))
-            p = PRE_SRC * src(a + HALO, b + HALO) + PRE_SEC * second[a + 1, b + 1] + PRE_T * t
+        for b, t in enumerate(plane_sum(second, a + 1, range(CY + 2))):
+            p = PRE_SRC * src(a + HALO, b + HALO) + PRE_SEC * second(a + 1, b + 1) + PRE_T * t
             hi, lo = split(p)
             at = (a * (CY // 2) + b // 2) * modes
             lanes = (b % 2) * CZ
@@ -345,20 +394,21 @@
     rb, nb, bs, _ = kb_ref.shape
     pieces = []
     for q in range(rb):
-        acc = None
+        parts = []
         for n in range(nb):
             j = cols_ref[q, n]
             where = sub + j // rb - 1
             inside = jnp.where((where >= 0) & (where < groups), 1.0, 0.0)
-            part = lax.dot_general(
-                window[j] * inside,
-                kb_ref[q, n],
+            parts.append(window[j] * inside)
+        pieces.append(
+            lax.dot_general(
+                jnp.concatenate(parts, axis=1),
+                kb_ref[q].reshape(nb * bs, bs),
                 (((1,), (0,)), ((), ())),
                 precision=lax.Precision.HIGHEST,
                 preferred_element_type=F32,
             )
-            acc = part if acc is None else acc + part
-        pieces.append(acc)
+        )
     return diag * field + jnp.concatenate(pieces, axis=1)
 
 
@@ -563,7 +613,10 @@
     pairs = CY // 2
     half = HALO // 2
     width = min(local, capacity)
-    rhs = pltpu.VMEM((2 * CZ, 2 * width * groups), BF)
+
+    def operands(rows, chunk):
+        deep = 2 * min(chunk, width) * groups
+        return [pltpu.VMEM((rows, deep), BF), pltpu.VMEM((2 * CZ, deep), BF)]
 
     def field(*shape):
         return jax.ShapeDtypeStruct(shape, F32)
@@ -575,12 +628,13 @@
             field(CX * pairs * modes, 2 * CZ),
             field(CX * half * modes, 2 * CZ),
             field(CX * half * modes, 2 * CZ),
+            field(CX - 2, CY + 2, modes, CZ),
         ),
         [sub],
         [*packs, stiff],
-        [pltpu.VMEM((CX * pairs * modes, 2 * width * groups), BF), rhs],
+        operands(CX * pairs * modes, width) + 2 * operands(CX * half * modes, width),
         1 << 32,
-        16,
+        20 if groups <= 4 else 48,
     )
     force = call(
         functools.partial(fluid_kernel, modes, groups, capacity),
@@ -589,16 +643,20 @@
         [sub],
         [*packs, low, high, *source, mdiag, stiff],
         [
-            pltpu.VMEM((2, HALO * pairs * modes, 2 * CZ), F32),
-            pltpu.VMEM((4, HALO * half * modes, 2 * CZ), F32),
-            pltpu.VMEM((CX + 2, CY + 2, modes, CZ), F32),
+            *[pltpu.VMEM((HALO * pairs * modes, 2 * CZ), F32)] * 2,
+            *[pltpu.VMEM((HALO * half * modes, 2 * CZ), F32)] * 4,
+            pltpu.VMEM((4, CY + 2, modes, CZ), F32),
             pltpu.VMEM((CX * pairs * modes, 4 * CZ), BF),
-            pltpu.VMEM((HALO * pairs * modes, 2 * width * groups), BF),
-            rhs,
             pltpu.VMEM((groups, modes, local), F32),
+            *[
+                x
+                for chunk in (128, 256)
+                for x in operands(HALO * pairs * modes, chunk)
+                + 2 * operands(HALO * half * modes, chunk)
+            ],
         ],
         1 << 32,
-        16,
+        20 if groups <= 4 else 48,
     )
     parts = [force[0]] + [shifted(force[k], "sub", k) for k in range(1, groups)]
     keep, send, mass = call(

time: 64 us -> 62.9 us (0.983); the launches traced: 63 us -> 63 us
  Pallas kernels: 17.6 us -> 21.2 us
  waiting for transfers between devices: 24.9 us -> 21.3 us
    ppermute x8, waiting for transfers between devices: 16.3 us -> 12.5 us  [shifted(): return lax.ppermute(x, axis, [(i, (i + k) % n) for i in range(n)])]
    pallas_call x5, Pallas kernels: 16.1 us -> 19.7 us  [call(): pl.pallas_call(kernel, name=name, out_shape=out_shape, in_specs=[smem()]...]
  transfers between devices with their start and end apart: 16 -> 16, of which waited for: 12 -> 12; matrix products, arithmetic and copies ran while one was open for 0% -> 0% of each run, Pallas kernels for 9% -> 12%
where the time goes in v4:
time: 62.9 us; the launch traced here: 63 us
  waiting for transfers between devices  21.3 us (34%)
  Pallas kernels  21.2 us (34%)
  starting transfers between devices  19 us (30%)
  between operations  1.38 us (2%)
    pallas_call x5, Pallas kernels, call(): pl.pallas_call(kernel, name=name, out_shape=out_shape, in_specs=[smem()]...  19.7 us
    ppermute x8, waiting for transfers between devices, shifted(): return lax.ppermute(x, axis, [(i, (i + k) % n) for i in range(n)])  12.5 us
    ppermute x8, starting transfers between devices, shifted(): return lax.ppermute(x, axis, [(i, (i + k) % n) for i in range(n)])  10.6 us
    ppermute x8, waiting for transfers between devices, swapped(): return lax.ppermute(x, axis, [(i, i ^ k) for i in range(n)])  8.86 us
    ppermute x8, starting transfers between devices, swapped(): return lax.ppermute(x, axis, [(i, i ^ k) for i in range(n)])  8.4 us
    pallas_call x1, Pallas kernels, body(): pl.pallas_call(functools.partial(pack_kernel, modes, groups), name='pack'...  1.51 us
  transfers between devices with their start and end apart: 16, of which 12 were waited for; matrix products, arithmetic and copies ran while one was open for 0% of the time, Pallas kernels for 12%

profile of v4, /device:TPU:0, one launch (start us, length us, event | category | flops | bytes accessed | tf_op | source)
XLA Modules:
  0.0 63.0 jit_solution(8157645990150730273)
XLA Ops:
  1.3 1.5 %pack.1 = (f32[56,256]{1,0:T(8,128)S(1)}, f32[1,256]{1,0:T(1,128)S(1)}, f32[1,256]{1,0:T(1,128)S(1)}, s32[2,4]{1,0:T(2,128)S(1)}) custom-call(s32[1]{0:T(128)S(6)} %copy.13.live_ref, s32[8,128]{1,0:T(8,128)} %bitcast.16, s32[8,128]{1,0:T(8,128)} %bitcast.17, s32[8,128]{1,0:T(8,128)} %bitcast.18, f32[8,128]{1,0:T(8,128)} %bitcast.19, f32[32,256]{1,0:T(8,128)} %refs_4_.1, ...), custom_call_target="tpu_custom_call" | custom-call | flops 268435456 | bytes 1048576 | tf_op jit(solution)/shard_map/pack/pallas_call | solution.py:570
  2.8 5.1 %collective-permute-start.2 = (f32[56,256]{1,0:T(8,128)S(1)}, f32[56,256]{1,0:T(8,128)S(1)}, u32[]{:S(2)}, u32[]{:S(2)}) collective-permute-start(f32[56,256]{1,0:T(8,128)S(1)} %get-tuple-element.19.own.refs_0_.pack), channel_id=1, source_target_pairs={{0,3},{1,0},{2,1},{3,2},{4,7},{5,4},{6,5},{7,6},{8,11},{9,8},{10,9... | collective-permute-start | bytes 172040 | tf_op jit(solution)/shard_map/ppermute | solution.py:507
  7.9 1.0 %collective-permute-start = (f32[56,256]{1,0:T(8,128)S(1)}, f32[56,256]{1,0:T(8,128)S(1)}, u32[]{:S(2)}, u32[]{:S(2)}) collective-permute-start(f32[56,256]{1,0:T(8,128)S(1)} %get-tuple-element.19.own.refs_0_.pack), channel_id=1, source_target_pairs={{0,1},{1,2},{2,3},{3,0},{4,5},{5,6},{6,7},{7,4},{8,9},{9,10},{10,1... | collective-permute-start | bytes 172040 | tf_op jit(solution)/shard_map/ppermute | solution.py:507
  8.9 0.1 pad_add_fusion.sub_ref
  9.0 1.2 %collective-permute-done.2.nxt.refs_3_ = f32[56,256]{1,0:T(8,128)S(1)} collective-permute-done((f32[56,256]{1,0:T(8,128)S(1)}, f32[56,256]{1,0:T(8,128)S(1)}, u32[]{:S(2)}, u32[]{:S(2)}) %collective-permute-start.2) | collective-permute-done | bytes 57376 | tf_op jit(solution)/shard_map/ppermute | solution.py:507
  10.2 2.9 %collective-permute-done.1.refs_2_ = f32[56,256]{1,0:T(8,128)S(1)} collective-permute-done((f32[56,256]{1,0:T(8,128)S(1)}, f32[56,256]{1,0:T(8,128)S(1)}, u32[]{:S(2)}, u32[]{:S(2)}) %collective-permute-start.1) | collective-permute-done | bytes 57376 | tf_op jit(solution)/shard_map/ppermute | solution.py:507
  13.1 0.8 %collective-permute-done.prev.refs_1_ = f32[56,256]{1,0:T(8,128)S(1)} collective-permute-done((f32[56,256]{1,0:T(8,128)S(1)}, f32[56,256]{1,0:T(8,128)S(1)}, u32[]{:S(2)}, u32[]{:S(2)}) %collective-permute-start) | collective-permute-done | bytes 57376 | tf_op jit(solution)/shard_map/ppermute | solution.py:507
  13.9 0.5 collective-permute-start.4
  14.4 0.0 collective-permute-start.3
  14.5 0.9 %stiff.1.refs_4_.refs_11_ = f32[32,256]{1,0:T(8,128)S(1)} custom-call(s32[2]{0:T(128)S(1)} %pad_add_fusion.sub_ref, s32[2,4]{1,0:T(2,128)S(1)} %get-tuple-element.18.cols_ref, f32[56,256]{1,0:T(8,128)S(1)} %collective-permute-done.prev.refs_1_, f32[56,256]{1,0:T(8,128)S(1)} %get-tuple-element.19.own.refs_0_.pack, ...), custom_call_target="tpu_custom_call" | custom-call | flops 536870912 | bytes 1048576 | tf_op jit(solution)/shard_map/stiff/pallas_call | solution.py:537
  15.4 6.4 %own_source.1 = (f32[1024,256]{1,0:T(8,128)S(1)}, f32[256,256]{1,0:T(8,128)S(1)}, f32[256,256]{1,0:T(8,128)S(1)}, f32[6,10,32,128]{3,2,1,0:T(8,128)S(1)}) custom-call(s32[2]{0:T(128)S(1)} %pad_add_fusion.sub_ref, f32[56,256]{1,0:T(8,128)S(1)} %get-tuple-element.19.own.refs_0_.pack, f32[56,256]{1,0:T(8,128)S(1)} %collective-permute-done.prev.refs_1_, ...), custom_call_target="tpu_custom_call" | custom-call | flops 4294967296 | bytes 1048576 | tf_op jit(solution)/shard_map/own_source/pallas_call | solution.py:537
  21.9 1.0 %collective-permute-done.3.refs_4_ = f32[4,56,256]{2,1,0:T(8,128)S(1)} collective-permute-done((f32[4,56,256]{2,1,0:T(8,128)S(1)}, f32[4,56,256]{2,1,0:T(8,128)S(1)}, u32[]{:S(2)}, u32[]{:S(2)}) %collective-permute-start.3) | collective-permute-done | bytes 229408 | tf_op jit(solution)/shard_map/ppermute | solution.py:507
  22.9 9.6 %fluid.1 = (f32[3,32,256]{2,1,0:T(8,128)S(1)}, f32[4,32,256]{2,1,0:T(8,128)S(1)}, f32[3,32,256]{2,1,0:T(8,128)S(1)}, f32[4,32,256]{2,1,0:T(8,128)S(1)}) custom-call(s32[2]{0:T(128)S(1)} %pad_add_fusion.sub_ref, f32[56,256]{1,0:T(8,128)S(1)} %get-tuple-element.19.own.refs_0_.pack, f32[56,256]{1,0:T(8,128)S(1)} %collective-permute-done.prev.refs_1_, ...), custom_call_target="tpu_custom_call" | custom-call | flops 4294967296 | bytes 1048576 | tf_op jit(solution)/shard_map/fluid/pallas_call | solution.py:537
  32.5 0.1 collective-permute-start.5
  32.6 3.8 %collective-permute-start.7 = (f32[4,32,256]{2,1,0:T(8,128)S(1)}, f32[4,32,256]{2,1,0:T(8,128)S(1)}, u32[]{:S(2)}, u32[]{:S(2)}) collective-permute-start(f32[4,32,256]{2,1,0:T(8,128)S(1)} %get-tuple-element.29), channel_id=1, source_target_pairs={{0,3},{1,0},{2,1},{3,2},{4,7},{5,4},{6,5},{7,6},{8,11},{9,8},{10,9... | collective-permute-start | bytes 393224 | tf_op jit(solution)/shard_map/ppermute | solution.py:507
  36.4 6.6 %collective-permute-done.6.refs_2_ = f32[3,32,256]{2,1,0:T(8,128)S(1)} collective-permute-done((f32[3,32,256]{2,1,0:T(8,128)S(1)}, f32[3,32,256]{2,1,0:T(8,128)S(1)}, u32[]{:S(2)}, u32[]{:S(2)}) %collective-permute-start.6) | collective-permute-done | bytes 98336 | tf_op jit(solution)/shard_map/ppermute | solution.py:507
  42.9 1.3 %gram.1 = (f32[48,128]{1,0:T(8,128)S(1)}, f32[48,128]{1,0:T(8,128)S(1)}, f32[32,256]{1,0:T(8,128)S(1)}) custom-call(s32[2]{0:T(128)S(1)} %pad_add_fusion.sub_ref, s32[2,4]{1,0:T(2,128)S(1)} %get-tuple-element.18.cols_ref, f32[56,256]{1,0:T(8,128)S(1)} %get-tuple-element.19.own.refs_0_.pack, f32[3,32,256]{2,1,0:T(8,128)S(1)} %get-tuple-element.26.refs_0_, ...), custom_call_target="tpu_custom_call" | custom-call | flops 536870912 | bytes 1048576 | tf_op jit(solution)/shard_map/gram/pallas_call | solution.py:537
  44.2 0.1 collective-permute-start.8
  44.3 1.2 %collective-permute-done.8 = f32[48,128]{1,0:T(8,128)S(1)} collective-permute-done((f32[48,128]{1,0:T(8,128)S(1)}, f32[48,128]{1,0:T(8,128)S(1)}, u32[]{:S(2)}, u32[]{:S(2)}) %collective-permute-start.8) | collective-permute-done | bytes 24608 | tf_op jit(solution)/shard_map/ppermute | solution.py:512
  45.5 1.3 %collective-permute-start.11 = (f32[48,128]{1,0:T(8,128)S(1)}, f32[48,128]{1,0:T(8,128)S(1)}, u32[]{:S(2)}, u32[]{:S(2)}) collective-permute-start(f32[48,128]{1,0:T(8,128)S(1)} %add.21), channel_id=1, source_target_pairs={{0,24},{4,28},{8,16},{12,20},{16,8},{20,12},{24,0},{28,4},{1,25},{... | collective-permute-start | bytes 73736 | tf_op jit(solution)/shard_map/ppermute | solution.py:512
  46.8 0.7 %collective-permute-start.10 = (f32[48,128]{1,0:T(8,128)S(1)}, f32[48,128]{1,0:T(8,128)S(1)}, u32[]{:S(2)}, u32[]{:S(2)}) collective-permute-start(f32[48,128]{1,0:T(8,128)S(1)} %add.21), channel_id=1, source_target_pairs={{0,16},{4,20},{8,24},{12,28},{16,0},{20,4},{24,8},{28,12},{1,17},{... | collective-permute-start | bytes 73736 | tf_op jit(solution)/shard_map/ppermute | solution.py:512
  47.5 1.4 %collective-permute-start.9 = (f32[48,128]{1,0:T(8,128)S(1)}, f32[48,128]{1,0:T(8,128)S(1)}, u32[]{:S(2)}, u32[]{:S(2)}) collective-permute-start(f32[48,128]{1,0:T(8,128)S(1)} %add.21), channel_id=1, source_target_pairs={{0,8},{4,12},{8,0},{12,4},{16,24},{20,28},{24,16},{28,20},{1,9},{5... | collective-permute-start | bytes 73736 | tf_op jit(solution)/shard_map/ppermute | solution.py:512
  49.0 1.2 %collective-permute-done.11 = f32[48,128]{1,0:T(8,128)S(1)} collective-permute-done((f32[48,128]{1,0:T(8,128)S(1)}, f32[48,128]{1,0:T(8,128)S(1)}, u32[]{:S(2)}, u32[]{:S(2)}) %collective-permute-start.11) | collective-permute-done | bytes 24608 | tf_op jit(solution)/shard_map/ppermute | solution.py:512
  50.2 0.4 collective-permute-done.10
  50.6 0.7 %collective-permute-done.9 = f32[48,128]{1,0:T(8,128)S(1)} collective-permute-done((f32[48,128]{1,0:T(8,128)S(1)}, f32[48,128]{1,0:T(8,128)S(1)}, u32[]{:S(2)}, u32[]{:S(2)}) %collective-permute-start.9) | collective-permute-done | bytes 24608 | tf_op jit(solution)/shard_map/ppermute | solution.py:512
  51.4 4.1 %collective-permute-start.14 = (f32[48,128]{1,0:T(8,128)S(1)}, f32[48,128]{1,0:T(8,128)S(1)}, u32[]{:S(2)}, u32[]{:S(2)}) collective-permute-start(f32[48,128]{1,0:T(8,128)S(1)} %add_add_fusion.1), channel_id=1, source_target_pairs={{0,3},{1,2},{2,1},{3,0},{4,7},{5,6},{6,5},{7,4},{8,11},{9,10},{10,... | collective-permute-start | bytes 73736 | tf_op jit(solution)/shard_map/ppermute | solution.py:512
  55.5 0.6 %collective-permute-start.12 = (f32[48,128]{1,0:T(8,128)S(1)}, f32[48,128]{1,0:T(8,128)S(1)}, u32[]{:S(2)}, u32[]{:S(2)}) collective-permute-start(f32[48,128]{1,0:T(8,128)S(1)} %add_add_fusion.1), channel_id=1, source_target_pairs={{0,1},{1,0},{2,3},{3,2},{4,5},{5,4},{6,7},{7,6},{8,9},{9,8},{10,11... | collective-permute-start | bytes 73736 | tf_op jit(solution)/shard_map/ppermute | solution.py:512
  56.2 1.2 %collective-permute-done.14 = f32[48,128]{1,0:T(8,128)S(1)} collective-permute-done((f32[48,128]{1,0:T(8,128)S(1)}, f32[48,128]{1,0:T(8,128)S(1)}, u32[]{:S(2)}, u32[]{:S(2)}) %collective-permute-start.14) | collective-permute-done | bytes 24608 | tf_op jit(solution)/shard_map/ppermute | solution.py:512
  57.3 2.9 %collective-permute-done.13 = f32[48,128]{1,0:T(8,128)S(1)} collective-permute-done((f32[48,128]{1,0:T(8,128)S(1)}, f32[48,128]{1,0:T(8,128)S(1)}, u32[]{:S(2)}, u32[]{:S(2)}) %collective-permute-start.13) | collective-permute-done | bytes 24608 | tf_op jit(solution)/shard_map/ppermute | solution.py:512
  60.3 0.1 collective-permute-start.15
  60.3 1.2 %collective-permute-done.15.other = f32[48,128]{1,0:T(8,128)S(1)} collective-permute-done((f32[48,128]{1,0:T(8,128)S(1)}, f32[48,128]{1,0:T(8,128)S(1)}, u32[]{:S(2)}, u32[]{:S(2)}) %collective-permute-start.15) | collective-permute-done | bytes 24608 | tf_op jit(solution)/shard_map/ppermute | solution.py:512
  61.5 1.5 %final.1 = (f32[32,256]{1,0:T(8,128)}, f32[64,64]{1,0:T(8,128)}, f32[64,64]{1,0:T(8,128)}) custom-call(s32[2]{0:T(128)S(1)} %pad_add_fusion.sub_ref, f32[48,128]{1,0:T(8,128)S(1)} %add_add_fusion.mine, f32[48,128]{1,0:T(8,128)S(1)} %collective-permute-done.15.other, f32[32,256]{1,0:T(8,128)S(1)} %stiff.1.refs_4_.refs_11_, f32[32,256]{1,0:T(8,128)S(1)} %get-tuple-element.32.mass), custom_call_target="tpu_custom_call" | custom-call | flops 1048576 | bytes 1048576 | tf_op jit(solution)/shard_map/final/pallas_call | solution.py:537
  (13 shorter events, 0.1 us)
Async XLA Ops:
  1.3 13.2 %copy-start = (f32[2,4,128,128]{3,2,1,0:T(8,128)S(1)}, f32[2,4,128,128]{3,2,1,0:T(8,128)}, u32[]{:S(2)}) copy-start(f32[2,4,128,128]{3,2,1,0:T(8,128)} %refs_6_.1) | copy-start | bytes 1572868
  2.8 7.4 %collective-permute-start.2 = (f32[56,256]{1,0:T(8,128)S(1)}, f32[56,256]{1,0:T(8,128)S(1)}, u32[]{:S(2)}, u32[]{:S(2)}) collective-permute-start(f32[56,256]{1,0:T(8,128)S(1)} %get-tuple-element.19.own.refs_0_.pack), channel_id=1, source_target_pairs={{0,3},{1,0},{2,1},{3,2},{4,7},{5,4},{6,5},{7,6},{8,11},{9,8},{10,9... | collective-permute-start | bytes 172040 | tf_op jit(solution)/shard_map/ppermute | solution.py:507
  7.9 5.2 %collective-permute-start.1 = (f32[56,256]{1,0:T(8,128)S(1)}, f32[56,256]{1,0:T(8,128)S(1)}, u32[]{:S(2)}, u32[]{:S(2)}) collective-permute-start(f32[56,256]{1,0:T(8,128)S(1)} %get-tuple-element.19.own.refs_0_.pack), channel_id=1, source_target_pairs={{0,2},{1,3},{2,0},{3,1},{4,6},{5,7},{6,4},{7,5},{8,10},{9,11},{10,... | collective-permute-start | bytes 172040 | tf_op jit(solution)/shard_map/ppermute | solution.py:507
  7.9 6.0 %collective-permute-start = (f32[56,256]{1,0:T(8,128)S(1)}, f32[56,256]{1,0:T(8,128)S(1)}, u32[]{:S(2)}, u32[]{:S(2)}) collective-permute-start(f32[56,256]{1,0:T(8,128)S(1)} %get-tuple-element.19.own.refs_0_.pack), channel_id=1, source_target_pairs={{0,1},{1,2},{2,3},{3,0},{4,5},{5,6},{6,7},{7,4},{8,9},{9,10},{10,1... | collective-permute-start | bytes 172040 | tf_op jit(solution)/shard_map/ppermute | solution.py:507
  13.9 7.9 %collective-permute-start.4 = (f32[4,56,256]{2,1,0:T(8,128)S(1)}, f32[4,56,256]{2,1,0:T(8,128)S(1)}, u32[]{:S(2)}, u32[]{:S(2)}) collective-permute-start(f32[4,56,256]{2,1,0:T(8,128)S(1)} %pad_maximum_fusion), channel_id=1, source_target_pairs={{0,28},{4,0},{8,4},{12,8},{16,12},{20,16},{24,20},{28,24},{1,29},{... | collective-permute-start | bytes 688136 | tf_op jit(solution)/shard_map/ppermute | solution.py:507
  14.4 8.4 %collective-permute-start.3 = (f32[4,56,256]{2,1,0:T(8,128)S(1)}, f32[4,56,256]{2,1,0:T(8,128)S(1)}, u32[]{:S(2)}, u32[]{:S(2)}) collective-permute-start(f32[4,56,256]{2,1,0:T(8,128)S(1)} %pad_maximum_fusion), channel_id=1, source_target_pairs={{0,4},{4,8},{8,12},{12,16},{16,20},{20,24},{24,28},{28,0},{1,5},{5... | collective-permute-start | bytes 688136 | tf_op jit(solution)/shard_map/ppermute | solution.py:507
  32.5 10.4 %collective-permute-start.5 = (f32[4,32,256]{2,1,0:T(8,128)S(1)}, f32[4,32,256]{2,1,0:T(8,128)S(1)}, u32[]{:S(2)}, u32[]{:S(2)}) collective-permute-start(f32[4,32,256]{2,1,0:T(8,128)S(1)} %get-tuple-element.27), channel_id=1, source_target_pairs={{0,1},{1,2},{2,3},{3,0},{4,5},{5,6},{6,7},{7,4},{8,9},{9,10},{10,1... | collective-permute-start | bytes 393224 | tf_op jit(solution)/shard_map/ppermute | solution.py:507
  32.6 10.4 %collective-permute-start.7 = (f32[4,32,256]{2,1,0:T(8,128)S(1)}, f32[4,32,256]{2,1,0:T(8,128)S(1)}, u32[]{:S(2)}, u32[]{:S(2)}) collective-permute-start(f32[4,32,256]{2,1,0:T(8,128)S(1)} %get-tuple-element.29), channel_id=1, source_target_pairs={{0,3},{1,0},{2,1},{3,2},{4,7},{5,4},{6,5},{7,6},{8,11},{9,8},{10,9... | collective-permute-start | bytes 393224 | tf_op jit(solution)/shard_map/ppermute | solution.py:507
  36.4 6.6 %collective-permute-start.6 = (f32[3,32,256]{2,1,0:T(8,128)S(1)}, f32[3,32,256]{2,1,0:T(8,128)S(1)}, u32[]{:S(2)}, u32[]{:S(2)}) collective-permute-start(f32[3,32,256]{2,1,0:T(8,128)S(1)} %get-tuple-element.28), channel_id=1, source_target_pairs={{0,2},{1,3},{2,0},{3,1},{4,6},{5,7},{6,4},{7,5},{8,10},{9,11},{10,... | collective-permute-start | bytes 294920 | tf_op jit(solution)/shard_map/ppermute | solution.py:507
  44.2 1.3 %collective-permute-start.8 = (f32[48,128]{1,0:T(8,128)S(1)}, f32[48,128]{1,0:T(8,128)S(1)}, u32[]{:S(2)}, u32[]{:S(2)}) collective-permute-start(f32[48,128]{1,0:T(8,128)S(1)} %get-tuple-element.31), channel_id=1, source_target_pairs={{0,4},{4,0},{8,12},{12,8},{16,20},{20,16},{24,28},{28,24},{1,5},{5... | collective-permute-start | bytes 73736 | tf_op jit(solution)/shard_map/ppermute | solution.py:512
  45.5 4.7 %collective-permute-start.11 = (f32[48,128]{1,0:T(8,128)S(1)}, f32[48,128]{1,0:T(8,128)S(1)}, u32[]{:S(2)}, u32[]{:S(2)}) collective-permute-start(f32[48,128]{1,0:T(8,128)S(1)} %add.21), channel_id=1, source_target_pairs={{0,24},{4,28},{8,16},{12,20},{16,8},{20,12},{24,0},{28,4},{1,25},{... | collective-permute-start | bytes 73736 | tf_op jit(solution)/shard_map/ppermute | solution.py:512
  46.8 3.8 %collective-permute-start.10 = (f32[48,128]{1,0:T(8,128)S(1)}, f32[48,128]{1,0:T(8,128)S(1)}, u32[]{:S(2)}, u32[]{:S(2)}) collective-permute-start(f32[48,128]{1,0:T(8,128)S(1)} %add.21), channel_id=1, source_target_pairs={{0,16},{4,20},{8,24},{12,28},{16,0},{20,4},{24,8},{28,12},{1,17},{... | collective-permute-start | bytes 73736 | tf_op jit(solution)/shard_map/ppermute | solution.py:512
  47.5 3.8 %collective-permute-start.9 = (f32[48,128]{1,0:T(8,128)S(1)}, f32[48,128]{1,0:T(8,128)S(1)}, u32[]{:S(2)}, u32[]{:S(2)}) collective-permute-start(f32[48,128]{1,0:T(8,128)S(1)} %add.21), channel_id=1, source_target_pairs={{0,8},{4,12},{8,0},{12,4},{16,24},{20,28},{24,16},{28,20},{1,9},{5... | collective-permute-start | bytes 73736 | tf_op jit(solution)/shard_map/ppermute | solution.py:512
  51.4 5.9 %collective-permute-start.14 = (f32[48,128]{1,0:T(8,128)S(1)}, f32[48,128]{1,0:T(8,128)S(1)}, u32[]{:S(2)}, u32[]{:S(2)}) collective-permute-start(f32[48,128]{1,0:T(8,128)S(1)} %add_add_fusion.1), channel_id=1, source_target_pairs={{0,3},{1,2},{2,1},{3,0},{4,7},{5,6},{6,5},{7,4},{8,11},{9,10},{10,... | collective-permute-start | bytes 73736 | tf_op jit(solution)/shard_map/ppermute | solution.py:512
  55.5 4.7 %collective-permute-start.13 = (f32[48,128]{1,0:T(8,128)S(1)}, f32[48,128]{1,0:T(8,128)S(1)}, u32[]{:S(2)}, u32[]{:S(2)}) collective-permute-start(f32[48,128]{1,0:T(8,128)S(1)} %add_add_fusion.1), channel_id=1, source_target_pairs={{0,2},{1,3},{2,0},{3,1},{4,6},{5,7},{6,4},{7,5},{8,10},{9,11},{10,... | collective-permute-start | bytes 73736 | tf_op jit(solution)/shard_map/ppermute | solution.py:512
  55.5 4.7 %collective-permute-start.12 = (f32[48,128]{1,0:T(8,128)S(1)}, f32[48,128]{1,0:T(8,128)S(1)}, u32[]{:S(2)}, u32[]{:S(2)}) collective-permute-start(f32[48,128]{1,0:T(8,128)S(1)} %add_add_fusion.1), channel_id=1, source_target_pairs={{0,1},{1,0},{2,3},{3,2},{4,5},{5,4},{6,7},{7,6},{8,9},{9,8},{10,11... | collective-permute-start | bytes 73736 | tf_op jit(solution)/shard_map/ppermute | solution.py:512
  60.3 1.3 %collective-permute-start.15 = (f32[48,128]{1,0:T(8,128)S(1)}, f32[48,128]{1,0:T(8,128)S(1)}, u32[]{:S(2)}, u32[]{:S(2)}) collective-permute-start(f32[48,128]{1,0:T(8,128)S(1)} %add_add_fusion.mine), channel_id=1, source_target_pairs={{0,4},{4,0},{8,12},{12,8},{16,20},{20,16},{24,28},{28,24},{1,5},{5... | collective-permute-start | bytes 73736 | tf_op jit(solution)/shard_map/ppermute | solution.py:512

commit v5 on v4

--- a/solution.py
+++ b/solution.py
@@ -147,9 +147,12 @@
 
     def row(self, kind, owner, chunk):
         at = owner * self.capacity + chunk * self.width
-        line = lax.shift_right_logical(at, log2(self.local))
+        line = at // self.local if isinstance(at, int) else lax.shift_right_logical(at, log2(self.local))
         x = self.blk[pl.ds(self.modes + kind * self.lines + line, 1), :]
         if self.width < self.local:
+            if isinstance(at, int):
+                first = at % self.local
+                return x[:, first : first + self.width]
             group = lax.shift_right_logical(at, log2(self.width)) & (self.local // self.width - 1)
             got = x[:, : self.width]
             for g in range(1, self.local // self.width):
@@ -166,15 +169,25 @@
         return a, b, cell & (CZ - 1), node, weight
 
 
-def fill(lists, owner, chunk, a_first, a_count, b_first, b_count, inside, lhs, rhs, at, side):
+def each(n, step):
+    if n <= 4:
+        for i in range(n):
+            step(i)
+        return
+
+    def one(i, carry):
+        step(i)
+        return carry
+
+    lax.fori_loop(0, n, one, 0)
+
+
+def fill(lists, owner, chunk, a_first, a_count, lhs, rhs, at):
     modes, width = lists.modes, lists.width
     a, b, c, node, weight = lists.load(owner, chunk)
-    if inside is not None:
-        weight = weight * inside
-    aloc, bloc = a - a_first, b - b_first
-    valid = (aloc >= 0) & (aloc < a_count) & (bloc >= 0) & (bloc < 2 * b_count)
-    pair = jnp.where(valid, aloc * b_count + lax.shift_right_arithmetic(bloc, 1), -1)
-    place = (b & 1) * CZ + c
+    aloc = a - a_first
+    valid = (aloc >= 0) & (aloc < a_count)
+    pair = jnp.where(valid, lax.shift_right_logical(b, 1) * a_count + aloc, -16)
     pieces = []
     for h in range(width // 128):
         idx = node[:, h * 128 : (h + 1) * 128]
@@ -183,46 +196,59 @@
             part = lanes_from(lists.blk[0:modes, g * 128 : (g + 1) * 128], idx & 127)
             got = part if g == 0 else jnp.where(lax.shift_right_logical(idx, 7) == g, part, got)
         pieces.append(got)
-    hi, lo = split(jnp.concatenate(pieces, axis=1) * weight)
-    wide = jnp.broadcast_to(pair.astype(F32), (modes, width)).astype(BF)
-    zero = jnp.zeros((modes, width), BF)
-    for r in range(a_count * b_count):
+    vals = jnp.concatenate(pieces, axis=1) * weight
+    times = max(1, 16 // modes)
+    tall = times * modes
+    hi, lo = split(jnp.concatenate([vals] * times, axis=0))
+    step = lax.shift_right_logical(
+        lax.broadcasted_iota(jnp.int32, (tall, width), 0), log2(modes)
+    )
+    wide = (pair - step).astype(F32).astype(BF)
+    zero = jnp.zeros((tall, width), BF)
+    first, then = pl.ds(at, width), pl.ds(at + width, width)
+    for r in range(0, a_count * CY // 2, times):
         mask = wide == jnp.asarray(r, BF)
-        lhs[r * modes : (r + 1) * modes, at : at + width] = jnp.where(mask, hi, zero)
-        lhs[r * modes : (r + 1) * modes, at + width : at + 2 * width] = jnp.where(mask, lo, zero)
-    hot = onehot(place, 2 * CZ)
-    rhs[:, at : at + width] = hot
-    rhs[:, at + width : at + 2 * width] = hot
-
-
-def scatter(
-    blks, modes, capacity, owner, inside, a_first, a_count, b_first, b_count, out, lhs, rhs, width=None
-):
-    every = [Lists(blk, modes, capacity, width) for blk in blks]
-    width = every[0].width
-    spec = (a_first, a_count, b_first, b_count, inside)
-    counts = []
-    for k, lists in enumerate(every):
-        last = jnp.zeros((1, width), jnp.int32)
+        lhs[r * modes : r * modes + tall, first] = jnp.where(mask, hi, zero)
+        lhs[r * modes : r * modes + tall, then] = jnp.where(mask, lo, zero)
+    hot = onehot((b & 1) * CZ + c, 2 * CZ)
+    rhs[:, first] = hot
+    rhs[:, then] = hot
+
+
+def scatter(both, modes, capacity, owner, a_first, a_count, out, lhs, rhs, width=None):
+    groups = both.shape[0]
+
+    def lists_of(k):
+        return Lists(both.at[k], modes, capacity, width)
+
+    some = lists_of(0)
+    wide = some.width
+
+    def first(k):
+        at = 2 * k * wide
+        at = at if isinstance(k, int) else pl.multiple_of(at, 128)
+        fill(lists_of(k), owner, 0, a_first, a_count, lhs, rhs, at)
+
+    each(groups, first)
+    out[...] = dot_t(lhs[...], rhs[...])
+    jobs = []
+    if some.chunks == 1:
+        return jobs
+    for k in range(groups):
+        lists = lists_of(k)
+        last = jnp.zeros((1, wide), jnp.int32)
         for chunk in range(1, lists.chunks):
             a, b, c, node, weight = lists.load(owner, chunk)
             needed = (weight > 0.0) & (a >= a_first) & (a < a_first + a_count)
             last = jnp.where(needed, chunk + 1, last)
-        counts.append(last)
-        fill(lists, owner, 0, *spec, lhs, rhs, 2 * k * width, None)
-    out[...] = dot_t(lhs[...], rhs[...])
-    if every[0].chunks == 1:
-        return []
-
-    def more(lists):
-        def one(chunk, carry):
-            fill(lists, owner, chunk, *spec, lhs, rhs, 0, None)
-            out[...] += dot_t(lhs[:, 0 : 2 * width], rhs[:, 0 : 2 * width])
+
+        def one(chunk, carry, lists=lists):
+            fill(lists, owner, chunk, a_first, a_count, lhs, rhs, 0)
+            out[...] += dot_t(lhs[:, 0 : 2 * wide], rhs[:, 0 : 2 * wide])
             return carry
 
-        return one
-
-    return [(count, more(lists)) for count, lists in zip(counts, every)]
+        jobs.append((last, one))
+    return jobs
 
 
 def later_chunks(jobs):
@@ -239,12 +265,6 @@
             lax.fori_loop(1, last, one, 0)
 
 
-def around(sub, groups):
-    below = jnp.maximum(sub - 1, 0), jnp.where(sub > 0, 1.0, 0.0)
-    above = jnp.minimum(sub + 1, groups - 1), jnp.where(sub < groups - 1, 1.0, 0.0)
-    return below, above
-
-
 def shift_sum(x):
     lane = lax.broadcasted_iota(jnp.int32, x.shape, 1)
     left = jnp.where(lane == 0, 0.0, pltpu.roll(x, 1, 1))
@@ -252,96 +272,78 @@
     return x + 0.5 * (left + right)
 
 
-def plane_sum(src, a, b_range):
-    cols = [src(a, b) + 0.5 * (src(a - 1, b) + src(a + 1, b)) for b in b_range]
-    return [
-        shift_sum(cols[i] + 0.5 * (cols[i - 1] + cols[i + 1])) for i in range(1, len(cols) - 1)
-    ]
-
-
-def second_plane(src, a, lo_in, hi_in):
+def plane_sum(src, a, count):
+    cols = [src(a, b) + 0.5 * (src(a - 1, b) + src(a + 1, b)) for b in range(count)]
     out = []
-    for i, t in enumerate(plane_sum(src, a, range(CY + 2 * HALO))):
-        sec = SEC_U * src(a, i + 1) + SEC_T * t
-        if i + 1 < HALO:
-            sec = sec * lo_in
-        if i + 1 >= CY + HALO:
-            sec = sec * hi_in
-        out.append(sec)
+    for b in range(count):
+        beside = [cols[i] for i in (b - 1, b + 1) if 0 <= i < count]
+        total = beside[0] if len(beside) == 1 else beside[0] + beside[1]
+        out.append(shift_sum(cols[b] + 0.5 * total))
     return out
 
 
-def source_reader(modes, mid, below, above, edge=None, corner=None):
-    half = HALO // 2
-
+def second_plane(src, a, count):
+    return [SEC_U * src(a, b) + SEC_T * t for b, t in enumerate(plane_sum(src, a, count))]
+
+
+def source_reader(modes, mid, edge=None):
     def src(a, b):
         lanes = slice((b % 2) * CZ, (b % 2 + 1) * CZ)
-        outer = -1
+        owner, pair = b // CY, b % CY // 2
         if a < HALO:
-            outer = 0
+            ref, at = edge[0], pair * HALO + a
         elif a >= CX + HALO:
-            outer, a = 1, a - CX - HALO
+            ref, at = edge[1], pair * HALO + a - CX - HALO
         else:
-            a = a - HALO
-        if b < HALO:
-            ref, at = (below if outer < 0 else corner[2 * outer]), a * half + b // 2
-        elif b >= CY + HALO:
-            ref = above if outer < 0 else corner[2 * outer + 1]
-            at = a * half + (b - CY - HALO) // 2
-        else:
-            ref, at = (mid if outer < 0 else edge[outer]), a * (CY // 2) + (b - HALO) // 2
-        return ref[at * modes : (at + 1) * modes, lanes]
+            ref, at = mid, pair * CX + a - HALO
+        return ref[owner, at * modes : (at + 1) * modes, lanes]
 
     return src
 
 
-def own_source_kernel(modes, groups, capacity, sub_ref, *refs):
-    blks = refs[:groups]
-    own, below, above, inner, *scratch = refs[groups + 1 :]
-    sub = sub_ref[0]
-    (lo_owner, lo_in), (hi_owner, hi_in) = around(sub, groups)
-    args = (blks, modes, capacity)
-    half = HALO // 2
-    jobs = scatter(*args, sub, None, 0, CX, 0, CY // 2, own, *scratch[0:2])
-    jobs += scatter(*args, lo_owner, lo_in, 0, CX, CY - HALO, half, below, *scratch[2:4])
-    jobs += scatter(*args, hi_owner, hi_in, 0, CX, 0, half, above, *scratch[4:6])
+def own_source_kernel(modes, groups, capacity, both, _, own, inner, *scratch):
+    jobs = []
+
+    def one(o):
+        at = 2 * o if isinstance(o, int) else 0
+        mem = scratch[at : at + 2]
+        jobs.extend(scatter(both, modes, capacity, o, 0, CX, own.at[o], *mem))
+
+    each(groups, one)
     later_chunks(jobs)
-    src = source_reader(modes, own, below, above)
+    src = source_reader(modes, own)
     for a in range(HALO + 1, CX + HALO - 1):
-        for b, sec in enumerate(second_plane(src, a, lo_in, hi_in)):
+        for b, sec in enumerate(second_plane(src, a, groups * CY)):
             inner[a - HALO - 1, b] = sec
 
 
-def fluid_kernel(modes, groups, capacity, sub_ref, *refs):
-    blks = refs[:groups]
-    low, high, mid, below, above, inner, mdiag, stiff = refs[groups : groups + 8]
-    outs = refs[groups + 8 : 2 * groups + 8]
-    rest = refs[2 * groups + 8 :]
-    edge, corner, outer, press, force = rest[0:2], rest[2:6], rest[6], rest[7], rest[8]
-    scratch = rest[9:]
-    sub = sub_ref[0]
-    local = blks[0].shape[1]
-    half = HALO // 2
-    (lo_owner, lo_in), (hi_owner, hi_in) = around(sub, groups)
+def fluid_kernel(modes, groups, capacity, both, low, high, mid, inner, mdiag, stiff, *refs):
+    outs = refs[:groups]
+    edge, outer, press, force, scratch = (
+        refs[groups : groups + 2],
+        *refs[groups + 2 : groups + 5],
+        refs[groups + 5 :],
+    )
+    local = both.shape[2]
+    count = groups * CY
     jobs = []
-    for side, both in enumerate((low, high)):
-        there = [both.at[k] for k in range(groups)]
+    for side, there in enumerate((low, high)):
         a_first = CX - HALO if side == 0 else 0
         wide = 128 if side == 0 else 256
-        args = (there, modes, capacity)
-        mem = scratch[6 * side : 6 * side + 6]
-        spec = (a_first, HALO)
-        jobs += scatter(*args, sub, None, *spec, 0, CY // 2, edge[side], *mem[0:2], wide)
-        jobs += scatter(
-            *args, lo_owner, lo_in, *spec, CY - HALO, half, corner[2 * side], *mem[2:4], wide
-        )
-        jobs += scatter(
-            *args, hi_owner, hi_in, *spec, 0, half, corner[2 * side + 1], *mem[4:6], wide
-        )
+        half = len(scratch) // 2
+        sets = scratch[side * half : (side + 1) * half]
+
+        def one(o, there=there, a_first=a_first, wide=wide, sets=sets, side=side):
+            at = 2 * o if isinstance(o, int) else 0
+            mem = sets[at : at + 2]
+            target = edge[side].at[o]
+            jobs.extend(scatter(there, modes, capacity, o, a_first, HALO, target, *mem, wide))
+
+        each(groups, one)
     later_chunks(jobs)
-    src = source_reader(modes, mid, below, above, edge, corner)
+    src = source_reader(modes, mid, edge)
     for i, a in enumerate((1, 2, CX + HALO - 1, CX + HALO)):
-        for b, sec in enumerate(second_plane(src, a, lo_in, hi_in)):
+        for b, sec in enumerate(second_plane(src, a, count)):
             outer[i, b] = sec
 
     def second(a, b):
@@ -351,43 +353,73 @@
             return outer[a - CX + HALO, b]
         return inner[a - HALO, b]
 
-    for a in range(CX):
-        for b, t in enumerate(plane_sum(second, a + 1, range(CY + 2))):
-            p = PRE_SRC * src(a + HALO, b + HALO) + PRE_SEC * second(a + 1, b + 1) + PRE_T * t
+    for a in range(0, CX, 2):
+        two = [plane_sum(second, a + 1, count), plane_sum(second, a + 2, count)]
+        for b in range(count):
+            p = jnp.concatenate(
+                [
+                    PRE_SRC * src(a + i + HALO, b) + PRE_SEC * second(a + i + 1, b) + PRE_T * two[i][b]
+                    for i in range(2)
+                ],
+                axis=0,
+            )
             hi, lo = split(p)
-            at = (a * (CY // 2) + b // 2) * modes
+            owner, at = b // CY, (b % CY // 2 * CX + a) * modes
             lanes = (b % 2) * CZ
-            press[at : at + modes, lanes : lanes + CZ] = hi
-            press[at : at + modes, 2 * CZ + lanes : 3 * CZ + lanes] = lo
-
-    def collect(lists, chunk):
-        a, b, c, node, weight = lists.load(sub, chunk)
+            press[owner, at : at + 2 * modes, lanes : lanes + CZ] = hi
+            press[owner, at : at + 2 * modes, 2 * CZ + lanes : 3 * CZ + lanes] = lo
+
+    def collect(k, owner, chunk):
+        lists = Lists(both.at[k], modes, capacity)
+        a, b, c, node, weight = lists.load(owner, chunk)
         hot = onehot((b & 1) * CZ + c, 2 * CZ)
-        got = dot(press[...], jnp.concatenate([hot, hot], axis=0))
-        pair = a * (CY // 2) + lax.shift_right_logical(b, 1)
-        wide = jnp.broadcast_to(pair, (modes, lists.width))
+        got = dot(press[owner], jnp.concatenate([hot, hot], axis=0))
+        pair = jnp.broadcast_to(
+            lax.shift_right_logical(b, 1) * CX + a, (modes, lists.width)
+        )
         picked = jnp.zeros((modes, lists.width), F32)
         for r in range(CX * CY // 2):
-            picked = jnp.where(wide == r, got[r * modes : (r + 1) * modes], picked)
+            picked = jnp.where(pair == r, got[r * modes : (r + 1) * modes], picked)
         hi, lo = split(picked * weight)
-        both = dot_t(jnp.concatenate([hi, lo], axis=0), onehot(node, local))
-        return both[:modes] + both[modes:]
-
-    every = [Lists(blk, modes, capacity) for blk in blks]
-    for k, lists in enumerate(every):
-        add = collect(lists, 0)
-        force[k] = add + mdiag[...] * blks[0][0:modes, :] if k == 0 else add
-        for chunk in range(1, lists.chunks):
-
-            @pl.when(jnp.max(lists.row(2, sub, chunk)) > 0.0)
+        sums = dot_t(jnp.concatenate([hi, lo], axis=0), onehot(node, local))
+        return sums[:modes] + sums[modes:]
+
+    if groups <= 4:
+        for k in range(groups):
+            total = collect(k, 0, 0)
+            for o in range(1, groups):
+                total = total + collect(k, o, 0)
+            force[k] = total
+    else:
+
+        def per_device(k):
+            force[k] = jnp.zeros((modes, local), F32)
+
+            def per_owner(o):
+                force[k] = force[k] + collect(k, o, 0)
+
+            each(groups, per_owner)
+
+        each(groups, per_device)
+    chunks = Lists(both.at[0], modes, capacity).chunks
+    if chunks > 1:
+        later = [(k, o, c) for k in range(groups) for o in range(groups) for c in range(1, chunks)]
+        tops = [
+            jnp.max(Lists(both.at[k], modes, capacity).row(2, o, c)) for k, o, c in later
+        ]
+        for (k, o, c), top in zip(later, tops):
+
+            @pl.when(top > 0.0)
             def _():
-                force[k] += collect(lists, chunk)
+                force[k] = force[k] + collect(k, o, c)
 
     for k in range(groups):
         for w in range(3):
-            outs[k][w] = force[(1 - k - w) % groups]
+            outs[k][w * modes : (w + 1) * modes, :] = force[(1 - k - w) % groups]
         if k in (1, groups - 1):
-            outs[k][3] = stiff[...]
+            at = 3 * modes
+            outs[k][at : at + 8, :] = jnp.broadcast_to(mdiag[...], (8, local))
+            outs[k][at + 8 :, :] = stiff[...]
 
 
 def apply_blocks(window, cols_ref, kb_ref, sub, groups, diag, field):
@@ -426,20 +458,30 @@
     out[...] = apply_blocks(win, cols_ref, kb, sub_ref[0], groups, diag[...], own[0:modes, :])
 
 
-def gram_kernel(modes, groups, sub_ref, cols_ref, pack, *refs):
+def first_mode(modes, groups, count, sub):
+    return pl.multiple_of(lax.shift_right_logical(sub * (modes // groups), log2(count)) * count, count)
+
+
+def gram_kernel(modes, groups, count, sub_ref, cols_ref, prev, pack, nxt, mdiag, *refs):
     parts = refs[:groups]
-    stiff, diag, kb, keep, send, mass, win, gram = refs[groups:]
+    stiff, diag, kb, keep, send, mass, win, gram, force = refs[groups:]
     bs = kb.shape[2]
-    fields = []
-    for w in range(3):
-        m = parts[0][w]
-        for part in parts[1:]:
-            m = m + part[w]
-        fields.append(m)
+    for k in range(groups):
+        source = lax.rem(sub_ref[0] + groups - k, groups)
+        at = first_mode(modes, groups, count, source)
+        for w in range(3):
+            force[w, pl.ds(at, count), :] = parts[k][w * count : (w + 1) * count, :]
+    at = 3 * count
+    before, after = parts[1], parts[groups - 1]
+    fields = [
+        force[0] + before[at : at + 1, :] * prev[0:modes, :],
+        force[1] + mdiag[...] * pack[0:modes, :],
+        force[2] + after[at : at + 1, :] * nxt[0:modes, :],
+    ]
     own = fields[1]
     mass[...] = own
     s = stiff[...]
-    ends = [parts[1][3], s, parts[groups - 1][3]]
+    ends = [before[at + 8 :, :], s, after[at + 8 :, :]]
     both = [jnp.concatenate([x, y], axis=0) for x, y in zip(ends, fields)]
     fill_window(win, both, bs)
     image = apply_blocks(win, cols_ref, kb, sub_ref[0], groups, diag[...], both[1])
@@ -596,7 +638,14 @@
         ]
     )
     packs = [pack] + [shifted(pack, "sub", k) for k in range(1, groups)]
-    both = jnp.stack(packs)
+    mine = max(8, modes // groups)
+    start = first_mode(modes, groups, mine, lax.axis_index("sub").astype(jnp.int32))
+    both = jnp.stack(
+        [
+            jnp.concatenate([lax.dynamic_slice_in_dim(x, start, mine), x[modes:]], axis=0)
+            for x in packs
+        ]
+    )
     low = shifted(both, "passage", 1)
     high = shifted(both, "passage", -1)
     window = [packs[1], packs[0], packs[groups - 1]]
@@ -610,64 +659,60 @@
         [pltpu.VMEM((nwin, modes, bs), F32)],
         1 << 29,
     )
-    pairs = CY // 2
-    half = HALO // 2
     width = min(local, capacity)
+    sets = groups if groups <= 4 else 1
+
+    def field(*shape):
+        return jax.ShapeDtypeStruct(shape, F32)
 
     def operands(rows, chunk):
         deep = 2 * min(chunk, width) * groups
-        return [pltpu.VMEM((rows, deep), BF), pltpu.VMEM((2 * CZ, deep), BF)]
-
-    def field(*shape):
-        return jax.ShapeDtypeStruct(shape, F32)
-
-    source = call(
-        functools.partial(own_source_kernel, modes, groups, capacity),
+        return sets * [pltpu.VMEM((rows, deep), BF), pltpu.VMEM((2 * CZ, deep), BF)]
+
+    rows = CX * CY // 2 * mine
+    edge_rows = HALO * CY // 2 * mine
+    mib = 20 if groups <= 4 else 36
+    source, inner = call(
+        functools.partial(own_source_kernel, mine, groups, capacity),
         "own_source",
-        (
-            field(CX * pairs * modes, 2 * CZ),
-            field(CX * half * modes, 2 * CZ),
-            field(CX * half * modes, 2 * CZ),
-            field(CX - 2, CY + 2, modes, CZ),
+        (field(groups, rows, 2 * CZ), field(CX - 2, groups * CY, mine, CZ)),
+        [],
+        [both, stiff],
+        operands(rows, width),
+        1 << 32,
+        mib,
+    )
+    force = call(
+        functools.partial(fluid_kernel, mine, groups, capacity),
+        "fluid",
+        tuple(
+            field(3 * mine + (8 + modes if k in (1, groups - 1) else 0), local)
+            for k in range(groups)
         ),
-        [sub],
-        [*packs, stiff],
-        operands(CX * pairs * modes, width) + 2 * operands(CX * half * modes, width),
-        1 << 32,
-        20 if groups <= 4 else 48,
-    )
-    force = call(
-        functools.partial(fluid_kernel, modes, groups, capacity),
-        "fluid",
-        tuple(field(4 if k in (1, groups - 1) else 3, modes, local) for k in range(groups)),
-        [sub],
-        [*packs, low, high, *source, mdiag, stiff],
+        [],
+        [both, low, high, source, inner, mdiag, stiff],
         [
-            *[pltpu.VMEM((HALO * pairs * modes, 2 * CZ), F32)] * 2,
-            *[pltpu.VMEM((HALO * half * modes, 2 * CZ), F32)] * 4,
-            pltpu.VMEM((4, CY + 2, modes, CZ), F32),
-            pltpu.VMEM((CX * pairs * modes, 4 * CZ), BF),
-            pltpu.VMEM((groups, modes, local), F32),
-            *[
-                x
-                for chunk in (128, 256)
-                for x in operands(HALO * pairs * modes, chunk)
-                + 2 * operands(HALO * half * modes, chunk)
-            ],
+            *[pltpu.VMEM((groups, edge_rows, 2 * CZ), F32)] * 2,
+            pltpu.VMEM((4, groups * CY, mine, CZ), F32),
+            pltpu.VMEM((groups, rows, 4 * CZ), BF),
+            pltpu.VMEM((groups, mine, local), F32),
+            *operands(edge_rows, 128),
+            *operands(edge_rows, 256),
         ],
         1 << 32,
-        20 if groups <= 4 else 48,
+        mib,
     )
     parts = [force[0]] + [shifted(force[k], "sub", k) for k in range(1, groups)]
     keep, send, mass = call(
-        functools.partial(gram_kernel, modes, groups),
+        functools.partial(gram_kernel, modes, groups, mine),
         "gram",
         (field(3 * modes // 2, 4 * modes), field(3 * modes // 2, 4 * modes), field(modes, local)),
         [sub, cols],
-        [pack, *parts, stiff, diag, kblocks],
+        [*window, mdiag, *parts, stiff, diag, kblocks],
         [
             pltpu.VMEM((nwin, 2 * modes, bs), F32),
             pltpu.VMEM((2, 3 * modes // 2, 4 * modes), F32),
+            pltpu.VMEM((3, modes, local), F32),
         ],
         1 << 29,
     )

time: 62.9 us -> 57.1 us (0.908)
  Pallas kernels: 21.2 us -> 17.9 us
  waiting for transfers between devices: 21.3 us -> 19.2 us
    pallas_call x5, Pallas kernels: 19.7 us -> 16.5 us  [call(): pl.pallas_call(kernel, name=name, out_shape=out_shape, in_specs=[smem()]...]
    ppermute x8, waiting for transfers between devices: 8.86 us -> 7.33 us  [swapped(): return lax.ppermute(x, axis, [(i, i ^ k) for i in range(n)])]
  transfers between devices with their start and end apart: 16 -> 16, of which waited for: 12 -> 13; matrix products, arithmetic and copies ran while one was open for 0% -> 0% of each run, Pallas kernels for 12% -> 8%
where the time goes in v5:
time: 57.1 us; the launch traced here: 57.3 us
  waiting for transfers between devices  19.2 us (34%)
  starting transfers between devices  18.7 us (33%)
  Pallas kernels  17.9 us (31%)
  between operations  1.39 us (2%)
    pallas_call x5, Pallas kernels, call(): pl.pallas_call(kernel, name=name, out_shape=out_shape, in_specs=[smem()]...  16.5 us
    ppermute x8, waiting for transfers between devices, shifted(): return lax.ppermute(x, axis, [(i, (i + k) % n) for i in range(n)])  11.9 us
    ppermute x8, starting transfers between devices, shifted(): return lax.ppermute(x, axis, [(i, (i + k) % n) for i in range(n)])  10.6 us
    ppermute x8, starting transfers between devices, swapped(): return lax.ppermute(x, axis, [(i, i ^ k) for i in range(n)])  8.08 us
    ppermute x8, waiting for transfers between devices, swapped(): return lax.ppermute(x, axis, [(i, i ^ k) for i in range(n)])  7.33 us
    pallas_call x1, Pallas kernels, body(): pl.pallas_call(functools.partial(pack_kernel, modes, groups), name='pack'...  1.45 us
  transfers between devices with their start and end apart: 16, of which 13 were waited for; matrix products, arithmetic and copies ran while one was open for 0% of the time, Pallas kernels for 8%

profile of v5, /device:TPU:0, one launch (start us, length us, event | category | flops | bytes accessed | tf_op | source)
XLA Modules:
  0.0 57.3 jit_solution(6931259627038302136)
XLA Ops:
  1.3 1.5 %pack.1 = (f32[56,256]{1,0:T(8,128)S(1)}, f32[1,256]{1,0:T(1,128)S(1)}, f32[1,256]{1,0:T(1,128)S(1)}, s32[2,4]{1,0:T(2,128)S(1)}) custom-call(s32[1]{0:T(128)S(6)} %copy.13.live_ref, s32[8,128]{1,0:T(8,128)} %bitcast.16, s32[8,128]{1,0:T(8,128)} %bitcast.17, s32[8,128]{1,0:T(8,128)} %bitcast.18, f32[8,128]{1,0:T(8,128)} %bitcast.19, f32[32,256]{1,0:T(8,128)} %refs_4_.1, ...), custom_call_target="tpu_custom_call" | custom-call | flops 268435456 | bytes 1048576 | tf_op jit(solution)/shard_map/pack/pallas_call | solution.py:612
  2.8 4.1 %collective-permute-start.2 = (f32[56,256]{1,0:T(8,128)S(1)}, f32[56,256]{1,0:T(8,128)S(1)}, u32[]{:S(2)}, u32[]{:S(2)}) collective-permute-start(f32[56,256]{1,0:T(8,128)S(1)} %get-tuple-element.17.own.pack), channel_id=1, source_target_pairs={{0,2},{1,3},{2,0},{3,1},{4,6},{5,7},{6,4},{7,5},{8,10},{9,11},{10,... | collective-permute-start | bytes 172040 | tf_op jit(solution)/shard_map/ppermute | solution.py:549
  6.9 1.4 %collective-permute-start.1 = (f32[56,256]{1,0:T(8,128)S(1)}, f32[56,256]{1,0:T(8,128)S(1)}, u32[]{:S(2)}, u32[]{:S(2)}) collective-permute-start(f32[56,256]{1,0:T(8,128)S(1)} %get-tuple-element.17.own.pack), channel_id=1, source_target_pairs={{0,3},{1,0},{2,1},{3,2},{4,7},{5,4},{6,5},{7,6},{8,11},{9,8},{10,9... | collective-permute-start | bytes 172040 | tf_op jit(solution)/shard_map/ppermute | solution.py:549
  8.2 0.7 %collective-permute-start = (f32[56,256]{1,0:T(8,128)S(1)}, f32[56,256]{1,0:T(8,128)S(1)}, u32[]{:S(2)}, u32[]{:S(2)}) collective-permute-start(f32[56,256]{1,0:T(8,128)S(1)} %get-tuple-element.17.own.pack), channel_id=1, source_target_pairs={{0,1},{1,2},{2,3},{3,0},{4,5},{5,6},{6,7},{7,4},{8,9},{9,10},{10,1... | collective-permute-start | bytes 172040 | tf_op jit(solution)/shard_map/ppermute | solution.py:549
  8.9 0.1 pad_add_fusion.sub_ref
  9.0 0.8 %collective-permute-done.2 = f32[56,256]{1,0:T(8,128)S(1)} collective-permute-done((f32[56,256]{1,0:T(8,128)S(1)}, f32[56,256]{1,0:T(8,128)S(1)}, u32[]{:S(2)}, u32[]{:S(2)}) %collective-permute-start.2) | collective-permute-done | bytes 57376 | tf_op jit(solution)/shard_map/ppermute | solution.py:549
  9.8 1.3 %collective-permute-done.1.nxt = f32[56,256]{1,0:T(8,128)S(1)} collective-permute-done((f32[56,256]{1,0:T(8,128)S(1)}, f32[56,256]{1,0:T(8,128)S(1)}, u32[]{:S(2)}, u32[]{:S(2)}) %collective-permute-start.1) | collective-permute-done | bytes 57376 | tf_op jit(solution)/shard_map/ppermute | solution.py:549
  11.1 3.1 %collective-permute-done.prev = f32[56,256]{1,0:T(8,128)S(1)} collective-permute-done((f32[56,256]{1,0:T(8,128)S(1)}, f32[56,256]{1,0:T(8,128)S(1)}, u32[]{:S(2)}, u32[]{:S(2)}) %collective-permute-start) | collective-permute-done | bytes 57376 | tf_op jit(solution)/shard_map/ppermute | solution.py:549
  14.2 0.3 collective-permute-start.4
  14.6 0.2 collective-permute-start.3
  14.8 0.9 %stiff.1._.refs_4_ = f32[32,256]{1,0:T(8,128)S(1)} custom-call(s32[2]{0:T(128)S(1)} %pad_add_fusion.sub_ref, s32[2,4]{1,0:T(2,128)S(1)} %get-tuple-element.16.cols_ref, f32[56,256]{1,0:T(8,128)S(1)} %collective-permute-done.prev, f32[56,256]{1,0:T(8,128)S(1)} %get-tuple-element.17.own.pack, f32[56,256]{1,0:T(8,128)S(1)} %collective-permute-done.1.nxt, ...), custom_call_target="tpu_custom_call" | custom-call | flops 536870912 | bytes 1048576 | tf_op jit(solution)/shard_map/stiff/pallas_call | solution.py:579
  15.7 3.4 %own_source.1 = (f32[4,256,256]{2,1,0:T(8,128)S(1)}, f32[6,32,8,128]{3,2,1,0:T(8,128)S(1)}) custom-call(f32[4,32,256]{2,1,0:T(8,128)S(1)} %pad_maximum_fusion.both, f32[32,256]{1,0:T(8,128)S(1)} %stiff.1._.refs_4_), custom_call_target="tpu_custom_call" | custom-call | flops 4294967296 | bytes 1048576 | tf_op jit(solution)/shard_map/own_source/pallas_call | solution.py:579
  19.1 1.9 %collective-permute-done.3.low = f32[4,32,256]{2,1,0:T(8,128)S(1)} collective-permute-done((f32[4,32,256]{2,1,0:T(8,128)S(1)}, f32[4,32,256]{2,1,0:T(8,128)S(1)}, u32[]{:S(2)}, u32[]{:S(2)}) %collective-permute-start.3) | collective-permute-done | bytes 131104 | tf_op jit(solution)/shard_map/ppermute | solution.py:549
  21.1 9.4 %fluid.1 = (f32[24,256]{1,0:T(8,128)S(1)}, f32[64,256]{1,0:T(8,128)S(1)}, f32[24,256]{1,0:T(8,128)S(1)}, f32[64,256]{1,0:T(8,128)S(1)}) custom-call(f32[4,32,256]{2,1,0:T(8,128)S(1)} %pad_maximum_fusion.both, f32[4,32,256]{2,1,0:T(8,128)S(1)} %collective-permute-done.3.low, f32[4,32,256]{2,1,0:T(8,128)S(1)} %collective-permute-done.4.high, ...), custom_call_target="tpu_custom_call" | custom-call | flops 4294967296 | bytes 1048576 | tf_op jit(solution)/shard_map/fluid/pallas_call | solution.py:579
  30.5 3.8 %collective-permute-start.7 = (f32[64,256]{1,0:T(8,128)S(1)}, f32[64,256]{1,0:T(8,128)S(1)}, u32[]{:S(2)}, u32[]{:S(2)}) collective-permute-start(f32[64,256]{1,0:T(8,128)S(1)} %get-tuple-element.25), channel_id=1, source_target_pairs={{0,3},{1,0},{2,1},{3,2},{4,7},{5,4},{6,5},{7,6},{8,11},{9,8},{10,9... | collective-permute-start | bytes 196616 | tf_op jit(solution)/shard_map/ppermute | solution.py:549
  34.3 4.7 %collective-permute-done.6.refs_2_ = f32[24,256]{1,0:T(8,128)S(1)} collective-permute-done((f32[24,256]{1,0:T(8,128)S(1)}, f32[24,256]{1,0:T(8,128)S(1)}, u32[]{:S(2)}, u32[]{:S(2)}) %collective-permute-start.6) | collective-permute-done | bytes 24608 | tf_op jit(solution)/shard_map/ppermute | solution.py:549
  39.1 1.3 %gram.1 = (f32[48,128]{1,0:T(8,128)S(1)}, f32[48,128]{1,0:T(8,128)S(1)}, f32[32,256]{1,0:T(8,128)S(1)}) custom-call(s32[2]{0:T(128)S(1)} %pad_add_fusion.sub_ref, s32[2,4]{1,0:T(2,128)S(1)} %get-tuple-element.16.cols_ref, f32[56,256]{1,0:T(8,128)S(1)} %collective-permute-done.prev, f32[56,256]{1,0:T(8,128)S(1)} %get-tuple-element.17.own.pack, ...), custom_call_target="tpu_custom_call" | custom-call | flops 536870912 | bytes 1048576 | tf_op jit(solution)/shard_map/gram/pallas_call | solution.py:579
  40.3 0.1 collective-permute-start.8
  40.4 1.2 %collective-permute-done.8 = f32[48,128]{1,0:T(8,128)S(1)} collective-permute-done((f32[48,128]{1,0:T(8,128)S(1)}, f32[48,128]{1,0:T(8,128)S(1)}, u32[]{:S(2)}, u32[]{:S(2)}) %collective-permute-start.8) | collective-permute-done | bytes 24608 | tf_op jit(solution)/shard_map/ppermute | solution.py:554
  41.6 1.2 %collective-permute-start.11 = (f32[48,128]{1,0:T(8,128)S(1)}, f32[48,128]{1,0:T(8,128)S(1)}, u32[]{:S(2)}, u32[]{:S(2)}) collective-permute-start(f32[48,128]{1,0:T(8,128)S(1)} %add.28), channel_id=1, source_target_pairs={{0,24},{4,28},{8,16},{12,20},{16,8},{20,12},{24,0},{28,4},{1,25},{... | collective-permute-start | bytes 73736 | tf_op jit(solution)/shard_map/ppermute | solution.py:554
  42.8 1.4 %collective-permute-start.10 = (f32[48,128]{1,0:T(8,128)S(1)}, f32[48,128]{1,0:T(8,128)S(1)}, u32[]{:S(2)}, u32[]{:S(2)}) collective-permute-start(f32[48,128]{1,0:T(8,128)S(1)} %add.28), channel_id=1, source_target_pairs={{0,16},{4,20},{8,24},{12,28},{16,0},{20,4},{24,8},{28,12},{1,17},{... | collective-permute-start | bytes 73736 | tf_op jit(solution)/shard_map/ppermute | solution.py:554
  44.2 0.9 %collective-permute-start.9 = (f32[48,128]{1,0:T(8,128)S(1)}, f32[48,128]{1,0:T(8,128)S(1)}, u32[]{:S(2)}, u32[]{:S(2)}) collective-permute-start(f32[48,128]{1,0:T(8,128)S(1)} %add.28), channel_id=1, source_target_pairs={{0,8},{4,12},{8,0},{12,4},{16,24},{20,28},{24,16},{28,20},{1,9},{5... | collective-permute-start | bytes 73736 | tf_op jit(solution)/shard_map/ppermute | solution.py:554
  45.1 1.2 %collective-permute-done.11 = f32[48,128]{1,0:T(8,128)S(1)} collective-permute-done((f32[48,128]{1,0:T(8,128)S(1)}, f32[48,128]{1,0:T(8,128)S(1)}, u32[]{:S(2)}, u32[]{:S(2)}) %collective-permute-start.11) | collective-permute-done | bytes 24608 | tf_op jit(solution)/shard_map/ppermute | solution.py:554
  46.3 0.3 collective-permute-done.10
  46.6 1.4 %collective-permute-done.9 = f32[48,128]{1,0:T(8,128)S(1)} collective-permute-done((f32[48,128]{1,0:T(8,128)S(1)}, f32[48,128]{1,0:T(8,128)S(1)}, u32[]{:S(2)}, u32[]{:S(2)}) %collective-permute-start.9) | collective-permute-done | bytes 24608 | tf_op jit(solution)/shard_map/ppermute | solution.py:554
  48.1 1.4 %collective-permute-start.14 = (f32[48,128]{1,0:T(8,128)S(1)}, f32[48,128]{1,0:T(8,128)S(1)}, u32[]{:S(2)}, u32[]{:S(2)}) collective-permute-start(f32[48,128]{1,0:T(8,128)S(1)} %add_add_fusion.1), channel_id=1, source_target_pairs={{0,3},{1,2},{2,1},{3,0},{4,7},{5,6},{6,5},{7,4},{8,11},{9,10},{10,... | collective-permute-start | bytes 73736 | tf_op jit(solution)/shard_map/ppermute | solution.py:554
  49.5 3.1 %collective-permute-start.12 = (f32[48,128]{1,0:T(8,128)S(1)}, f32[48,128]{1,0:T(8,128)S(1)}, u32[]{:S(2)}, u32[]{:S(2)}) collective-permute-start(f32[48,128]{1,0:T(8,128)S(1)} %add_add_fusion.1), channel_id=1, source_target_pairs={{0,1},{1,0},{2,3},{3,2},{4,5},{5,4},{6,7},{7,6},{8,9},{9,8},{10,11... | collective-permute-start | bytes 73736 | tf_op jit(solution)/shard_map/ppermute | solution.py:554
  52.5 1.2 %collective-permute-done.14 = f32[48,128]{1,0:T(8,128)S(1)} collective-permute-done((f32[48,128]{1,0:T(8,128)S(1)}, f32[48,128]{1,0:T(8,128)S(1)}, u32[]{:S(2)}, u32[]{:S(2)}) %collective-permute-start.14) | collective-permute-done | bytes 24608 | tf_op jit(solution)/shard_map/ppermute | solution.py:554
  53.7 0.5 collective-permute-done.13
  54.3 0.2 collective-permute-done.12
  54.6 1.2 %collective-permute-done.15.other = f32[48,128]{1,0:T(8,128)S(1)} collective-permute-done((f32[48,128]{1,0:T(8,128)S(1)}, f32[48,128]{1,0:T(8,128)S(1)}, u32[]{:S(2)}, u32[]{:S(2)}) %collective-permute-start.15) | collective-permute-done | bytes 24608 | tf_op jit(solution)/shard_map/ppermute | solution.py:554
  55.8 1.5 %final.1 = (f32[32,256]{1,0:T(8,128)}, f32[64,64]{1,0:T(8,128)}, f32[64,64]{1,0:T(8,128)}) custom-call(s32[2]{0:T(128)S(1)} %pad_add_fusion.sub_ref, f32[48,128]{1,0:T(8,128)S(1)} %add_add_fusion.mine, f32[48,128]{1,0:T(8,128)S(1)} %collective-permute-done.15.other, f32[32,256]{1,0:T(8,128)S(1)} %stiff.1._.refs_4_, f32[32,256]{1,0:T(8,128)S(1)} %get-tuple-element.28.mass), custom_call_target="tpu_custom_call" | custom-call | flops 1048576 | bytes 1048576 | tf_op jit(solution)/shard_map/final/pallas_call | solution.py:579
  (25 shorter events, 0.2 us)
Async XLA Ops:
  2.7 12.1 %copy-start = (f32[2,4,128,128]{3,2,1,0:T(8,128)S(1)}, f32[2,4,128,128]{3,2,1,0:T(8,128)}, u32[]{:S(2)}) copy-start(f32[2,4,128,128]{3,2,1,0:T(8,128)} %refs_6_.1) | copy-start | bytes 1572868
  2.8 7.0 %collective-permute-start.2 = (f32[56,256]{1,0:T(8,128)S(1)}, f32[56,256]{1,0:T(8,128)S(1)}, u32[]{:S(2)}, u32[]{:S(2)}) collective-permute-start(f32[56,256]{1,0:T(8,128)S(1)} %get-tuple-element.17.own.pack), channel_id=1, source_target_pairs={{0,2},{1,3},{2,0},{3,1},{4,6},{5,7},{6,4},{7,5},{8,10},{9,11},{10,... | collective-permute-start | bytes 172040 | tf_op jit(solution)/shard_map/ppermute | solution.py:549
  6.9 4.2 %collective-permute-start.1 = (f32[56,256]{1,0:T(8,128)S(1)}, f32[56,256]{1,0:T(8,128)S(1)}, u32[]{:S(2)}, u32[]{:S(2)}) collective-permute-start(f32[56,256]{1,0:T(8,128)S(1)} %get-tuple-element.17.own.pack), channel_id=1, source_target_pairs={{0,3},{1,0},{2,1},{3,2},{4,7},{5,4},{6,5},{7,6},{8,11},{9,8},{10,9... | collective-permute-start | bytes 172040 | tf_op jit(solution)/shard_map/ppermute | solution.py:549
  8.2 6.0 %collective-permute-start = (f32[56,256]{1,0:T(8,128)S(1)}, f32[56,256]{1,0:T(8,128)S(1)}, u32[]{:S(2)}, u32[]{:S(2)}) collective-permute-start(f32[56,256]{1,0:T(8,128)S(1)} %get-tuple-element.17.own.pack), channel_id=1, source_target_pairs={{0,1},{1,2},{2,3},{3,0},{4,5},{5,6},{6,7},{7,4},{8,9},{9,10},{10,1... | collective-permute-start | bytes 172040 | tf_op jit(solution)/shard_map/ppermute | solution.py:549
  14.2 4.9 %collective-permute-start.4 = (f32[4,32,256]{2,1,0:T(8,128)S(1)}, f32[4,32,256]{2,1,0:T(8,128)S(1)}, u32[]{:S(2)}, u32[]{:S(2)}) collective-permute-start(f32[4,32,256]{2,1,0:T(8,128)S(1)} %pad_maximum_fusion.both), channel_id=1, source_target_pairs={{0,28},{4,0},{8,4},{12,8},{16,12},{20,16},{24,20},{28,24},{1,29},{... | collective-permute-start | bytes 393224 | tf_op jit(solution)/shard_map/ppermute | solution.py:549
  14.6 6.5 %collective-permute-start.3 = (f32[4,32,256]{2,1,0:T(8,128)S(1)}, f32[4,32,256]{2,1,0:T(8,128)S(1)}, u32[]{:S(2)}, u32[]{:S(2)}) collective-permute-start(f32[4,32,256]{2,1,0:T(8,128)S(1)} %pad_maximum_fusion.both), channel_id=1, source_target_pairs={{0,4},{4,8},{8,12},{12,16},{16,20},{20,24},{24,28},{28,0},{1,5},{5... | collective-permute-start | bytes 393224 | tf_op jit(solution)/shard_map/ppermute | solution.py:549
  30.5 8.6 %collective-permute-start.5 = (f32[64,256]{1,0:T(8,128)S(1)}, f32[64,256]{1,0:T(8,128)S(1)}, u32[]{:S(2)}, u32[]{:S(2)}) collective-permute-start(f32[64,256]{1,0:T(8,128)S(1)} %get-tuple-element.23), channel_id=1, source_target_pairs={{0,1},{1,2},{2,3},{3,0},{4,5},{5,6},{6,7},{7,4},{8,9},{9,10},{10,1... | collective-permute-start | bytes 196616 | tf_op jit(solution)/shard_map/ppermute | solution.py:549
  30.5 8.5 %collective-permute-start.7 = (f32[64,256]{1,0:T(8,128)S(1)}, f32[64,256]{1,0:T(8,128)S(1)}, u32[]{:S(2)}, u32[]{:S(2)}) collective-permute-start(f32[64,256]{1,0:T(8,128)S(1)} %get-tuple-element.25), channel_id=1, source_target_pairs={{0,3},{1,0},{2,1},{3,2},{4,7},{5,4},{6,5},{7,6},{8,11},{9,8},{10,9... | collective-permute-start | bytes 196616 | tf_op jit(solution)/shard_map/ppermute | solution.py:549
  34.3 4.7 %collective-permute-start.6 = (f32[24,256]{1,0:T(8,128)S(1)}, f32[24,256]{1,0:T(8,128)S(1)}, u32[]{:S(2)}, u32[]{:S(2)}) collective-permute-start(f32[24,256]{1,0:T(8,128)S(1)} %get-tuple-element.24), channel_id=1, source_target_pairs={{0,2},{1,3},{2,0},{3,1},{4,6},{5,7},{6,4},{7,5},{8,10},{9,11},{10,... | collective-permute-start | bytes 73736 | tf_op jit(solution)/shard_map/ppermute | solution.py:549
  40.3 1.3 %collective-permute-start.8 = (f32[48,128]{1,0:T(8,128)S(1)}, f32[48,128]{1,0:T(8,128)S(1)}, u32[]{:S(2)}, u32[]{:S(2)}) collective-permute-start(f32[48,128]{1,0:T(8,128)S(1)} %get-tuple-element.27), channel_id=1, source_target_pairs={{0,4},{4,0},{8,12},{12,8},{16,20},{20,16},{24,28},{28,24},{1,5},{5... | collective-permute-start | bytes 73736 | tf_op jit(solution)/shard_map/ppermute | solution.py:554
  41.6 4.7 %collective-permute-start.11 = (f32[48,128]{1,0:T(8,128)S(1)}, f32[48,128]{1,0:T(8,128)S(1)}, u32[]{:S(2)}, u32[]{:S(2)}) collective-permute-start(f32[48,128]{1,0:T(8,128)S(1)} %add.28), channel_id=1, source_target_pairs={{0,24},{4,28},{8,16},{12,20},{16,8},{20,12},{24,0},{28,4},{1,25},{... | collective-permute-start | bytes 73736 | tf_op jit(solution)/shard_map/ppermute | solution.py:554
  42.8 3.8 %collective-permute-start.10 = (f32[48,128]{1,0:T(8,128)S(1)}, f32[48,128]{1,0:T(8,128)S(1)}, u32[]{:S(2)}, u32[]{:S(2)}) collective-permute-start(f32[48,128]{1,0:T(8,128)S(1)} %add.28), channel_id=1, source_target_pairs={{0,16},{4,20},{8,24},{12,28},{16,0},{20,4},{24,8},{28,12},{1,17},{... | collective-permute-start | bytes 73736 | tf_op jit(solution)/shard_map/ppermute | solution.py:554
  44.2 3.8 %collective-permute-start.9 = (f32[48,128]{1,0:T(8,128)S(1)}, f32[48,128]{1,0:T(8,128)S(1)}, u32[]{:S(2)}, u32[]{:S(2)}) collective-permute-start(f32[48,128]{1,0:T(8,128)S(1)} %add.28), channel_id=1, source_target_pairs={{0,8},{4,12},{8,0},{12,4},{16,24},{20,28},{24,16},{28,20},{1,9},{5... | collective-permute-start | bytes 73736 | tf_op jit(solution)/shard_map/ppermute | solution.py:554
  48.1 5.7 %collective-permute-start.14 = (f32[48,128]{1,0:T(8,128)S(1)}, f32[48,128]{1,0:T(8,128)S(1)}, u32[]{:S(2)}, u32[]{:S(2)}) collective-permute-start(f32[48,128]{1,0:T(8,128)S(1)} %add_add_fusion.1), channel_id=1, source_target_pairs={{0,3},{1,2},{2,1},{3,0},{4,7},{5,6},{6,5},{7,4},{8,11},{9,10},{10,... | collective-permute-start | bytes 73736 | tf_op jit(solution)/shard_map/ppermute | solution.py:554
  49.5 4.8 %collective-permute-start.13 = (f32[48,128]{1,0:T(8,128)S(1)}, f32[48,128]{1,0:T(8,128)S(1)}, u32[]{:S(2)}, u32[]{:S(2)}) collective-permute-start(f32[48,128]{1,0:T(8,128)S(1)} %add_add_fusion.1), channel_id=1, source_target_pairs={{0,2},{1,3},{2,0},{3,1},{4,6},{5,7},{6,4},{7,5},{8,10},{9,11},{10,... | collective-permute-start | bytes 73736 | tf_op jit(solution)/shard_map/ppermute | solution.py:554
  49.5 5.1 %collective-permute-start.12 = (f32[48,128]{1,0:T(8,128)S(1)}, f32[48,128]{1,0:T(8,128)S(1)}, u32[]{:S(2)}, u32[]{:S(2)}) collective-permute-start(f32[48,128]{1,0:T(8,128)S(1)} %add_add_fusion.1), channel_id=1, source_target_pairs={{0,1},{1,0},{2,3},{3,2},{4,5},{5,4},{6,7},{7,6},{8,9},{9,8},{10,11... | collective-permute-start | bytes 73736 | tf_op jit(solution)/shard_map/ppermute | solution.py:554
  54.5 1.3 %collective-permute-start.15 = (f32[48,128]{1,0:T(8,128)S(1)}, f32[48,128]{1,0:T(8,128)S(1)}, u32[]{:S(2)}, u32[]{:S(2)}) collective-permute-start(f32[48,128]{1,0:T(8,128)S(1)} %add_add_fusion.mine), channel_id=1, source_target_pairs={{0,4},{4,0},{8,12},{12,8},{16,20},{20,16},{24,28},{28,24},{1,5},{5... | collective-permute-start | bytes 73736 | tf_op jit(solution)/shard_map/ppermute | solution.py:554

commit v6 on v5

--- a/solution.py
+++ b/solution.py
@@ -205,14 +205,14 @@
     )
     wide = (pair - step).astype(F32).astype(BF)
     zero = jnp.zeros((tall, width), BF)
-    first, then = pl.ds(at, width), pl.ds(at + width, width)
+    lanes = pl.ds(at, width)
+    half = a_count * CY // 2 * modes
     for r in range(0, a_count * CY // 2, times):
         mask = wide == jnp.asarray(r, BF)
-        lhs[r * modes : r * modes + tall, first] = jnp.where(mask, hi, zero)
-        lhs[r * modes : r * modes + tall, then] = jnp.where(mask, lo, zero)
-    hot = onehot((b & 1) * CZ + c, 2 * CZ)
-    rhs[:, first] = hot
-    rhs[:, then] = hot
+        row = r * modes
+        lhs[row : row + tall, lanes] = jnp.where(mask, hi, zero)
+        lhs[half + row : half + row + tall, lanes] = jnp.where(mask, lo, zero)
+    rhs[:, lanes] = onehot((b & 1) * CZ + c, 2 * CZ)
 
 
 def scatter(both, modes, capacity, owner, a_first, a_count, out, lhs, rhs, width=None):
@@ -225,12 +225,17 @@
     wide = some.width
 
     def first(k):
-        at = 2 * k * wide
+        at = k * wide
         at = at if isinstance(k, int) else pl.multiple_of(at, 128)
         fill(lists_of(k), owner, 0, a_first, a_count, lhs, rhs, at)
 
+    def product(lanes):
+        got = dot_t(lhs[:, 0:lanes], rhs[:, 0:lanes])
+        half = got.shape[0] // 2
+        return got[:half] + got[half:]
+
     each(groups, first)
-    out[...] = dot_t(lhs[...], rhs[...])
+    out[...] = product(wide * groups)
     jobs = []
     if some.chunks == 1:
         return jobs
@@ -244,7 +249,7 @@
 
         def one(chunk, carry, lists=lists):
             fill(lists, owner, chunk, a_first, a_count, lhs, rhs, 0)
-            out[...] += dot_t(lhs[:, 0 : 2 * wide], rhs[:, 0 : 2 * wide])
+            out[...] += product(wide)
             return carry
 
         jobs.append((last, one))
@@ -326,6 +331,7 @@
     )
     local = both.shape[2]
     count = groups * CY
+    width = min(local, capacity)
     jobs = []
     for side, there in enumerate((low, high)):
         a_first = CX - HALO if side == 0 else 0
@@ -369,27 +375,34 @@
             press[owner, at : at + 2 * modes, lanes : lanes + CZ] = hi
             press[owner, at : at + 2 * modes, 2 * CZ + lanes : 3 * CZ + lanes] = lo
 
-    def collect(k, owner, chunk):
-        lists = Lists(both.at[k], modes, capacity)
-        a, b, c, node, weight = lists.load(owner, chunk)
+    def joined(owner, chunk, devices):
+        loads = [Lists(both.at[k], modes, capacity).load(owner, chunk) for k in devices]
+        return [jnp.concatenate(x, axis=1) for x in zip(*loads)]
+
+    def pick(owner, chunk, devices):
+        a, b, c, node, weight = joined(owner, chunk, devices)
         hot = onehot((b & 1) * CZ + c, 2 * CZ)
         got = dot(press[owner], jnp.concatenate([hot, hot], axis=0))
-        pair = jnp.broadcast_to(
-            lax.shift_right_logical(b, 1) * CX + a, (modes, lists.width)
-        )
-        picked = jnp.zeros((modes, lists.width), F32)
+        pair = jnp.broadcast_to(lax.shift_right_logical(b, 1) * CX + a, (modes, a.shape[1]))
+        picked = jnp.zeros(pair.shape, F32)
         for r in range(CX * CY // 2):
             picked = jnp.where(pair == r, got[r * modes : (r + 1) * modes], picked)
-        hi, lo = split(picked * weight)
+        return picked * weight, node
+
+    def to_nodes(picked, node):
+        hi, lo = split(picked)
         sums = dot_t(jnp.concatenate([hi, lo], axis=0), onehot(node, local))
         return sums[:modes] + sums[modes:]
 
+    def collect(k, owner, chunk):
+        return to_nodes(*pick(owner, chunk, [k]))
+
     if groups <= 4:
+        every = [pick(o, 0, range(groups)) for o in range(groups)]
         for k in range(groups):
-            total = collect(k, 0, 0)
-            for o in range(1, groups):
-                total = total + collect(k, o, 0)
-            force[k] = total
+            lanes = slice(k * width, (k + 1) * width)
+            parts = [[x[:, lanes] for x in one] for one in every]
+            force[k] = to_nodes(*[jnp.concatenate(x, axis=1) for x in zip(*parts)])
     else:
 
         def per_device(k):
@@ -666,8 +679,8 @@
         return jax.ShapeDtypeStruct(shape, F32)
 
     def operands(rows, chunk):
-        deep = 2 * min(chunk, width) * groups
-        return sets * [pltpu.VMEM((rows, deep), BF), pltpu.VMEM((2 * CZ, deep), BF)]
+        deep = min(chunk, width) * groups
+        return sets * [pltpu.VMEM((2 * rows, deep), BF), pltpu.VMEM((2 * CZ, deep), BF)]
 
     rows = CX * CY // 2 * mine
     edge_rows = HALO * CY // 2 * mine

time: 57.1 us -> 53.7 us (0.940); the launches traced: 57.3 us -> 53.3 us
  Pallas kernels: 17.9 us -> 15 us
  waiting for transfers between devices: 19.2 us -> 18.1 us
    pallas_call x5, Pallas kernels: 16.5 us -> 13.6 us  [call(): pl.pallas_call(kernel, name=name, out_shape=out_shape, in_specs=[smem()]...]
    ppermute x8, waiting for transfers between devices: 7.33 us -> 6.19 us  [swapped(): return lax.ppermute(x, axis, [(i, i ^ k) for i in range(n)])]
  transfers between devices with their start and end apart: 16 -> 16, of which waited for: 13 -> 12; matrix products, arithmetic and copies ran while one was open for 0% -> 0% of each run, Pallas kernels for 8% -> 8%
where the time goes in v6:
time: 53.7 us; the launch traced here: 53.3 us
  starting transfers between devices  18.7 us (35%)
  waiting for transfers between devices  18.1 us (34%)
  Pallas kernels  15 us (28%)
  between operations  1.39 us (3%)
    pallas_call x5, Pallas kernels, call(): pl.pallas_call(kernel, name=name, out_shape=out_shape, in_specs=[smem()]...  13.6 us
    ppermute x8, waiting for transfers between devices, shifted(): return lax.ppermute(x, axis, [(i, (i + k) % n) for i in range(n)])  11.9 us
    ppermute x8, starting transfers between devices, shifted(): return lax.ppermute(x, axis, [(i, (i + k) % n) for i in range(n)])  10.6 us
    ppermute x8, starting transfers between devices, swapped(): return lax.ppermute(x, axis, [(i, i ^ k) for i in range(n)])  8.08 us
    ppermute x8, waiting for transfers between devices, swapped(): return lax.ppermute(x, axis, [(i, i ^ k) for i in range(n)])  6.19 us
    pallas_call x1, Pallas kernels, body(): pl.pallas_call(functools.partial(pack_kernel, modes, groups), name='pack'...  1.45 us
  transfers between devices with their start and end apart: 16, of which 12 were waited for; matrix products, arithmetic and copies ran while one was open for 0% of the time, Pallas kernels for 8%

profile of v6, /device:TPU:0, one launch (start us, length us, event | category | flops | bytes accessed | tf_op | source)
XLA Modules:
  0.0 53.3 jit_solution(5107683110466862874)
XLA Ops:
  1.3 1.5 %pack.1 = (f32[56,256]{1,0:T(8,128)S(1)}, f32[1,256]{1,0:T(1,128)S(1)}, f32[1,256]{1,0:T(1,128)S(1)}, s32[2,4]{1,0:T(2,128)S(1)}) custom-call(s32[1]{0:T(128)S(6)} %copy.13.live_ref, s32[8,128]{1,0:T(8,128)} %bitcast.16, s32[8,128]{1,0:T(8,128)} %bitcast.17, s32[8,128]{1,0:T(8,128)} %bitcast.18, f32[8,128]{1,0:T(8,128)} %bitcast.19, f32[32,256]{1,0:T(8,128)} %refs_4_.1, ...), custom_call_target="tpu_custom_call" | custom-call | flops 268435456 | bytes 1048576 | tf_op jit(solution)/shard_map/pack/pallas_call | solution.py:625
  2.8 4.1 %collective-permute-start.2 = (f32[56,256]{1,0:T(8,128)S(1)}, f32[56,256]{1,0:T(8,128)S(1)}, u32[]{:S(2)}, u32[]{:S(2)}) collective-permute-start(f32[56,256]{1,0:T(8,128)S(1)} %get-tuple-element.17.own.pack), channel_id=1, source_target_pairs={{0,2},{1,3},{2,0},{3,1},{4,6},{5,7},{6,4},{7,5},{8,10},{9,11},{10,... | collective-permute-start | bytes 172040 | tf_op jit(solution)/shard_map/ppermute | solution.py:562
  6.9 1.4 %collective-permute-start.1 = (f32[56,256]{1,0:T(8,128)S(1)}, f32[56,256]{1,0:T(8,128)S(1)}, u32[]{:S(2)}, u32[]{:S(2)}) collective-permute-start(f32[56,256]{1,0:T(8,128)S(1)} %get-tuple-element.17.own.pack), channel_id=1, source_target_pairs={{0,3},{1,0},{2,1},{3,2},{4,7},{5,4},{6,5},{7,6},{8,11},{9,8},{10,9... | collective-permute-start | bytes 172040 | tf_op jit(solution)/shard_map/ppermute | solution.py:562
  8.2 0.7 %collective-permute-start = (f32[56,256]{1,0:T(8,128)S(1)}, f32[56,256]{1,0:T(8,128)S(1)}, u32[]{:S(2)}, u32[]{:S(2)}) collective-permute-start(f32[56,256]{1,0:T(8,128)S(1)} %get-tuple-element.17.own.pack), channel_id=1, source_target_pairs={{0,1},{1,2},{2,3},{3,0},{4,5},{5,6},{6,7},{7,4},{8,9},{9,10},{10,1... | collective-permute-start | bytes 172040 | tf_op jit(solution)/shard_map/ppermute | solution.py:562
  8.9 0.1 pad_add_fusion.sub_ref
  9.0 0.8 %collective-permute-done.2 = f32[56,256]{1,0:T(8,128)S(1)} collective-permute-done((f32[56,256]{1,0:T(8,128)S(1)}, f32[56,256]{1,0:T(8,128)S(1)}, u32[]{:S(2)}, u32[]{:S(2)}) %collective-permute-start.2) | collective-permute-done | bytes 57376 | tf_op jit(solution)/shard_map/ppermute | solution.py:562
  9.8 1.3 %collective-permute-done.1.nxt = f32[56,256]{1,0:T(8,128)S(1)} collective-permute-done((f32[56,256]{1,0:T(8,128)S(1)}, f32[56,256]{1,0:T(8,128)S(1)}, u32[]{:S(2)}, u32[]{:S(2)}) %collective-permute-start.1) | collective-permute-done | bytes 57376 | tf_op jit(solution)/shard_map/ppermute | solution.py:562
  11.1 3.1 %collective-permute-done.prev = f32[56,256]{1,0:T(8,128)S(1)} collective-permute-done((f32[56,256]{1,0:T(8,128)S(1)}, f32[56,256]{1,0:T(8,128)S(1)}, u32[]{:S(2)}, u32[]{:S(2)}) %collective-permute-start) | collective-permute-done | bytes 57376 | tf_op jit(solution)/shard_map/ppermute | solution.py:562
  14.2 0.3 collective-permute-start.4
  14.6 0.2 collective-permute-start.3
  14.8 0.9 %stiff.1._.refs_4_ = f32[32,256]{1,0:T(8,128)S(1)} custom-call(s32[2]{0:T(128)S(1)} %pad_add_fusion.sub_ref, s32[2,4]{1,0:T(2,128)S(1)} %get-tuple-element.16.cols_ref, f32[56,256]{1,0:T(8,128)S(1)} %collective-permute-done.prev, f32[56,256]{1,0:T(8,128)S(1)} %get-tuple-element.17.own.pack, f32[56,256]{1,0:T(8,128)S(1)} %collective-permute-done.1.nxt, ...), custom_call_target="tpu_custom_call" | custom-call | flops 536870912 | bytes 1048576 | tf_op jit(solution)/shard_map/stiff/pallas_call | solution.py:592
  15.7 3.4 %own_source.1 = (f32[4,256,256]{2,1,0:T(8,128)S(1)}, f32[6,32,8,128]{3,2,1,0:T(8,128)S(1)}) custom-call(f32[4,32,256]{2,1,0:T(8,128)S(1)} %pad_maximum_fusion.both, f32[32,256]{1,0:T(8,128)S(1)} %stiff.1._.refs_4_), custom_call_target="tpu_custom_call" | custom-call | flops 4294967296 | bytes 1048576 | tf_op jit(solution)/shard_map/own_source/pallas_call | solution.py:592
  19.1 2.0 %collective-permute-done.3.low = f32[4,32,256]{2,1,0:T(8,128)S(1)} collective-permute-done((f32[4,32,256]{2,1,0:T(8,128)S(1)}, f32[4,32,256]{2,1,0:T(8,128)S(1)}, u32[]{:S(2)}, u32[]{:S(2)}) %collective-permute-start.3) | collective-permute-done | bytes 131104 | tf_op jit(solution)/shard_map/ppermute | solution.py:562
  21.1 6.5 %fluid.1 = (f32[24,256]{1,0:T(8,128)S(1)}, f32[64,256]{1,0:T(8,128)S(1)}, f32[24,256]{1,0:T(8,128)S(1)}, f32[64,256]{1,0:T(8,128)S(1)}) custom-call(f32[4,32,256]{2,1,0:T(8,128)S(1)} %pad_maximum_fusion.both, f32[4,32,256]{2,1,0:T(8,128)S(1)} %collective-permute-done.3.low, f32[4,32,256]{2,1,0:T(8,128)S(1)} %collective-permute-done.4.high, ...), custom_call_target="tpu_custom_call" | custom-call | flops 4294967296 | bytes 1048576 | tf_op jit(solution)/shard_map/fluid/pallas_call | solution.py:592
  27.6 3.8 %collective-permute-start.7 = (f32[64,256]{1,0:T(8,128)S(1)}, f32[64,256]{1,0:T(8,128)S(1)}, u32[]{:S(2)}, u32[]{:S(2)}) collective-permute-start(f32[64,256]{1,0:T(8,128)S(1)} %get-tuple-element.25), channel_id=1, source_target_pairs={{0,3},{1,0},{2,1},{3,2},{4,7},{5,4},{6,5},{7,6},{8,11},{9,8},{10,9... | collective-permute-start | bytes 196616 | tf_op jit(solution)/shard_map/ppermute | solution.py:562
  31.5 4.7 %collective-permute-done.6.refs_2_ = f32[24,256]{1,0:T(8,128)S(1)} collective-permute-done((f32[24,256]{1,0:T(8,128)S(1)}, f32[24,256]{1,0:T(8,128)S(1)}, u32[]{:S(2)}, u32[]{:S(2)}) %collective-permute-start.6) | collective-permute-done | bytes 24608 | tf_op jit(solution)/shard_map/ppermute | solution.py:562
  36.2 1.3 %gram.1 = (f32[48,128]{1,0:T(8,128)S(1)}, f32[48,128]{1,0:T(8,128)S(1)}, f32[32,256]{1,0:T(8,128)S(1)}) custom-call(s32[2]{0:T(128)S(1)} %pad_add_fusion.sub_ref, s32[2,4]{1,0:T(2,128)S(1)} %get-tuple-element.16.cols_ref, f32[56,256]{1,0:T(8,128)S(1)} %collective-permute-done.prev, f32[56,256]{1,0:T(8,128)S(1)} %get-tuple-element.17.own.pack, ...), custom_call_target="tpu_custom_call" | custom-call | flops 536870912 | bytes 1048576 | tf_op jit(solution)/shard_map/gram/pallas_call | solution.py:592
  37.5 0.1 collective-permute-start.8
  37.5 1.2 %collective-permute-done.8 = f32[48,128]{1,0:T(8,128)S(1)} collective-permute-done((f32[48,128]{1,0:T(8,128)S(1)}, f32[48,128]{1,0:T(8,128)S(1)}, u32[]{:S(2)}, u32[]{:S(2)}) %collective-permute-start.8) | collective-permute-done | bytes 24608 | tf_op jit(solution)/shard_map/ppermute | solution.py:567
  38.7 0.7 %collective-permute-start.11 = (f32[48,128]{1,0:T(8,128)S(1)}, f32[48,128]{1,0:T(8,128)S(1)}, u32[]{:S(2)}, u32[]{:S(2)}) collective-permute-start(f32[48,128]{1,0:T(8,128)S(1)} %add.28), channel_id=1, source_target_pairs={{0,24},{4,28},{8,16},{12,20},{16,8},{20,12},{24,0},{28,4},{1,25},{... | collective-permute-start | bytes 73736 | tf_op jit(solution)/shard_map/ppermute | solution.py:567
  39.4 0.4 collective-permute-start.10
  39.8 2.4 %collective-permute-start.9 = (f32[48,128]{1,0:T(8,128)S(1)}, f32[48,128]{1,0:T(8,128)S(1)}, u32[]{:S(2)}, u32[]{:S(2)}) collective-permute-start(f32[48,128]{1,0:T(8,128)S(1)} %add.28), channel_id=1, source_target_pairs={{0,8},{4,12},{8,0},{12,4},{16,24},{20,28},{24,16},{28,20},{1,9},{5... | collective-permute-start | bytes 73736 | tf_op jit(solution)/shard_map/ppermute | solution.py:567
  42.2 1.5 %collective-permute-done.11 = f32[48,128]{1,0:T(8,128)S(1)} collective-permute-done((f32[48,128]{1,0:T(8,128)S(1)}, f32[48,128]{1,0:T(8,128)S(1)}, u32[]{:S(2)}, u32[]{:S(2)}) %collective-permute-start.11) | collective-permute-done | bytes 24608 | tf_op jit(solution)/shard_map/ppermute | solution.py:567
  43.7 0.3 collective-permute-done.9
  44.0 1.4 %collective-permute-start.14 = (f32[48,128]{1,0:T(8,128)S(1)}, f32[48,128]{1,0:T(8,128)S(1)}, u32[]{:S(2)}, u32[]{:S(2)}) collective-permute-start(f32[48,128]{1,0:T(8,128)S(1)} %add_add_fusion.1), channel_id=1, source_target_pairs={{0,3},{1,2},{2,1},{3,0},{4,7},{5,6},{6,5},{7,4},{8,11},{9,10},{10,... | collective-permute-start | bytes 73736 | tf_op jit(solution)/shard_map/ppermute | solution.py:567
  45.4 3.1 %collective-permute-start.12 = (f32[48,128]{1,0:T(8,128)S(1)}, f32[48,128]{1,0:T(8,128)S(1)}, u32[]{:S(2)}, u32[]{:S(2)}) collective-permute-start(f32[48,128]{1,0:T(8,128)S(1)} %add_add_fusion.1), channel_id=1, source_target_pairs={{0,1},{1,0},{2,3},{3,2},{4,5},{5,4},{6,7},{7,6},{8,9},{9,8},{10,11... | collective-permute-start | bytes 73736 | tf_op jit(solution)/shard_map/ppermute | solution.py:567
  48.5 1.2 %collective-permute-done.14 = f32[48,128]{1,0:T(8,128)S(1)} collective-permute-done((f32[48,128]{1,0:T(8,128)S(1)}, f32[48,128]{1,0:T(8,128)S(1)}, u32[]{:S(2)}, u32[]{:S(2)}) %collective-permute-start.14) | collective-permute-done | bytes 24608 | tf_op jit(solution)/shard_map/ppermute | solution.py:567
  49.7 0.5 %collective-permute-done.13 = f32[48,128]{1,0:T(8,128)S(1)} collective-permute-done((f32[48,128]{1,0:T(8,128)S(1)}, f32[48,128]{1,0:T(8,128)S(1)}, u32[]{:S(2)}, u32[]{:S(2)}) %collective-permute-start.13) | collective-permute-done | bytes 24608 | tf_op jit(solution)/shard_map/ppermute | solution.py:567
  50.3 0.2 collective-permute-done.12
  50.5 0.1 collective-permute-start.15
  50.6 1.2 %collective-permute-done.15.other = f32[48,128]{1,0:T(8,128)S(1)} collective-permute-done((f32[48,128]{1,0:T(8,128)S(1)}, f32[48,128]{1,0:T(8,128)S(1)}, u32[]{:S(2)}, u32[]{:S(2)}) %collective-permute-start.15) | collective-permute-done | bytes 24608 | tf_op jit(solution)/shard_map/ppermute | solution.py:567
  51.8 1.5 %final.1 = (f32[32,256]{1,0:T(8,128)}, f32[64,64]{1,0:T(8,128)}, f32[64,64]{1,0:T(8,128)}) custom-call(s32[2]{0:T(128)S(1)} %pad_add_fusion.sub_ref, f32[48,128]{1,0:T(8,128)S(1)} %add_add_fusion.mine, f32[48,128]{1,0:T(8,128)S(1)} %collective-permute-done.15.other, f32[32,256]{1,0:T(8,128)S(1)} %stiff.1._.refs_4_, f32[32,256]{1,0:T(8,128)S(1)} %get-tuple-element.28.mass), custom_call_target="tpu_custom_call" | custom-call | flops 1048576 | bytes 1048576 | tf_op jit(solution)/shard_map/final/pallas_call | solution.py:592
  (25 shorter events, 0.2 us)
Async XLA Ops:
  2.7 12.1 %copy-start = (f32[2,4,128,128]{3,2,1,0:T(8,128)S(1)}, f32[2,4,128,128]{3,2,1,0:T(8,128)}, u32[]{:S(2)}) copy-start(f32[2,4,128,128]{3,2,1,0:T(8,128)} %refs_6_.1) | copy-start | bytes 1572868
  2.8 7.0 %collective-permute-start.2 = (f32[56,256]{1,0:T(8,128)S(1)}, f32[56,256]{1,0:T(8,128)S(1)}, u32[]{:S(2)}, u32[]{:S(2)}) collective-permute-start(f32[56,256]{1,0:T(8,128)S(1)} %get-tuple-element.17.own.pack), channel_id=1, source_target_pairs={{0,2},{1,3},{2,0},{3,1},{4,6},{5,7},{6,4},{7,5},{8,10},{9,11},{10,... | collective-permute-start | bytes 172040 | tf_op jit(solution)/shard_map/ppermute | solution.py:562
  6.9 4.2 %collective-permute-start.1 = (f32[56,256]{1,0:T(8,128)S(1)}, f32[56,256]{1,0:T(8,128)S(1)}, u32[]{:S(2)}, u32[]{:S(2)}) collective-permute-start(f32[56,256]{1,0:T(8,128)S(1)} %get-tuple-element.17.own.pack), channel_id=1, source_target_pairs={{0,3},{1,0},{2,1},{3,2},{4,7},{5,4},{6,5},{7,6},{8,11},{9,8},{10,9... | collective-permute-start | bytes 172040 | tf_op jit(solution)/shard_map/ppermute | solution.py:562
  8.2 6.0 %collective-permute-start = (f32[56,256]{1,0:T(8,128)S(1)}, f32[56,256]{1,0:T(8,128)S(1)}, u32[]{:S(2)}, u32[]{:S(2)}) collective-permute-start(f32[56,256]{1,0:T(8,128)S(1)} %get-tuple-element.17.own.pack), channel_id=1, source_target_pairs={{0,1},{1,2},{2,3},{3,0},{4,5},{5,6},{6,7},{7,4},{8,9},{9,10},{10,1... | collective-permute-start | bytes 172040 | tf_op jit(solution)/shard_map/ppermute | solution.py:562
  14.2 4.9 %collective-permute-start.4 = (f32[4,32,256]{2,1,0:T(8,128)S(1)}, f32[4,32,256]{2,1,0:T(8,128)S(1)}, u32[]{:S(2)}, u32[]{:S(2)}) collective-permute-start(f32[4,32,256]{2,1,0:T(8,128)S(1)} %pad_maximum_fusion.both), channel_id=1, source_target_pairs={{0,28},{4,0},{8,4},{12,8},{16,12},{20,16},{24,20},{28,24},{1,29},{... | collective-permute-start | bytes 393224 | tf_op jit(solution)/shard_map/ppermute | solution.py:562
  14.6 6.5 %collective-permute-start.3 = (f32[4,32,256]{2,1,0:T(8,128)S(1)}, f32[4,32,256]{2,1,0:T(8,128)S(1)}, u32[]{:S(2)}, u32[]{:S(2)}) collective-permute-start(f32[4,32,256]{2,1,0:T(8,128)S(1)} %pad_maximum_fusion.both), channel_id=1, source_target_pairs={{0,4},{4,8},{8,12},{12,16},{16,20},{20,24},{24,28},{28,0},{1,5},{5... | collective-permute-start | bytes 393224 | tf_op jit(solution)/shard_map/ppermute | solution.py:562
  27.6 8.6 %collective-permute-start.5 = (f32[64,256]{1,0:T(8,128)S(1)}, f32[64,256]{1,0:T(8,128)S(1)}, u32[]{:S(2)}, u32[]{:S(2)}) collective-permute-start(f32[64,256]{1,0:T(8,128)S(1)} %get-tuple-element.23), channel_id=1, source_target_pairs={{0,1},{1,2},{2,3},{3,0},{4,5},{5,6},{6,7},{7,4},{8,9},{9,10},{10,1... | collective-permute-start | bytes 196616 | tf_op jit(solution)/shard_map/ppermute | solution.py:562
  27.6 8.5 %collective-permute-start.7 = (f32[64,256]{1,0:T(8,128)S(1)}, f32[64,256]{1,0:T(8,128)S(1)}, u32[]{:S(2)}, u32[]{:S(2)}) collective-permute-start(f32[64,256]{1,0:T(8,128)S(1)} %get-tuple-element.25), channel_id=1, source_target_pairs={{0,3},{1,0},{2,1},{3,2},{4,7},{5,4},{6,5},{7,6},{8,11},{9,8},{10,9... | collective-permute-start | bytes 196616 | tf_op jit(solution)/shard_map/ppermute | solution.py:562
  31.5 4.7 %collective-permute-start.6 = (f32[24,256]{1,0:T(8,128)S(1)}, f32[24,256]{1,0:T(8,128)S(1)}, u32[]{:S(2)}, u32[]{:S(2)}) collective-permute-start(f32[24,256]{1,0:T(8,128)S(1)} %get-tuple-element.24), channel_id=1, source_target_pairs={{0,2},{1,3},{2,0},{3,1},{4,6},{5,7},{6,4},{7,5},{8,10},{9,11},{10,... | collective-permute-start | bytes 73736 | tf_op jit(solution)/shard_map/ppermute | solution.py:562
  37.5 1.3 %collective-permute-start.8 = (f32[48,128]{1,0:T(8,128)S(1)}, f32[48,128]{1,0:T(8,128)S(1)}, u32[]{:S(2)}, u32[]{:S(2)}) collective-permute-start(f32[48,128]{1,0:T(8,128)S(1)} %get-tuple-element.27), channel_id=1, source_target_pairs={{0,4},{4,0},{8,12},{12,8},{16,20},{20,16},{24,28},{28,24},{1,5},{5... | collective-permute-start | bytes 73736 | tf_op jit(solution)/shard_map/ppermute | solution.py:567
  38.7 5.0 %collective-permute-start.11 = (f32[48,128]{1,0:T(8,128)S(1)}, f32[48,128]{1,0:T(8,128)S(1)}, u32[]{:S(2)}, u32[]{:S(2)}) collective-permute-start(f32[48,128]{1,0:T(8,128)S(1)} %add.28), channel_id=1, source_target_pairs={{0,24},{4,28},{8,16},{12,20},{16,8},{20,12},{24,0},{28,4},{1,25},{... | collective-permute-start | bytes 73736 | tf_op jit(solution)/shard_map/ppermute | solution.py:567
  39.4 4.3 %collective-permute-start.10 = (f32[48,128]{1,0:T(8,128)S(1)}, f32[48,128]{1,0:T(8,128)S(1)}, u32[]{:S(2)}, u32[]{:S(2)}) collective-permute-start(f32[48,128]{1,0:T(8,128)S(1)} %add.28), channel_id=1, source_target_pairs={{0,16},{4,20},{8,24},{12,28},{16,0},{20,4},{24,8},{28,12},{1,17},{... | collective-permute-start | bytes 73736 | tf_op jit(solution)/shard_map/ppermute | solution.py:567
  39.8 4.2 %collective-permute-start.9 = (f32[48,128]{1,0:T(8,128)S(1)}, f32[48,128]{1,0:T(8,128)S(1)}, u32[]{:S(2)}, u32[]{:S(2)}) collective-permute-start(f32[48,128]{1,0:T(8,128)S(1)} %add.28), channel_id=1, source_target_pairs={{0,8},{4,12},{8,0},{12,4},{16,24},{20,28},{24,16},{28,20},{1,9},{5... | collective-permute-start | bytes 73736 | tf_op jit(solution)/shard_map/ppermute | solution.py:567
  44.0 5.7 %collective-permute-start.14 = (f32[48,128]{1,0:T(8,128)S(1)}, f32[48,128]{1,0:T(8,128)S(1)}, u32[]{:S(2)}, u32[]{:S(2)}) collective-permute-start(f32[48,128]{1,0:T(8,128)S(1)} %add_add_fusion.1), channel_id=1, source_target_pairs={{0,3},{1,2},{2,1},{3,0},{4,7},{5,6},{6,5},{7,4},{8,11},{9,10},{10,... | collective-permute-start | bytes 73736 | tf_op jit(solution)/shard_map/ppermute | solution.py:567
  45.4 4.8 %collective-permute-start.13 = (f32[48,128]{1,0:T(8,128)S(1)}, f32[48,128]{1,0:T(8,128)S(1)}, u32[]{:S(2)}, u32[]{:S(2)}) collective-permute-start(f32[48,128]{1,0:T(8,128)S(1)} %add_add_fusion.1), channel_id=1, source_target_pairs={{0,2},{1,3},{2,0},{3,1},{4,6},{5,7},{6,4},{7,5},{8,10},{9,11},{10,... | collective-permute-start | bytes 73736 | tf_op jit(solution)/shard_map/ppermute | solution.py:567
  45.4 5.1 %collective-permute-start.12 = (f32[48,128]{1,0:T(8,128)S(1)}, f32[48,128]{1,0:T(8,128)S(1)}, u32[]{:S(2)}, u32[]{:S(2)}) collective-permute-start(f32[48,128]{1,0:T(8,128)S(1)} %add_add_fusion.1), channel_id=1, source_target_pairs={{0,1},{1,0},{2,3},{3,2},{4,5},{5,4},{6,7},{7,6},{8,9},{9,8},{10,11... | collective-permute-start | bytes 73736 | tf_op jit(solution)/shard_map/ppermute | solution.py:567
  50.5 1.3 %collective-permute-start.15 = (f32[48,128]{1,0:T(8,128)S(1)}, f32[48,128]{1,0:T(8,128)S(1)}, u32[]{:S(2)}, u32[]{:S(2)}) collective-permute-start(f32[48,128]{1,0:T(8,128)S(1)} %add_add_fusion.mine), channel_id=1, source_target_pairs={{0,4},{4,0},{8,12},{12,8},{16,20},{20,16},{24,28},{28,24},{1,5},{5... | collective-permute-start | bytes 73736 | tf_op jit(solution)/shard_map/ppermute | solution.py:567

commit v7 on v6

--- a/solution.py
+++ b/solution.py
@@ -296,9 +296,9 @@
         lanes = slice((b % 2) * CZ, (b % 2 + 1) * CZ)
         owner, pair = b // CY, b % CY // 2
         if a < HALO:
-            ref, at = edge[0], pair * HALO + a
+            ref, at = edge.at[0], pair * HALO + a
         elif a >= CX + HALO:
-            ref, at = edge[1], pair * HALO + a - CX - HALO
+            ref, at = edge.at[1], pair * HALO + a - CX - HALO
         else:
             ref, at = mid, pair * CX + a - HALO
         return ref[owner, at * modes : (at + 1) * modes, lanes]
@@ -306,8 +306,21 @@
     return src
 
 
-def own_source_kernel(modes, groups, capacity, both, _, own, inner, *scratch):
+def edge_source(there, modes, groups, capacity, low, out, sets, jobs):
+    a_first = jnp.where(low > 0, CX - HALO, 0)
+
+    def one(o):
+        at = 2 * o if isinstance(o, int) else 0
+        mem = sets[at : at + 2]
+        jobs.extend(scatter(there, modes, capacity, o, a_first, HALO, out.at[o], *mem))
+
+    each(groups, one)
+
+
+def own_source_kernel(modes, groups, capacity, odd_ref, both, near, _, own, inner, edge, *scratch):
     jobs = []
+    half = len(scratch) // 2
+    edges, scratch = scratch[half:], scratch[:half]
 
     def one(o):
         at = 2 * o if isinstance(o, int) else 0
@@ -315,6 +328,7 @@
         jobs.extend(scatter(both, modes, capacity, o, 0, CX, own.at[o], *mem))
 
     each(groups, one)
+    edge_source(near, modes, groups, capacity, odd_ref[0], edge, edges, jobs)
     later_chunks(jobs)
     src = source_reader(modes, own)
     for a in range(HALO + 1, CX + HALO - 1):
@@ -322,30 +336,22 @@
             inner[a - HALO - 1, b] = sec
 
 
-def fluid_kernel(modes, groups, capacity, both, low, high, mid, inner, mdiag, stiff, *refs):
+def fluid_kernel(
+    modes, groups, capacity, odd_ref, both, far, near_edge, mid, inner, mdiag, stiff, *refs
+):
     outs = refs[:groups]
     edge, outer, press, force, scratch = (
-        refs[groups : groups + 2],
-        *refs[groups + 2 : groups + 5],
-        refs[groups + 5 :],
+        refs[groups],
+        *refs[groups + 1 : groups + 4],
+        refs[groups + 4 :],
     )
     local = both.shape[2]
     count = groups * CY
     width = min(local, capacity)
     jobs = []
-    for side, there in enumerate((low, high)):
-        a_first = CX - HALO if side == 0 else 0
-        wide = 128 if side == 0 else 256
-        half = len(scratch) // 2
-        sets = scratch[side * half : (side + 1) * half]
-
-        def one(o, there=there, a_first=a_first, wide=wide, sets=sets, side=side):
-            at = 2 * o if isinstance(o, int) else 0
-            mem = sets[at : at + 2]
-            target = edge[side].at[o]
-            jobs.extend(scatter(there, modes, capacity, o, a_first, HALO, target, *mem, wide))
-
-        each(groups, one)
+    odd = odd_ref[0]
+    edge[1 - odd] = near_edge[...]
+    edge_source(far, modes, groups, capacity, 1 - odd, edge.at[odd], scratch, jobs)
     later_chunks(jobs)
     src = source_reader(modes, mid, edge)
     for i, a in enumerate((1, 2, CX + HALO - 1, CX + HALO)):
@@ -659,8 +665,11 @@
             for x in packs
         ]
     )
-    low = shifted(both, "passage", 1)
-    high = shifted(both, "passage", -1)
+    ring = lax.axis_size("passage")
+    pairs = [(i, (i + 1 if i % 2 else i - 1) % ring) for i in range(ring)]
+    far = lax.ppermute(both, "passage", pairs)
+    near = swapped(both, "passage", 1)
+    odd = (lax.axis_index("passage") & 1).astype(jnp.int32).reshape(1)
     window = [packs[1], packs[0], packs[groups - 1]]
     nwin = 3 * local // bs
     stiff = call(
@@ -685,13 +694,17 @@
     rows = CX * CY // 2 * mine
     edge_rows = HALO * CY // 2 * mine
     mib = 20 if groups <= 4 else 36
-    source, inner = call(
+    source, inner, near_edge = call(
         functools.partial(own_source_kernel, mine, groups, capacity),
         "own_source",
-        (field(groups, rows, 2 * CZ), field(CX - 2, groups * CY, mine, CZ)),
-        [],
-        [both, stiff],
-        operands(rows, width),
+        (
+            field(groups, rows, 2 * CZ),
+            field(CX - 2, groups * CY, mine, CZ),
+            field(groups, edge_rows, 2 * CZ),
+        ),
+        [odd],
+        [both, near, stiff],
+        operands(rows, width) + operands(edge_rows, width),
         1 << 32,
         mib,
     )
@@ -702,15 +715,14 @@
             field(3 * mine + (8 + modes if k in (1, groups - 1) else 0), local)
             for k in range(groups)
         ),
-        [],
-        [both, low, high, source, inner, mdiag, stiff],
+        [odd],
+        [both, far, near_edge, source, inner, mdiag, stiff],
         [
-            *[pltpu.VMEM((groups, edge_rows, 2 * CZ), F32)] * 2,
+            pltpu.VMEM((2, groups, edge_rows, 2 * CZ), F32),
             pltpu.VMEM((4, groups * CY, mine, CZ), F32),
             pltpu.VMEM((groups, rows, 4 * CZ), BF),
             pltpu.VMEM((groups, mine, local), F32),
-            *operands(edge_rows, 128),
-            *operands(edge_rows, 256),
+            *operands(edge_rows, width),
         ],
         1 << 32,
         mib,

time: 53.7 us -> 54.1 us (level)
  starting transfers between devices: 18.7 us -> 20.7 us
  waiting for transfers between devices: 18.1 us -> 16.9 us
    ppermute x0 -> x1, starting transfers between devices: none -> 2.54 us  [body(): far = lax.ppermute(both, 'passage', pairs)]
    ppermute x8 -> x6, waiting for transfers between devices: 11.9 us -> 9.99 us  [shifted(): return lax.ppermute(x, axis, [(i, (i + k) % n) for i in range(n)])]
    ppermute x8 -> x9, waiting for transfers between devices: 6.19 us -> 6.88 us  [swapped(): return lax.ppermute(x, axis, [(i, i ^ k) for i in range(n)])]
    ppermute x8 -> x6, starting transfers between devices: 10.6 us -> 10 us  [shifted(): return lax.ppermute(x, axis, [(i, (i + k) % n) for i in range(n)])]
    ppermute x8 -> x9, starting transfers between devices: 8.08 us -> 8.15 us  [swapped(): return lax.ppermute(x, axis, [(i, i ^ k) for i in range(n)])]
  transfers between devices with their start and end apart: 16 -> 16, of which waited for: 12 -> 11; matrix products, arithmetic and copies ran while one was open for 0% -> 0% of each run, Pallas kernels for 8% -> 10%
where the time goes in v7:
time: 54.1 us
  starting transfers between devices  20.7 us (38%)
  waiting for transfers between devices  16.9 us (31%)
  Pallas kernels  14.9 us (28%)
  between operations  1.4 us (3%)
    pallas_call x5, Pallas kernels, call(): pl.pallas_call(kernel, name=name, out_shape=out_shape, in_specs=[smem()]...  13.5 us
    ppermute x6, starting transfers between devices, shifted(): return lax.ppermute(x, axis, [(i, (i + k) % n) for i in range(n)])  10 us
    ppermute x6, waiting for transfers between devices, shifted(): return lax.ppermute(x, axis, [(i, (i + k) % n) for i in range(n)])  9.99 us
    ppermute x9, starting transfers between devices, swapped(): return lax.ppermute(x, axis, [(i, i ^ k) for i in range(n)])  8.15 us
    ppermute x9, waiting for transfers between devices, swapped(): return lax.ppermute(x, axis, [(i, i ^ k) for i in range(n)])  6.88 us
    ppermute x1, starting transfers between devices, body(): far = lax.ppermute(both, 'passage', pairs)  2.54 us
    pallas_call x1, Pallas kernels, body(): pl.pallas_call(functools.partial(pack_kernel, modes, groups), name='pack'...  1.45 us
  transfers between devices with their start and end apart: 16, of which 11 were waited for; matrix products, arithmetic and copies ran while one was open for 0% of the time, Pallas kernels for 10%

profile of v7, /device:TPU:0, one launch (start us, length us, event | category | flops | bytes accessed | tf_op | source)
XLA Modules:
  0.0 54.1 jit_solution(17904489837177233793)
XLA Ops:
  1.3 1.5 %pack.1 = (f32[56,256]{1,0:T(8,128)S(1)}, f32[1,256]{1,0:T(1,128)S(1)}, f32[1,256]{1,0:T(1,128)S(1)}, s32[2,4]{1,0:T(2,128)S(1)}) custom-call(s32[1]{0:T(128)S(6)} %copy.13.live_ref, s32[8,128]{1,0:T(8,128)} %bitcast.16, s32[8,128]{1,0:T(8,128)} %bitcast.17, s32[8,128]{1,0:T(8,128)} %bitcast.18, f32[8,128]{1,0:T(8,128)} %bitcast.19, f32[32,256]{1,0:T(8,128)} %refs_4_.1, ...), custom_call_target="tpu_custom_call" | custom-call | flops 268435456 | bytes 1048576 | tf_op jit(solution)/shard_map/pack/pallas_call | solution.py:631
  2.8 4.1 %collective-permute-start.2 = (f32[56,256]{1,0:T(8,128)S(1)}, f32[56,256]{1,0:T(8,128)S(1)}, u32[]{:S(2)}, u32[]{:S(2)}) collective-permute-start(f32[56,256]{1,0:T(8,128)S(1)} %get-tuple-element.18.own.pack), channel_id=1, source_target_pairs={{0,2},{1,3},{2,0},{3,1},{4,6},{5,7},{6,4},{7,5},{8,10},{9,11},{10,... | collective-permute-start | bytes 172040 | tf_op jit(solution)/shard_map/ppermute | solution.py:568
  6.9 1.4 %collective-permute-start.1 = (f32[56,256]{1,0:T(8,128)S(1)}, f32[56,256]{1,0:T(8,128)S(1)}, u32[]{:S(2)}, u32[]{:S(2)}) collective-permute-start(f32[56,256]{1,0:T(8,128)S(1)} %get-tuple-element.18.own.pack), channel_id=1, source_target_pairs={{0,3},{1,0},{2,1},{3,2},{4,7},{5,4},{6,5},{7,6},{8,11},{9,8},{10,9... | collective-permute-start | bytes 172040 | tf_op jit(solution)/shard_map/ppermute | solution.py:568
  8.2 0.7 %collective-permute-start = (f32[56,256]{1,0:T(8,128)S(1)}, f32[56,256]{1,0:T(8,128)S(1)}, u32[]{:S(2)}, u32[]{:S(2)}) collective-permute-start(f32[56,256]{1,0:T(8,128)S(1)} %get-tuple-element.18.own.pack), channel_id=1, source_target_pairs={{0,1},{1,2},{2,3},{3,0},{4,5},{5,6},{6,7},{7,4},{8,9},{9,10},{10,1... | collective-permute-start | bytes 172040 | tf_op jit(solution)/shard_map/ppermute | solution.py:568
  8.9 0.8 %collective-permute-done.2 = f32[56,256]{1,0:T(8,128)S(1)} collective-permute-done((f32[56,256]{1,0:T(8,128)S(1)}, f32[56,256]{1,0:T(8,128)S(1)}, u32[]{:S(2)}, u32[]{:S(2)}) %collective-permute-start.2) | collective-permute-done | bytes 57376 | tf_op jit(solution)/shard_map/ppermute | solution.py:568
  9.8 1.3 %collective-permute-done.1.nxt = f32[56,256]{1,0:T(8,128)S(1)} collective-permute-done((f32[56,256]{1,0:T(8,128)S(1)}, f32[56,256]{1,0:T(8,128)S(1)}, u32[]{:S(2)}, u32[]{:S(2)}) %collective-permute-start.1) | collective-permute-done | bytes 57376 | tf_op jit(solution)/shard_map/ppermute | solution.py:568
  11.1 3.1 %collective-permute-done.prev = f32[56,256]{1,0:T(8,128)S(1)} collective-permute-done((f32[56,256]{1,0:T(8,128)S(1)}, f32[56,256]{1,0:T(8,128)S(1)}, u32[]{:S(2)}, u32[]{:S(2)}) %collective-permute-start) | collective-permute-done | bytes 57376 | tf_op jit(solution)/shard_map/ppermute | solution.py:568
  14.2 0.1 collective-permute-start.4
  14.3 0.1 pad_add_fusion.sub_ref
  14.4 2.5 %collective-permute-start.3 = (f32[4,32,256]{2,1,0:T(8,128)S(1)}, f32[4,32,256]{2,1,0:T(8,128)S(1)}, u32[]{:S(2)}, u32[]{:S(2)}) collective-permute-start(f32[4,32,256]{2,1,0:T(8,128)S(1)} %pad_maximum_fusion.both), channel_id=1, source_target_pairs={{0,28},{4,8},{8,4},{12,16},{16,12},{20,24},{24,20},{28,0},{1,29},{... | collective-permute-start | bytes 393224 | tf_op jit(solution)/shard_map/ppermute | solution.py:670
  16.9 0.9 %stiff.1._.refs_4_ = f32[32,256]{1,0:T(8,128)S(1)} custom-call(s32[2]{0:T(128)S(1)} %pad_add_fusion.sub_ref, s32[2,4]{1,0:T(2,128)S(1)} %get-tuple-element.17.cols_ref, f32[56,256]{1,0:T(8,128)S(1)} %collective-permute-done.prev, f32[56,256]{1,0:T(8,128)S(1)} %get-tuple-element.18.own.pack, f32[56,256]{1,0:T(8,128)S(1)} %collective-permute-done.1.nxt, ...), custom_call_target="tpu_custom_call" | custom-call | flops 536870912 | bytes 1048576 | tf_op jit(solution)/shard_map/stiff/pallas_call | solution.py:598
  17.9 4.3 %own_source.1 = (f32[4,256,256]{2,1,0:T(8,128)S(1)}, f32[6,32,8,128]{3,2,1,0:T(8,128)S(1)}, f32[4,64,256]{2,1,0:T(8,128)S(1)}) custom-call(s32[1]{0:T(128)} %bitcast.1.odd_ref, f32[4,32,256]{2,1,0:T(8,128)S(1)} %pad_maximum_fusion.both, f32[4,32,256]{2,1,0:T(8,128)S(1)} %collective-permute-done.4.near, f32[32,256]{1,0:T(8,128)S(1)} %stiff.1._.refs_4_), custom_call_target="tpu_custom_call" | custom-call | flops 4294967296 | bytes 1048576 | tf_op jit(solution)/shard_map/own_source/pallas_call | solution.py:598
  22.2 5.5 %fluid.1 = (f32[24,256]{1,0:T(8,128)S(1)}, f32[64,256]{1,0:T(8,128)S(1)}, f32[24,256]{1,0:T(8,128)S(1)}, f32[64,256]{1,0:T(8,128)S(1)}) custom-call(s32[1]{0:T(128)} %bitcast.1.odd_ref, f32[4,32,256]{2,1,0:T(8,128)S(1)} %pad_maximum_fusion.both, f32[4,32,256]{2,1,0:T(8,128)S(1)} %collective-permute-done.3.far, ...), custom_call_target="tpu_custom_call" | custom-call | flops 4294967296 | bytes 1048576 | tf_op jit(solution)/shard_map/fluid/pallas_call | solution.py:598
  27.7 0.1 collective-permute-start.5
  27.8 3.8 %collective-permute-start.7 = (f32[64,256]{1,0:T(8,128)S(1)}, f32[64,256]{1,0:T(8,128)S(1)}, u32[]{:S(2)}, u32[]{:S(2)}) collective-permute-start(f32[64,256]{1,0:T(8,128)S(1)} %get-tuple-element.27), channel_id=1, source_target_pairs={{0,3},{1,0},{2,1},{3,2},{4,7},{5,4},{6,5},{7,6},{8,11},{9,8},{10,9... | collective-permute-start | bytes 196616 | tf_op jit(solution)/shard_map/ppermute | solution.py:568
  31.6 4.7 %collective-permute-done.6.refs_2_ = f32[24,256]{1,0:T(8,128)S(1)} collective-permute-done((f32[24,256]{1,0:T(8,128)S(1)}, f32[24,256]{1,0:T(8,128)S(1)}, u32[]{:S(2)}, u32[]{:S(2)}) %collective-permute-start.6) | collective-permute-done | bytes 24608 | tf_op jit(solution)/shard_map/ppermute | solution.py:568
  36.3 1.3 %gram.1 = (f32[48,128]{1,0:T(8,128)S(1)}, f32[48,128]{1,0:T(8,128)S(1)}, f32[32,256]{1,0:T(8,128)S(1)}) custom-call(s32[2]{0:T(128)S(1)} %pad_add_fusion.sub_ref, s32[2,4]{1,0:T(2,128)S(1)} %get-tuple-element.17.cols_ref, f32[56,256]{1,0:T(8,128)S(1)} %collective-permute-done.prev, f32[56,256]{1,0:T(8,128)S(1)} %get-tuple-element.18.own.pack, ...), custom_call_target="tpu_custom_call" | custom-call | flops 536870912 | bytes 1048576 | tf_op jit(solution)/shard_map/gram/pallas_call | solution.py:598
  37.6 0.1 collective-permute-start.8
  37.7 1.2 %collective-permute-done.8 = f32[48,128]{1,0:T(8,128)S(1)} collective-permute-done((f32[48,128]{1,0:T(8,128)S(1)}, f32[48,128]{1,0:T(8,128)S(1)}, u32[]{:S(2)}, u32[]{:S(2)}) %collective-permute-start.8) | collective-permute-done | bytes 24608 | tf_op jit(solution)/shard_map/ppermute | solution.py:573
  38.8 0.4 collective-permute-start.11
  39.2 1.8 %collective-permute-start.10 = (f32[48,128]{1,0:T(8,128)S(1)}, f32[48,128]{1,0:T(8,128)S(1)}, u32[]{:S(2)}, u32[]{:S(2)}) collective-permute-start(f32[48,128]{1,0:T(8,128)S(1)} %add.28), channel_id=1, source_target_pairs={{0,16},{4,20},{8,24},{12,28},{16,0},{20,4},{24,8},{28,12},{1,17},{... | collective-permute-start | bytes 73736 | tf_op jit(solution)/shard_map/ppermute | solution.py:573
  41.0 1.3 %collective-permute-start.9 = (f32[48,128]{1,0:T(8,128)S(1)}, f32[48,128]{1,0:T(8,128)S(1)}, u32[]{:S(2)}, u32[]{:S(2)}) collective-permute-start(f32[48,128]{1,0:T(8,128)S(1)} %add.28), channel_id=1, source_target_pairs={{0,8},{4,12},{8,0},{12,4},{16,24},{20,28},{24,16},{28,20},{1,9},{5... | collective-permute-start | bytes 73736 | tf_op jit(solution)/shard_map/ppermute | solution.py:573
  42.3 1.2 %collective-permute-done.11 = f32[48,128]{1,0:T(8,128)S(1)} collective-permute-done((f32[48,128]{1,0:T(8,128)S(1)}, f32[48,128]{1,0:T(8,128)S(1)}, u32[]{:S(2)}, u32[]{:S(2)}) %collective-permute-start.11) | collective-permute-done | bytes 24608 | tf_op jit(solution)/shard_map/ppermute | solution.py:573
  43.6 1.3 %collective-permute-done.9 = f32[48,128]{1,0:T(8,128)S(1)} collective-permute-done((f32[48,128]{1,0:T(8,128)S(1)}, f32[48,128]{1,0:T(8,128)S(1)}, u32[]{:S(2)}, u32[]{:S(2)}) %collective-permute-start.9) | collective-permute-done | bytes 24608 | tf_op jit(solution)/shard_map/ppermute | solution.py:573
  44.8 1.5 %collective-permute-start.14 = (f32[48,128]{1,0:T(8,128)S(1)}, f32[48,128]{1,0:T(8,128)S(1)}, u32[]{:S(2)}, u32[]{:S(2)}) collective-permute-start(f32[48,128]{1,0:T(8,128)S(1)} %add_add_fusion.1), channel_id=1, source_target_pairs={{0,3},{1,2},{2,1},{3,0},{4,7},{5,6},{6,5},{7,4},{8,11},{9,10},{10,... | collective-permute-start | bytes 73736 | tf_op jit(solution)/shard_map/ppermute | solution.py:573
  46.3 3.0 %collective-permute-start.12 = (f32[48,128]{1,0:T(8,128)S(1)}, f32[48,128]{1,0:T(8,128)S(1)}, u32[]{:S(2)}, u32[]{:S(2)}) collective-permute-start(f32[48,128]{1,0:T(8,128)S(1)} %add_add_fusion.1), channel_id=1, source_target_pairs={{0,1},{1,0},{2,3},{3,2},{4,5},{5,4},{6,7},{7,6},{8,9},{9,8},{10,11... | collective-permute-start | bytes 73736 | tf_op jit(solution)/shard_map/ppermute | solution.py:573
  49.3 1.2 %collective-permute-done.14 = f32[48,128]{1,0:T(8,128)S(1)} collective-permute-done((f32[48,128]{1,0:T(8,128)S(1)}, f32[48,128]{1,0:T(8,128)S(1)}, u32[]{:S(2)}, u32[]{:S(2)}) %collective-permute-start.14) | collective-permute-done | bytes 24608 | tf_op jit(solution)/shard_map/ppermute | solution.py:573
  50.5 0.5 %collective-permute-done.13 = f32[48,128]{1,0:T(8,128)S(1)} collective-permute-done((f32[48,128]{1,0:T(8,128)S(1)}, f32[48,128]{1,0:T(8,128)S(1)}, u32[]{:S(2)}, u32[]{:S(2)}) %collective-permute-start.13) | collective-permute-done | bytes 24608 | tf_op jit(solution)/shard_map/ppermute | solution.py:573
  51.1 0.2 collective-permute-done.12
  51.3 0.1 collective-permute-start.15
  51.4 1.2 %collective-permute-done.15.other = f32[48,128]{1,0:T(8,128)S(1)} collective-permute-done((f32[48,128]{1,0:T(8,128)S(1)}, f32[48,128]{1,0:T(8,128)S(1)}, u32[]{:S(2)}, u32[]{:S(2)}) %collective-permute-start.15) | collective-permute-done | bytes 24608 | tf_op jit(solution)/shard_map/ppermute | solution.py:573
  52.6 1.5 %final.1 = (f32[32,256]{1,0:T(8,128)}, f32[64,64]{1,0:T(8,128)}, f32[64,64]{1,0:T(8,128)}) custom-call(s32[2]{0:T(128)S(1)} %pad_add_fusion.sub_ref, f32[48,128]{1,0:T(8,128)S(1)} %add_add_fusion.mine, f32[48,128]{1,0:T(8,128)S(1)} %collective-permute-done.15.other, f32[32,256]{1,0:T(8,128)S(1)} %stiff.1._.refs_4_, f32[32,256]{1,0:T(8,128)S(1)} %get-tuple-element.30.mass), custom_call_target="tpu_custom_call" | custom-call | flops 1048576 | bytes 1048576 | tf_op jit(solution)/shard_map/final/pallas_call | solution.py:598
  (25 shorter events, 0.1 us)
Async XLA Ops:
  2.7 14.2 %copy-start = (f32[2,4,128,128]{3,2,1,0:T(8,128)S(1)}, f32[2,4,128,128]{3,2,1,0:T(8,128)}, u32[]{:S(2)}) copy-start(f32[2,4,128,128]{3,2,1,0:T(8,128)} %refs_6_.1) | copy-start | bytes 1572868
  2.8 7.0 %collective-permute-start.2 = (f32[56,256]{1,0:T(8,128)S(1)}, f32[56,256]{1,0:T(8,128)S(1)}, u32[]{:S(2)}, u32[]{:S(2)}) collective-permute-start(f32[56,256]{1,0:T(8,128)S(1)} %get-tuple-element.18.own.pack), channel_id=1, source_target_pairs={{0,2},{1,3},{2,0},{3,1},{4,6},{5,7},{6,4},{7,5},{8,10},{9,11},{10,... | collective-permute-start | bytes 172040 | tf_op jit(solution)/shard_map/ppermute | solution.py:568
  6.9 4.2 %collective-permute-start.1 = (f32[56,256]{1,0:T(8,128)S(1)}, f32[56,256]{1,0:T(8,128)S(1)}, u32[]{:S(2)}, u32[]{:S(2)}) collective-permute-start(f32[56,256]{1,0:T(8,128)S(1)} %get-tuple-element.18.own.pack), channel_id=1, source_target_pairs={{0,3},{1,0},{2,1},{3,2},{4,7},{5,4},{6,5},{7,6},{8,11},{9,8},{10,9... | collective-permute-start | bytes 172040 | tf_op jit(solution)/shard_map/ppermute | solution.py:568
  8.2 6.0 %collective-permute-start = (f32[56,256]{1,0:T(8,128)S(1)}, f32[56,256]{1,0:T(8,128)S(1)}, u32[]{:S(2)}, u32[]{:S(2)}) collective-permute-start(f32[56,256]{1,0:T(8,128)S(1)} %get-tuple-element.18.own.pack), channel_id=1, source_target_pairs={{0,1},{1,2},{2,3},{3,0},{4,5},{5,6},{6,7},{7,4},{8,9},{9,10},{10,1... | collective-permute-start | bytes 172040 | tf_op jit(solution)/shard_map/ppermute | solution.py:568
  14.2 3.6 %collective-permute-start.4 = (f32[4,32,256]{2,1,0:T(8,128)S(1)}, f32[4,32,256]{2,1,0:T(8,128)S(1)}, u32[]{:S(2)}, u32[]{:S(2)}) collective-permute-start(f32[4,32,256]{2,1,0:T(8,128)S(1)} %pad_maximum_fusion.both), channel_id=1, source_target_pairs={{0,4},{4,0},{8,12},{12,8},{16,20},{20,16},{24,28},{28,24},{1,5},{5... | collective-permute-start | bytes 393224 | tf_op jit(solution)/shard_map/ppermute | solution.py:573
  14.4 7.8 %collective-permute-start.3 = (f32[4,32,256]{2,1,0:T(8,128)S(1)}, f32[4,32,256]{2,1,0:T(8,128)S(1)}, u32[]{:S(2)}, u32[]{:S(2)}) collective-permute-start(f32[4,32,256]{2,1,0:T(8,128)S(1)} %pad_maximum_fusion.both), channel_id=1, source_target_pairs={{0,28},{4,8},{8,4},{12,16},{16,12},{20,24},{24,20},{28,0},{1,29},{... | collective-permute-start | bytes 393224 | tf_op jit(solution)/shard_map/ppermute | solution.py:670
  27.7 8.6 %collective-permute-start.5 = (f32[64,256]{1,0:T(8,128)S(1)}, f32[64,256]{1,0:T(8,128)S(1)}, u32[]{:S(2)}, u32[]{:S(2)}) collective-permute-start(f32[64,256]{1,0:T(8,128)S(1)} %get-tuple-element.25), channel_id=1, source_target_pairs={{0,1},{1,2},{2,3},{3,0},{4,5},{5,6},{6,7},{7,4},{8,9},{9,10},{10,1... | collective-permute-start | bytes 196616 | tf_op jit(solution)/shard_map/ppermute | solution.py:568
  27.8 8.5 %collective-permute-start.7 = (f32[64,256]{1,0:T(8,128)S(1)}, f32[64,256]{1,0:T(8,128)S(1)}, u32[]{:S(2)}, u32[]{:S(2)}) collective-permute-start(f32[64,256]{1,0:T(8,128)S(1)} %get-tuple-element.27), channel_id=1, source_target_pairs={{0,3},{1,0},{2,1},{3,2},{4,7},{5,4},{6,5},{7,6},{8,11},{9,8},{10,9... | collective-permute-start | bytes 196616 | tf_op jit(solution)/shard_map/ppermute | solution.py:568
  31.6 4.7 %collective-permute-start.6 = (f32[24,256]{1,0:T(8,128)S(1)}, f32[24,256]{1,0:T(8,128)S(1)}, u32[]{:S(2)}, u32[]{:S(2)}) collective-permute-start(f32[24,256]{1,0:T(8,128)S(1)} %get-tuple-element.26), channel_id=1, source_target_pairs={{0,2},{1,3},{2,0},{3,1},{4,6},{5,7},{6,4},{7,5},{8,10},{9,11},{10,... | collective-permute-start | bytes 73736 | tf_op jit(solution)/shard_map/ppermute | solution.py:568
  37.6 1.3 %collective-permute-start.8 = (f32[48,128]{1,0:T(8,128)S(1)}, f32[48,128]{1,0:T(8,128)S(1)}, u32[]{:S(2)}, u32[]{:S(2)}) collective-permute-start(f32[48,128]{1,0:T(8,128)S(1)} %get-tuple-element.29), channel_id=1, source_target_pairs={{0,4},{4,0},{8,12},{12,8},{16,20},{20,16},{24,28},{28,24},{1,5},{5... | collective-permute-start | bytes 73736 | tf_op jit(solution)/shard_map/ppermute | solution.py:573
  38.8 4.7 %collective-permute-start.11 = (f32[48,128]{1,0:T(8,128)S(1)}, f32[48,128]{1,0:T(8,128)S(1)}, u32[]{:S(2)}, u32[]{:S(2)}) collective-permute-start(f32[48,128]{1,0:T(8,128)S(1)} %add.28), channel_id=1, source_target_pairs={{0,24},{4,28},{8,16},{12,20},{16,8},{20,12},{24,0},{28,4},{1,25},{... | collective-permute-start | bytes 73736 | tf_op jit(solution)/shard_map/ppermute | solution.py:573
  39.2 4.3 %collective-permute-start.10 = (f32[48,128]{1,0:T(8,128)S(1)}, f32[48,128]{1,0:T(8,128)S(1)}, u32[]{:S(2)}, u32[]{:S(2)}) collective-permute-start(f32[48,128]{1,0:T(8,128)S(1)} %add.28), channel_id=1, source_target_pairs={{0,16},{4,20},{8,24},{12,28},{16,0},{20,4},{24,8},{28,12},{1,17},{... | collective-permute-start | bytes 73736 | tf_op jit(solution)/shard_map/ppermute | solution.py:573
  41.0 3.8 %collective-permute-start.9 = (f32[48,128]{1,0:T(8,128)S(1)}, f32[48,128]{1,0:T(8,128)S(1)}, u32[]{:S(2)}, u32[]{:S(2)}) collective-permute-start(f32[48,128]{1,0:T(8,128)S(1)} %add.28), channel_id=1, source_target_pairs={{0,8},{4,12},{8,0},{12,4},{16,24},{20,28},{24,16},{28,20},{1,9},{5... | collective-permute-start | bytes 73736 | tf_op jit(solution)/shard_map/ppermute | solution.py:573
  44.8 5.7 %collective-permute-start.14 = (f32[48,128]{1,0:T(8,128)S(1)}, f32[48,128]{1,0:T(8,128)S(1)}, u32[]{:S(2)}, u32[]{:S(2)}) collective-permute-start(f32[48,128]{1,0:T(8,128)S(1)} %add_add_fusion.1), channel_id=1, source_target_pairs={{0,3},{1,2},{2,1},{3,0},{4,7},{5,6},{6,5},{7,4},{8,11},{9,10},{10,... | collective-permute-start | bytes 73736 | tf_op jit(solution)/shard_map/ppermute | solution.py:573
  46.3 4.8 %collective-permute-start.13 = (f32[48,128]{1,0:T(8,128)S(1)}, f32[48,128]{1,0:T(8,128)S(1)}, u32[]{:S(2)}, u32[]{:S(2)}) collective-permute-start(f32[48,128]{1,0:T(8,128)S(1)} %add_add_fusion.1), channel_id=1, source_target_pairs={{0,2},{1,3},{2,0},{3,1},{4,6},{5,7},{6,4},{7,5},{8,10},{9,11},{10,... | collective-permute-start | bytes 73736 | tf_op jit(solution)/shard_map/ppermute | solution.py:573
  46.3 5.0 %collective-permute-start.12 = (f32[48,128]{1,0:T(8,128)S(1)}, f32[48,128]{1,0:T(8,128)S(1)}, u32[]{:S(2)}, u32[]{:S(2)}) collective-permute-start(f32[48,128]{1,0:T(8,128)S(1)} %add_add_fusion.1), channel_id=1, source_target_pairs={{0,1},{1,0},{2,3},{3,2},{4,5},{5,4},{6,7},{7,6},{8,9},{9,8},{10,11... | collective-permute-start | bytes 73736 | tf_op jit(solution)/shard_map/ppermute | solution.py:573
  51.3 1.3 %collective-permute-start.15 = (f32[48,128]{1,0:T(8,128)S(1)}, f32[48,128]{1,0:T(8,128)S(1)}, u32[]{:S(2)}, u32[]{:S(2)}) collective-permute-start(f32[48,128]{1,0:T(8,128)S(1)} %add_add_fusion.mine), channel_id=1, source_target_pairs={{0,4},{4,0},{8,12},{12,8},{16,20},{20,16},{24,28},{28,24},{1,5},{5... | collective-permute-start | bytes 73736 | tf_op jit(solution)/shard_map/ppermute | solution.py:573

commit v8 on v6

--- a/solution.py
+++ b/solution.py
@@ -65,9 +65,10 @@
     return lax.dot_general(x, y, (((1,), (0,)), ((), ())), preferred_element_type=F32)
 
 
-def pack_kernel(modes, groups, live_ref, *refs):
+def pack_kernel(modes, groups, count, live_ref, *refs):
     sources, (out, mdiag, diag, cols) = refs[:8], refs[8:12]
-    owner_ref, cell_ref, node_ref, weight_ref, sems = refs[12:]
+    distant = refs[12:-5]
+    owner_ref, cell_ref, node_ref, weight_ref, sems = refs[-5:]
     targets = [owner_ref, cell_ref, node_ref, weight_ref]
     targets += [out.at[0:modes, :], mdiag, diag, cols]
     copies = [
@@ -134,6 +135,10 @@
         out[at : at + half, wide : 2 * wide] = x[half:]
     for copy in copies[4:]:
         copy.wait()
+    for k, far in enumerate(distant, 2):
+        at = first_mode(modes, groups, count, lax.rem(lax.axis_index("sub").astype(jnp.int32) + k, groups))
+        far[0:count, :] = out[pl.ds(at, count), :]
+        far[count:, :] = out[modes:, :]
 
 
 class Lists:
@@ -622,17 +627,20 @@
     deep, wide = slots // 128, 128
     capacity = 2 * slots // groups
     slotted = [x.reshape(deep, wide) for x in (slot_owner, slot_cell, slot_node, slot_weight)]
-    pack, mdiag, diag, cols = pl.pallas_call(
-        functools.partial(pack_kernel, modes, groups),
+    mine = max(8, modes // groups)
+    beyond = range(2, groups - 1)
+    pack, mdiag, diag, cols, *distant = pl.pallas_call(
+        functools.partial(pack_kernel, modes, groups, mine),
         name="pack",
         out_shape=(
             jax.ShapeDtypeStruct((modes + 3 * deep, local), F32),
             jax.ShapeDtypeStruct((1, local), F32),
             jax.ShapeDtypeStruct((1, local), F32),
             jax.ShapeDtypeStruct(block_cols.shape, jnp.int32),
+            *[jax.ShapeDtypeStruct((mine + 3 * deep, local), F32) for _ in beyond],
         ),
         in_specs=[smem()] + [pl.BlockSpec(memory_space=pltpu.MemorySpace.HBM)] * 8,
-        out_specs=(vmem(), vmem(), vmem(), vmem()),
+        out_specs=(vmem(), vmem(), vmem(), vmem(), *[vmem() for _ in beyond]),
         scratch_shapes=[pltpu.VMEM((deep, wide), x.dtype) for x in slotted]
         + [pltpu.SemaphoreType.DMA((8,))],
         compiler_params=pltpu.CompilerParams(vmem_limit_bytes=4 << 20),
@@ -650,13 +658,16 @@
             )
         ]
     )
-    packs = [pack] + [shifted(pack, "sub", k) for k in range(1, groups)]
-    mine = max(8, modes // groups)
+    packs = [pack] + [
+        shifted(distant[k - 2] if k in beyond else pack, "sub", k) for k in range(1, groups)
+    ]
     start = first_mode(modes, groups, mine, lax.axis_index("sub").astype(jnp.int32))
     both = jnp.stack(
         [
-            jnp.concatenate([lax.dynamic_slice_in_dim(x, start, mine), x[modes:]], axis=0)
-            for x in packs
+            x
+            if k in beyond
+            else jnp.concatenate([lax.dynamic_slice_in_dim(x, start, mine), x[modes:]], axis=0)
+            for k, x in enumerate(packs)
         ]
     )
     low = shifted(both, "passage", 1)

time: 53.7 us -> 53.8 us (level)
  transfers between devices with their start and end apart: 16 -> 16, of which waited for: 12 -> 10; matrix products, arithmetic and copies ran while one was open for 0% -> 0% of each run, Pallas kernels for 8% -> 8%
where the time goes in v8:
time: 53.8 us; the launch traced here: 53.1 us
  starting transfers between devices  18.7 us (35%)
  waiting for transfers between devices  17.9 us (33%)
  Pallas kernels  15 us (28%)
  between operations  1.39 us (3%)
    pallas_call x5, Pallas kernels, call(): pl.pallas_call(kernel, name=name, out_shape=out_shape, in_specs=[smem()]...  13.6 us
    ppermute x8, waiting for transfers between devices, shifted(): return lax.ppermute(x, axis, [(i, (i + k) % n) for i in range(n)])  11.6 us
    ppermute x8, starting transfers between devices, shifted(): return lax.ppermute(x, axis, [(i, (i + k) % n) for i in range(n)])  10.6 us
    ppermute x8, starting transfers between devices, swapped(): return lax.ppermute(x, axis, [(i, i ^ k) for i in range(n)])  8.08 us
    ppermute x8, waiting for transfers between devices, swapped(): return lax.ppermute(x, axis, [(i, i ^ k) for i in range(n)])  6.31 us
    pallas_call x1, Pallas kernels, body(): pl.pallas_call(functools.partial(pack_kernel, modes, groups, mine), name=...  1.45 us
  transfers between devices with their start and end apart: 16, of which 10 were waited for; matrix products, arithmetic and copies ran while one was open for 0% of the time, Pallas kernels for 8%

profile of v8, /device:TPU:0, one launch (start us, length us, event | category | flops | bytes accessed | tf_op | source)
XLA Modules:
  0.0 53.1 jit_solution(3606755547284462985)
XLA Ops:
  1.3 1.5 %pack.1 = (f32[56,256]{1,0:T(8,128)S(1)}, f32[1,256]{1,0:T(1,128)S(1)}, f32[1,256]{1,0:T(1,128)S(1)}, s32[2,4]{1,0:T(2,128)S(1)}, f32[32,256]{1,0:T(8,128)S(1)}) custom-call(s32[1]{0:T(128)S(6)} %copy.13.live_ref, s32[8,128]{1,0:T(8,128)} %bitcast.16, s32[8,128]{1,0:T(8,128)} %bitcast.17, s32[8,128]{1,0:T(8,128)} %bitcast.18, f32[8,128]{1,0:T(8,128)} %bitcast.19, ...), custom_call_target="tpu_custom_call" | custom-call | flops 268435456 | bytes 1048576 | tf_op jit(solution)/shard_map/pack/pallas_call | solution.py:632
  2.7 0.0 copy-start
  2.8 5.1 %collective-permute-start.1 = (f32[56,256]{1,0:T(8,128)S(1)}, f32[56,256]{1,0:T(8,128)S(1)}, u32[]{:S(2)}, u32[]{:S(2)}) collective-permute-start(f32[56,256]{1,0:T(8,128)S(1)} %get-tuple-element.18.own.pack), channel_id=1, source_target_pairs={{0,3},{1,0},{2,1},{3,2},{4,7},{5,4},{6,5},{7,6},{8,11},{9,8},{10,9... | collective-permute-start | bytes 172040 | tf_op jit(solution)/shard_map/ppermute | solution.py:567
  7.9 1.0 %collective-permute-start.2 = (f32[32,256]{1,0:T(8,128)S(1)}, f32[32,256]{1,0:T(8,128)S(1)}, u32[]{:S(2)}, u32[]{:S(2)}) collective-permute-start(f32[32,256]{1,0:T(8,128)S(1)} %get-tuple-element.20), channel_id=1, source_target_pairs={{0,2},{1,3},{2,0},{3,1},{4,6},{5,7},{6,4},{7,5},{8,10},{9,11},{10,... | collective-permute-start | bytes 98312 | tf_op jit(solution)/shard_map/ppermute | solution.py:567
  8.9 0.1 pad_add_fusion.sub_ref
  9.0 1.0 %collective-permute-done.1.nxt = f32[56,256]{1,0:T(8,128)S(1)} collective-permute-done((f32[56,256]{1,0:T(8,128)S(1)}, f32[56,256]{1,0:T(8,128)S(1)}, u32[]{:S(2)}, u32[]{:S(2)}) %collective-permute-start.1) | collective-permute-done | bytes 57376 | tf_op jit(solution)/shard_map/ppermute | solution.py:567
  10.0 3.8 %collective-permute-done.prev = f32[56,256]{1,0:T(8,128)S(1)} collective-permute-done((f32[56,256]{1,0:T(8,128)S(1)}, f32[56,256]{1,0:T(8,128)S(1)}, u32[]{:S(2)}, u32[]{:S(2)}) %collective-permute-start) | collective-permute-done | bytes 57376 | tf_op jit(solution)/shard_map/ppermute | solution.py:567
  13.9 0.5 collective-permute-start.4
  14.4 0.0 collective-permute-start.3
  14.5 0.9 %stiff.1._.refs_4_ = f32[32,256]{1,0:T(8,128)S(1)} custom-call(s32[2]{0:T(128)S(1)} %pad_add_fusion.sub_ref, s32[2,4]{1,0:T(2,128)S(1)} %get-tuple-element.17.cols_ref, f32[56,256]{1,0:T(8,128)S(1)} %collective-permute-done.prev, f32[56,256]{1,0:T(8,128)S(1)} %get-tuple-element.18.own.pack, f32[56,256]{1,0:T(8,128)S(1)} %collective-permute-done.1.nxt, ...), custom_call_target="tpu_custom_call" | custom-call | flops 536870912 | bytes 1048576 | tf_op jit(solution)/shard_map/stiff/pallas_call | solution.py:597
  15.4 3.4 %own_source.1 = (f32[4,256,256]{2,1,0:T(8,128)S(1)}, f32[6,32,8,128]{3,2,1,0:T(8,128)S(1)}) custom-call(f32[4,32,256]{2,1,0:T(8,128)S(1)} %pad_maximum_fusion.both, f32[32,256]{1,0:T(8,128)S(1)} %stiff.1._.refs_4_), custom_call_target="tpu_custom_call" | custom-call | flops 4294967296 | bytes 1048576 | tf_op jit(solution)/shard_map/own_source/pallas_call | solution.py:597
  18.8 0.0 collective-permute-done.4.high
  18.8 2.0 %collective-permute-done.3.low = f32[4,32,256]{2,1,0:T(8,128)S(1)} collective-permute-done((f32[4,32,256]{2,1,0:T(8,128)S(1)}, f32[4,32,256]{2,1,0:T(8,128)S(1)}, u32[]{:S(2)}, u32[]{:S(2)}) %collective-permute-start.3) | collective-permute-done | bytes 131104 | tf_op jit(solution)/shard_map/ppermute | solution.py:567
  20.8 6.5 %fluid.1 = (f32[24,256]{1,0:T(8,128)S(1)}, f32[64,256]{1,0:T(8,128)S(1)}, f32[24,256]{1,0:T(8,128)S(1)}, f32[64,256]{1,0:T(8,128)S(1)}) custom-call(f32[4,32,256]{2,1,0:T(8,128)S(1)} %pad_maximum_fusion.both, f32[4,32,256]{2,1,0:T(8,128)S(1)} %collective-permute-done.3.low, f32[4,32,256]{2,1,0:T(8,128)S(1)} %collective-permute-done.4.high, ...), custom_call_target="tpu_custom_call" | custom-call | flops 4294967296 | bytes 1048576 | tf_op jit(solution)/shard_map/fluid/pallas_call | solution.py:597
  27.3 0.9 %collective-permute-start.5 = (f32[64,256]{1,0:T(8,128)S(1)}, f32[64,256]{1,0:T(8,128)S(1)}, u32[]{:S(2)}, u32[]{:S(2)}) collective-permute-start(f32[64,256]{1,0:T(8,128)S(1)} %get-tuple-element.25), channel_id=1, source_target_pairs={{0,1},{1,2},{2,3},{3,0},{4,5},{5,6},{6,7},{7,4},{8,9},{9,10},{10,1... | collective-permute-start | bytes 196616 | tf_op jit(solution)/shard_map/ppermute | solution.py:567
  28.2 2.9 %collective-permute-start.7 = (f32[64,256]{1,0:T(8,128)S(1)}, f32[64,256]{1,0:T(8,128)S(1)}, u32[]{:S(2)}, u32[]{:S(2)}) collective-permute-start(f32[64,256]{1,0:T(8,128)S(1)} %get-tuple-element.27), channel_id=1, source_target_pairs={{0,3},{1,0},{2,1},{3,2},{4,7},{5,4},{6,5},{7,6},{8,11},{9,8},{10,9... | collective-permute-start | bytes 196616 | tf_op jit(solution)/shard_map/ppermute | solution.py:567
  31.1 4.7 %collective-permute-done.6.refs_2_ = f32[24,256]{1,0:T(8,128)S(1)} collective-permute-done((f32[24,256]{1,0:T(8,128)S(1)}, f32[24,256]{1,0:T(8,128)S(1)}, u32[]{:S(2)}, u32[]{:S(2)}) %collective-permute-start.6) | collective-permute-done | bytes 24608 | tf_op jit(solution)/shard_map/ppermute | solution.py:567
  35.9 1.3 %gram.1 = (f32[48,128]{1,0:T(8,128)S(1)}, f32[48,128]{1,0:T(8,128)S(1)}, f32[32,256]{1,0:T(8,128)S(1)}) custom-call(s32[2]{0:T(128)S(1)} %pad_add_fusion.sub_ref, s32[2,4]{1,0:T(2,128)S(1)} %get-tuple-element.17.cols_ref, f32[56,256]{1,0:T(8,128)S(1)} %collective-permute-done.prev, f32[56,256]{1,0:T(8,128)S(1)} %get-tuple-element.18.own.pack, ...), custom_call_target="tpu_custom_call" | custom-call | flops 536870912 | bytes 1048576 | tf_op jit(solution)/shard_map/gram/pallas_call | solution.py:597
  37.1 0.1 collective-permute-start.8
  37.2 1.2 %collective-permute-done.8 = f32[48,128]{1,0:T(8,128)S(1)} collective-permute-done((f32[48,128]{1,0:T(8,128)S(1)}, f32[48,128]{1,0:T(8,128)S(1)}, u32[]{:S(2)}, u32[]{:S(2)}) %collective-permute-start.8) | collective-permute-done | bytes 24608 | tf_op jit(solution)/shard_map/ppermute | solution.py:572
  38.4 0.7 %collective-permute-start.11 = (f32[48,128]{1,0:T(8,128)S(1)}, f32[48,128]{1,0:T(8,128)S(1)}, u32[]{:S(2)}, u32[]{:S(2)}) collective-permute-start(f32[48,128]{1,0:T(8,128)S(1)} %add.27), channel_id=1, source_target_pairs={{0,24},{4,28},{8,16},{12,20},{16,8},{20,12},{24,0},{28,4},{1,25},{... | collective-permute-start | bytes 73736 | tf_op jit(solution)/shard_map/ppermute | solution.py:572
  39.1 0.4 collective-permute-start.10
  39.5 2.4 %collective-permute-start.9 = (f32[48,128]{1,0:T(8,128)S(1)}, f32[48,128]{1,0:T(8,128)S(1)}, u32[]{:S(2)}, u32[]{:S(2)}) collective-permute-start(f32[48,128]{1,0:T(8,128)S(1)} %add.27), channel_id=1, source_target_pairs={{0,8},{4,12},{8,0},{12,4},{16,24},{20,28},{24,16},{28,20},{1,9},{5... | collective-permute-start | bytes 73736 | tf_op jit(solution)/shard_map/ppermute | solution.py:572
  41.9 1.5 %collective-permute-done.11 = f32[48,128]{1,0:T(8,128)S(1)} collective-permute-done((f32[48,128]{1,0:T(8,128)S(1)}, f32[48,128]{1,0:T(8,128)S(1)}, u32[]{:S(2)}, u32[]{:S(2)}) %collective-permute-start.11) | collective-permute-done | bytes 24608 | tf_op jit(solution)/shard_map/ppermute | solution.py:572
  43.4 0.3 collective-permute-done.9
  43.7 1.9 %collective-permute-start.14 = (f32[48,128]{1,0:T(8,128)S(1)}, f32[48,128]{1,0:T(8,128)S(1)}, u32[]{:S(2)}, u32[]{:S(2)}) collective-permute-start(f32[48,128]{1,0:T(8,128)S(1)} %add_add_fusion.1), channel_id=1, source_target_pairs={{0,3},{1,2},{2,1},{3,0},{4,7},{5,6},{6,5},{7,4},{8,11},{9,10},{10,... | collective-permute-start | bytes 73736 | tf_op jit(solution)/shard_map/ppermute | solution.py:572
  45.6 2.6 %collective-permute-start.12 = (f32[48,128]{1,0:T(8,128)S(1)}, f32[48,128]{1,0:T(8,128)S(1)}, u32[]{:S(2)}, u32[]{:S(2)}) collective-permute-start(f32[48,128]{1,0:T(8,128)S(1)} %add_add_fusion.1), channel_id=1, source_target_pairs={{0,1},{1,0},{2,3},{3,2},{4,5},{5,4},{6,7},{7,6},{8,9},{9,8},{10,11... | collective-permute-start | bytes 73736 | tf_op jit(solution)/shard_map/ppermute | solution.py:572
  48.2 1.5 %collective-permute-done.14 = f32[48,128]{1,0:T(8,128)S(1)} collective-permute-done((f32[48,128]{1,0:T(8,128)S(1)}, f32[48,128]{1,0:T(8,128)S(1)}, u32[]{:S(2)}, u32[]{:S(2)}) %collective-permute-start.14) | collective-permute-done | bytes 24608 | tf_op jit(solution)/shard_map/ppermute | solution.py:572
  49.6 0.7 %collective-permute-done.13 = f32[48,128]{1,0:T(8,128)S(1)} collective-permute-done((f32[48,128]{1,0:T(8,128)S(1)}, f32[48,128]{1,0:T(8,128)S(1)}, u32[]{:S(2)}, u32[]{:S(2)}) %collective-permute-start.13) | collective-permute-done | bytes 24608 | tf_op jit(solution)/shard_map/ppermute | solution.py:572
  50.3 0.1 collective-permute-start.15
  50.4 1.2 %collective-permute-done.15.other = f32[48,128]{1,0:T(8,128)S(1)} collective-permute-done((f32[48,128]{1,0:T(8,128)S(1)}, f32[48,128]{1,0:T(8,128)S(1)}, u32[]{:S(2)}, u32[]{:S(2)}) %collective-permute-start.15) | collective-permute-done | bytes 24608 | tf_op jit(solution)/shard_map/ppermute | solution.py:572
  51.6 1.5 %final.1 = (f32[32,256]{1,0:T(8,128)}, f32[64,64]{1,0:T(8,128)}, f32[64,64]{1,0:T(8,128)}) custom-call(s32[2]{0:T(128)S(1)} %pad_add_fusion.sub_ref, f32[48,128]{1,0:T(8,128)S(1)} %add_add_fusion.mine, f32[48,128]{1,0:T(8,128)S(1)} %collective-permute-done.15.other, f32[32,256]{1,0:T(8,128)S(1)} %stiff.1._.refs_4_, f32[32,256]{1,0:T(8,128)S(1)} %get-tuple-element.30.mass), custom_call_target="tpu_custom_call" | custom-call | flops 1048576 | bytes 1048576 | tf_op jit(solution)/shard_map/final/pallas_call | solution.py:597
  (22 shorter events, 0.1 us)
Async XLA Ops:
  2.7 11.7 %copy-start = (f32[2,4,128,128]{3,2,1,0:T(8,128)S(1)}, f32[2,4,128,128]{3,2,1,0:T(8,128)}, u32[]{:S(2)}) copy-start(f32[2,4,128,128]{3,2,1,0:T(8,128)} %refs_6_.1) | copy-start | bytes 1572868
  2.8 7.3 %collective-permute-start.1 = (f32[56,256]{1,0:T(8,128)S(1)}, f32[56,256]{1,0:T(8,128)S(1)}, u32[]{:S(2)}, u32[]{:S(2)}) collective-permute-start(f32[56,256]{1,0:T(8,128)S(1)} %get-tuple-element.18.own.pack), channel_id=1, source_target_pairs={{0,3},{1,0},{2,1},{3,2},{4,7},{5,4},{6,5},{7,6},{8,11},{9,8},{10,9... | collective-permute-start | bytes 172040 | tf_op jit(solution)/shard_map/ppermute | solution.py:567
  7.9 6.0 %collective-permute-start = (f32[56,256]{1,0:T(8,128)S(1)}, f32[56,256]{1,0:T(8,128)S(1)}, u32[]{:S(2)}, u32[]{:S(2)}) collective-permute-start(f32[56,256]{1,0:T(8,128)S(1)} %get-tuple-element.18.own.pack), channel_id=1, source_target_pairs={{0,1},{1,2},{2,3},{3,0},{4,5},{5,6},{6,7},{7,4},{8,9},{9,10},{10,1... | collective-permute-start | bytes 172040 | tf_op jit(solution)/shard_map/ppermute | solution.py:567
  7.9 6.0 %collective-permute-start.2 = (f32[32,256]{1,0:T(8,128)S(1)}, f32[32,256]{1,0:T(8,128)S(1)}, u32[]{:S(2)}, u32[]{:S(2)}) collective-permute-start(f32[32,256]{1,0:T(8,128)S(1)} %get-tuple-element.20), channel_id=1, source_target_pairs={{0,2},{1,3},{2,0},{3,1},{4,6},{5,7},{6,4},{7,5},{8,10},{9,11},{10,... | collective-permute-start | bytes 98312 | tf_op jit(solution)/shard_map/ppermute | solution.py:567
  13.9 4.9 %collective-permute-start.4 = (f32[4,32,256]{2,1,0:T(8,128)S(1)}, f32[4,32,256]{2,1,0:T(8,128)S(1)}, u32[]{:S(2)}, u32[]{:S(2)}) collective-permute-start(f32[4,32,256]{2,1,0:T(8,128)S(1)} %pad_maximum_fusion.both), channel_id=1, source_target_pairs={{0,28},{4,0},{8,4},{12,8},{16,12},{20,16},{24,20},{28,24},{1,29},{... | collective-permute-start | bytes 393224 | tf_op jit(solution)/shard_map/ppermute | solution.py:567
  14.4 6.3 %collective-permute-start.3 = (f32[4,32,256]{2,1,0:T(8,128)S(1)}, f32[4,32,256]{2,1,0:T(8,128)S(1)}, u32[]{:S(2)}, u32[]{:S(2)}) collective-permute-start(f32[4,32,256]{2,1,0:T(8,128)S(1)} %pad_maximum_fusion.both), channel_id=1, source_target_pairs={{0,4},{4,8},{8,12},{12,16},{16,20},{20,24},{24,28},{28,0},{1,5},{5... | collective-permute-start | bytes 393224 | tf_op jit(solution)/shard_map/ppermute | solution.py:567
  27.3 8.6 %collective-permute-start.5 = (f32[64,256]{1,0:T(8,128)S(1)}, f32[64,256]{1,0:T(8,128)S(1)}, u32[]{:S(2)}, u32[]{:S(2)}) collective-permute-start(f32[64,256]{1,0:T(8,128)S(1)} %get-tuple-element.25), channel_id=1, source_target_pairs={{0,1},{1,2},{2,3},{3,0},{4,5},{5,6},{6,7},{7,4},{8,9},{9,10},{10,1... | collective-permute-start | bytes 196616 | tf_op jit(solution)/shard_map/ppermute | solution.py:567
  28.2 7.7 %collective-permute-start.7 = (f32[64,256]{1,0:T(8,128)S(1)}, f32[64,256]{1,0:T(8,128)S(1)}, u32[]{:S(2)}, u32[]{:S(2)}) collective-permute-start(f32[64,256]{1,0:T(8,128)S(1)} %get-tuple-element.27), channel_id=1, source_target_pairs={{0,3},{1,0},{2,1},{3,2},{4,7},{5,4},{6,5},{7,6},{8,11},{9,8},{10,9... | collective-permute-start | bytes 196616 | tf_op jit(solution)/shard_map/ppermute | solution.py:567
  31.1 4.7 %collective-permute-start.6 = (f32[24,256]{1,0:T(8,128)S(1)}, f32[24,256]{1,0:T(8,128)S(1)}, u32[]{:S(2)}, u32[]{:S(2)}) collective-permute-start(f32[24,256]{1,0:T(8,128)S(1)} %get-tuple-element.26), channel_id=1, source_target_pairs={{0,2},{1,3},{2,0},{3,1},{4,6},{5,7},{6,4},{7,5},{8,10},{9,11},{10,... | collective-permute-start | bytes 73736 | tf_op jit(solution)/shard_map/ppermute | solution.py:567
  37.1 1.3 %collective-permute-start.8 = (f32[48,128]{1,0:T(8,128)S(1)}, f32[48,128]{1,0:T(8,128)S(1)}, u32[]{:S(2)}, u32[]{:S(2)}) collective-permute-start(f32[48,128]{1,0:T(8,128)S(1)} %get-tuple-element.29), channel_id=1, source_target_pairs={{0,4},{4,0},{8,12},{12,8},{16,20},{20,16},{24,28},{28,24},{1,5},{5... | collective-permute-start | bytes 73736 | tf_op jit(solution)/shard_map/ppermute | solution.py:572
  38.4 5.0 %collective-permute-start.11 = (f32[48,128]{1,0:T(8,128)S(1)}, f32[48,128]{1,0:T(8,128)S(1)}, u32[]{:S(2)}, u32[]{:S(2)}) collective-permute-start(f32[48,128]{1,0:T(8,128)S(1)} %add.27), channel_id=1, source_target_pairs={{0,24},{4,28},{8,16},{12,20},{16,8},{20,12},{24,0},{28,4},{1,25},{... | collective-permute-start | bytes 73736 | tf_op jit(solution)/shard_map/ppermute | solution.py:572
  39.1 4.2 %collective-permute-start.10 = (f32[48,128]{1,0:T(8,128)S(1)}, f32[48,128]{1,0:T(8,128)S(1)}, u32[]{:S(2)}, u32[]{:S(2)}) collective-permute-start(f32[48,128]{1,0:T(8,128)S(1)} %add.27), channel_id=1, source_target_pairs={{0,16},{4,20},{8,24},{12,28},{16,0},{20,4},{24,8},{28,12},{1,17},{... | collective-permute-start | bytes 73736 | tf_op jit(solution)/shard_map/ppermute | solution.py:572
  39.5 4.2 %collective-permute-start.9 = (f32[48,128]{1,0:T(8,128)S(1)}, f32[48,128]{1,0:T(8,128)S(1)}, u32[]{:S(2)}, u32[]{:S(2)}) collective-permute-start(f32[48,128]{1,0:T(8,128)S(1)} %add.27), channel_id=1, source_target_pairs={{0,8},{4,12},{8,0},{12,4},{16,24},{20,28},{24,16},{28,20},{1,9},{5... | collective-permute-start | bytes 73736 | tf_op jit(solution)/shard_map/ppermute | solution.py:572
  43.7 5.9 %collective-permute-start.14 = (f32[48,128]{1,0:T(8,128)S(1)}, f32[48,128]{1,0:T(8,128)S(1)}, u32[]{:S(2)}, u32[]{:S(2)}) collective-permute-start(f32[48,128]{1,0:T(8,128)S(1)} %add_add_fusion.1), channel_id=1, source_target_pairs={{0,3},{1,2},{2,1},{3,0},{4,7},{5,6},{6,5},{7,4},{8,11},{9,10},{10,... | collective-permute-start | bytes 73736 | tf_op jit(solution)/shard_map/ppermute | solution.py:572
  45.6 4.7 %collective-permute-start.13 = (f32[48,128]{1,0:T(8,128)S(1)}, f32[48,128]{1,0:T(8,128)S(1)}, u32[]{:S(2)}, u32[]{:S(2)}) collective-permute-start(f32[48,128]{1,0:T(8,128)S(1)} %add_add_fusion.1), channel_id=1, source_target_pairs={{0,2},{1,3},{2,0},{3,1},{4,6},{5,7},{6,4},{7,5},{8,10},{9,11},{10,... | collective-permute-start | bytes 73736 | tf_op jit(solution)/shard_map/ppermute | solution.py:572
  45.6 4.7 %collective-permute-start.12 = (f32[48,128]{1,0:T(8,128)S(1)}, f32[48,128]{1,0:T(8,128)S(1)}, u32[]{:S(2)}, u32[]{:S(2)}) collective-permute-start(f32[48,128]{1,0:T(8,128)S(1)} %add_add_fusion.1), channel_id=1, source_target_pairs={{0,1},{1,0},{2,3},{3,2},{4,5},{5,4},{6,7},{7,6},{8,9},{9,8},{10,11... | collective-permute-start | bytes 73736 | tf_op jit(solution)/shard_map/ppermute | solution.py:572
  50.3 1.3 %collective-permute-start.15 = (f32[48,128]{1,0:T(8,128)S(1)}, f32[48,128]{1,0:T(8,128)S(1)}, u32[]{:S(2)}, u32[]{:S(2)}) collective-permute-start(f32[48,128]{1,0:T(8,128)S(1)} %add_add_fusion.mine), channel_id=1, source_target_pairs={{0,4},{4,0},{8,12},{12,8},{16,20},{20,16},{24,28},{28,24},{1,5},{5... | collective-permute-start | bytes 73736 | tf_op jit(solution)/shard_map/ppermute | solution.py:572
